TPU v7x, 512 devices: a whole 4x4x16 slice. The times are simulated.
512 devices in a mesh: hist: 32 (over x, y, core), second: 16 (over z).
Axes of the slice: x: 4, y: 4, z: 16, core: 2. Of those that a mesh axis runs over, the one named last changes fastest.
Arguments:
- history: bfloat16 [32768, 32768], P('hist', 'second'), may hold values from -0.03125 to 0.03125
- self_rows: bfloat16 [256, 32768], P(None, 'hist'), may hold values from -6 to 6
- edge_rows: bfloat16 [128, 32768], P(None, 'second'), may hold values from -6 to 6
- step_inv: float32 [128, 128], replicated, may hold values from -0.08 to 0.98, as said below
- coupling: float32 [128], replicated, may hold values from 0.1 to 1
- reach: int32 [3, 256], replicated, may hold values from 1 to 256, as said below
Outputs:
- green_last: bfloat16 [256, 32768], P(None, 'second')
Inputs may be any that keep to these rules, and one draw needn't show every extreme that they name: `step_inv`: entries other than the diagonal lie within 0.08 of zero; diagonal entries between 0.5 and 0.9. reach[b, c] is at least c + 1 and at most min(256, c + 2 * b + 4).
All inputs are finite; a program needn't handle non-finite values.
Results may differ from a plain program's by a relative error of at most 0.014.
Values may be sent and summed in bfloat16 or wider, within the bound.
No kernel may reach another device: no remote copies, remote signals or barrier semaphores. Data moves between devices by JAX's collectives and lax.ppermute only.
A program may use at most 64 MiB of HBM per device.

v0:
```python
import jax
import jax.numpy as jnp
from jax import lax
from jax.sharding import Mesh
from jax.sharding import PartitionSpec as P

HIST = ("hist_0", "hist_1", "hist_2")


def rows_for(lines, devices):
    spare = -len(lines) % devices
    return jnp.pad(lines, [(0, spare)] + [(0, 0)] * (lines.ndim - 1))


def sent_to_all(x, axis):
    devices = lax.axis_size(axis)
    return lax.all_to_all(jnp.broadcast_to(x[None], (devices, *x.shape)), axis, 0, 0, tiled=True)


def joined_along(parts, dim):
    dims = list(parts.shape[1:])
    dims[dim] *= parts.shape[0]
    return jnp.moveaxis(parts, 0, dim).reshape(dims)


def gathered_by_axis(x, axes, dim):
    far, near = axes
    initial = sent_to_all(x, far)
    parts = jnp.swapaxes(sent_to_all(initial, near), 0, 1)
    return joined_along(parts.reshape(-1, *x.shape), dim)


def split_up(x, dim, devices):
    before, after = (x.shape[:dim], x.shape[dim + 1 :])
    return jnp.moveaxis(x.reshape(*before, devices, -1, *after), dim, 0)


def summed_on_arrival(x, axis, dim):
    devices = lax.axis_size(axis)
    parts = lax.all_to_all(split_up(x, dim, devices), axis, 0, 0, tiled=True)
    return jnp.sum(parts.astype(jnp.float32), axis=0)


def sum_in_two_steps(x, axes, dim):
    far, near = axes
    own = summed_on_arrival(split_up(x, dim, lax.axis_size(far)), near, dim + 1)
    return jnp.sum(
        lax.all_to_all(own.astype(jnp.bfloat16), far, 0, 0, tiled=True).astype(jnp.float32), axis=0
    )


def nested_sum(x, axes):
    lines = x.reshape(-1, x.shape[-1])
    padded = rows_for(lines, lax.axis_size(axes[0]) * lax.axis_size(axes[1]))
    whole = gathered_by_axis(sum_in_two_steps(padded, axes, 0).astype(jnp.bfloat16), axes, 0)
    return lax.slice_in_dim(whole, 0, len(lines)).reshape(x.shape).astype(jnp.float32)


def collect(x, axis, dim):
    return joined_along(sent_to_all(x, axis), dim)


def nested_sum_2(x, axes):
    lines = x.reshape(-1, x.shape[-1])
    own = summed_on_arrival(rows_for(lines, lax.axis_size(axes)), axes, 0)
    whole = collect(own.astype(jnp.bfloat16), axes, 0)
    return whole[: len(lines)].reshape(x.shape).astype(jnp.float32)


def screened(block_rows, weights):
    square = block_rows * block_rows
    return weights[:, None] * block_rows * square / (1.0 + square)


def advance(green_now, integral, step_inv, row_t, time_steps):
    rows_out = []
    for step_number in range(time_steps):
        source = green_now + integral[step_number * row_t : (step_number + 1) * row_t]
        green_now = jnp.dot(
            step_inv, source, precision=lax.Precision.HIGHEST, preferred_element_type=jnp.float32
        )
        rows_out.append(green_now)
    return (green_now, jnp.concatenate(rows_out, 0))


def local(history, self_rows, edge_rows, step_inv, coupling, reach):
    hist_count = lax.axis_size(HIST)
    second_count = lax.axis_size("second")
    hist_place = lax.axis_index(HIST)
    second_place = lax.axis_index("second")
    rows_loc, cols_loc = history.shape
    row_t = step_inv.shape[0]
    time_steps = self_rows.shape[0] // row_t
    past_loc = rows_loc // row_t
    tiles_loc = cols_loc // row_t
    ratio_axes = hist_count // second_count
    past_ids = hist_place * past_loc + jnp.arange(past_loc, dtype=jnp.int32)
    weights = jnp.tile(coupling, time_steps)
    tiled_hist = history.reshape(past_loc, row_t, tiles_loc, row_t)
    blocks = reach.shape[0]
    sigma_rows = self_rows
    green_now = edge_rows.astype(jnp.float32)
    finished = None
    for moment in range(blocks):
        limit_row = lax.dynamic_slice_in_dim(reach[moment], second_place * tiles_loc, tiles_loc)
        live_mask = past_ids[:, None] < limit_row[None, :]
        masked = jnp.where(
            live_mask[:, None, :, None], tiled_hist, jnp.zeros((), history.dtype)
        ).reshape(rows_loc, cols_loc)
        partial_value = jnp.dot(sigma_rows, masked, preferred_element_type=jnp.float32)
        final_block = moment + 1 == blocks
        fresh_rows = None
        integral = nested_sum(partial_value.astype(jnp.bfloat16), (("hist_0", "hist_1"), "hist_2"))
        green_now, block_rows = advance(green_now, integral, step_inv, row_t, time_steps)
        if final_block:
            finished = block_rows.astype(jnp.bfloat16)
        else:
            fresh_rows = screened(block_rows, weights).astype(jnp.bfloat16)
        if not final_block:
            own_piece = lax.dynamic_slice_in_dim(
                fresh_rows, hist_place % ratio_axes * rows_loc, rows_loc, 1
            )
            holder = second_place == hist_place // ratio_axes
            kept_piece = jnp.where(
                holder, own_piece.astype(jnp.float32), jnp.zeros((), jnp.float32)
            )
            sigma_rows = nested_sum_2(kept_piece.astype(jnp.bfloat16), "second").astype(
                jnp.bfloat16
            )
    return finished


def solution(mesh):
    torus = Mesh(
        mesh.devices.reshape(4, 4, 2, mesh.shape["second"]),
        ("hist_0", "hist_1", "hist_2", "second"),
    )
    placed = (P(HIST, "second"), P(None, HIST), P(None, "second"), P(), P(), P())
    return jax.shard_map(
        local, mesh=torus, in_specs=placed, out_specs=P(None, "second"), check_vma=False
    )
```

profile of v0, /device:TPU:1, one launch (start us, length us, event | category | flops | bytes accessed | tf_op | source)
XLA Modules:
  0.0 298.0 jit_solution(13844465018463023356)
XLA Ops:
  0.0 0.8 fusion.22
  1.0 0.6 broadcast_in_dim.92
  1.7 3.7 %fusion.5 = bf16[2048,256]{0,1:T(8,128)(2,1)S(1)} fusion(bf16[256,1024]{1,0:T(8,128)(2,1)S(1)} %copy-done, bf16[1024,2048]{1,0:T(8,128)(2,1)} %param.6, pred[128,8,16,128]{3,2,1,0:T(8,128)(4,1)S(1)} %bitcast.97), kind=kOutput, calls=%fused_computation.8 | convolution fusion | flops 1076363264 | bytes 7864320 | tf_op jit(solution)/shard_map/dot_general | solution.py:110
  5.5 11.0 %all_to_all.80 = bf16[2,16,8,2048]{3,2,1,0:T(8,128)(2,1)S(1)} all-to-all(bf16[2,16,8,2048]{3,2,1,0:T(8,128)(2,1)S(1)} %bitcast.92), channel_id=1, replica_groups=mesh['hist_0'=4,'hist_1'=4,'hist_2'=2,'second'=16] {'hist_2'}, dimensions={0} | all-to-all | bytes 2097152 | tf_op jit(solution)/shard_map/all_to_all | solution.py:40
  16.8 12.8 %all_to_all.81 = bf16[16,8,2048]{2,1,0:T(8,128)(2,1)S(1)} all-to-all(bf16[16,8,2048]{2,1,0:T(8,128)(2,1)S(1)} %reduce_sum.96), channel_id=1, replica_groups=mesh['hist_0'=4,'hist_1'=4,'hist_2'=2,'second'=16] {'hist_0','hist_1'}, dimensions={0} | all-to-all | bytes 1048576 | tf_op jit(solution)/shard_map/all_to_all | solution.py:48
  29.7 0.8 broadcast_in_dim.95
  30.6 4.2 %all-to-all-start.2 = ((bf16[16,8,2048]{2,1,0:T(8,128)(2,1)}), bf16[16,8,2048]{2,1,0:T(8,128)(2,1)S(1)}, u32[]{:S(2)}, u32[]{:S(2)}) async-start(bf16[16,8,2048]{2,1,0:T(8,128)(2,1)} %broadcast_in_dim.95), calls=%async_computation.2 | async-start | bytes 1048576 | tf_op jit(solution)/shard_map/all_to_all | solution.py:17
  34.8 8.8 %all-to-all-done.2 = bf16[16,8,2048]{2,1,0:T(8,128)(2,1)S(1)} async-done(((bf16[16,8,2048]{2,1,0:T(8,128)(2,1)}), bf16[16,8,2048]{2,1,0:T(8,128)(2,1)S(1)}, u32[]{:S(2)}, u32[]{:S(2)}) %all-to-all-start.2) | async-done | bytes 524320 | tf_op jit(solution)/shard_map/all_to_all | solution.py:17
  43.7 7.8 %all_to_all.82 = bf16[2,16,8,2048]{3,2,1,0:T(8,128)(2,1)S(1)} all-to-all(bf16[2,16,8,2048]{3,2,1,0:T(8,128)(2,1)S(1)} %broadcast_in_dim.96), channel_id=1, replica_groups=mesh['hist_0'=4,'hist_1'=4,'hist_2'=2,'second'=16] {'hist_2'}, dimensions={0} | all-to-all | bytes 2097152 | tf_op jit(solution)/shard_map/all_to_all | solution.py:17
  52.0 0.8 copy-done.3
  53.0 1.1 bitcast_add_fusion.4
  54.1 1.1 convolution_bitcast_fusion.3
  55.4 35.8 %all_to_all.83 = bf16[16,16,1024]{2,1,0:T(8,128)(2,1)S(1)} all-to-all(bf16[16,16,1024]{2,1,0:T(8,128)(2,1)S(1)} %bitcast.99), channel_id=1, replica_groups=mesh['hist_0'=4,'hist_1'=4,'hist_2'=2,'second'=16] {'second'}, dimensions={0} | all-to-all | bytes 1048576 | tf_op jit(solution)/shard_map/all_to_all | solution.py:40
  91.3 35.5 %all_to_all.84 = bf16[16,16,1024]{2,1,0:T(8,128)(2,1)S(1)} all-to-all(bf16[16,16,1024]{2,1,0:T(8,128)(2,1)S(1)} %broadcast_in_dim.98), channel_id=1, replica_groups=mesh['hist_0'=4,'hist_1'=4,'hist_2'=2,'second'=16] {'second'}, dimensions={0} | all-to-all | bytes 1048576 | tf_op jit(solution)/shard_map/all_to_all | solution.py:17
  127.5 3.7 %fusion.4 = bf16[256,2048]{1,0:T(8,128)(2,1)S(1)} fusion(bf16[256,1024]{1,0:T(8,128)(2,1)S(1)} %bitcast.104, bf16[1024,2048]{1,0:T(8,128)(2,1)} %param.6, pred[128,8,16,128]{3,2,1,0:T(8,128)(4,1)S(1)} %bitcast.95), kind=kOutput, calls=%fused_computation.7 | convolution fusion | flops 1076363264 | bytes 7864320 | tf_op jit(solution)/shard_map/dot_general | solution.py:110
  131.3 11.2 %all_to_all.85 = bf16[2,16,8,2048]{3,2,1,0:T(8,128)(2,1)S(1)} all-to-all(bf16[2,16,8,2048]{3,2,1,0:T(8,128)(2,1)S(1)} %bitcast.93), channel_id=1, replica_groups=mesh['hist_0'=4,'hist_1'=4,'hist_2'=2,'second'=16] {'hist_2'}, dimensions={0} | all-to-all | bytes 2097152 | tf_op jit(solution)/shard_map/all_to_all | solution.py:40
  142.8 13.3 %all_to_all.86 = bf16[16,8,2048]{2,1,0:T(8,128)(2,1)S(1)} all-to-all(bf16[16,8,2048]{2,1,0:T(8,128)(2,1)S(1)} %reduce_sum.99), channel_id=1, replica_groups=mesh['hist_0'=4,'hist_1'=4,'hist_2'=2,'second'=16] {'hist_0','hist_1'}, dimensions={0} | all-to-all | bytes 1048576 | tf_op jit(solution)/shard_map/all_to_all | solution.py:48
  156.3 12.7 %all_to_all.87 = bf16[16,8,2048]{2,1,0:T(8,128)(2,1)S(1)} all-to-all(bf16[16,8,2048]{2,1,0:T(8,128)(2,1)S(1)} %broadcast_in_dim.101), channel_id=1, replica_groups=mesh['hist_0'=4,'hist_1'=4,'hist_2'=2,'second'=16] {'hist_0','hist_1'}, dimensions={0} | all-to-all | bytes 1048576 | tf_op jit(solution)/shard_map/all_to_all | solution.py:17
  169.1 7.5 %all_to_all.88 = bf16[2,16,8,2048]{3,2,1,0:T(8,128)(2,1)S(1)} all-to-all(bf16[2,16,8,2048]{3,2,1,0:T(8,128)(2,1)S(1)} %broadcast_in_dim.102), channel_id=1, replica_groups=mesh['hist_0'=4,'hist_1'=4,'hist_2'=2,'second'=16] {'hist_2'}, dimensions={0} | all-to-all | bytes 2097152 | tf_op jit(solution)/shard_map/all_to_all | solution.py:17
  177.5 1.1 bitcast_add_fusion.2
  178.5 1.1 convolution_bitcast_fusion.1
  179.9 28.7 %all_to_all.89 = bf16[16,16,1024]{2,1,0:T(8,128)(2,1)S(1)} all-to-all(bf16[16,16,1024]{2,1,0:T(8,128)(2,1)S(1)} %bitcast.98), channel_id=1, replica_groups=mesh['hist_0'=4,'hist_1'=4,'hist_2'=2,'second'=16] {'second'}, dimensions={0} | all-to-all | bytes 1048576 | tf_op jit(solution)/shard_map/all_to_all | solution.py:40
  208.7 35.6 %all_to_all.90 = bf16[16,16,1024]{2,1,0:T(8,128)(2,1)S(1)} all-to-all(bf16[16,16,1024]{2,1,0:T(8,128)(2,1)S(1)} %broadcast_in_dim.103), channel_id=1, replica_groups=mesh['hist_0'=4,'hist_1'=4,'hist_2'=2,'second'=16] {'second'}, dimensions={0} | all-to-all | bytes 1048576 | tf_op jit(solution)/shard_map/all_to_all | solution.py:17
  244.3 0.6 broadcast_in_dim.104
  244.9 3.7 %fusion.3 = bf16[256,2048]{1,0:T(8,128)(2,1)S(1)} fusion(bf16[256,1024]{1,0:T(8,128)(2,1)S(1)} %bitcast.103, bf16[1024,2048]{1,0:T(8,128)(2,1)} %param.6, pred[128,8,16,128]{3,2,1,0:T(8,128)(4,1)S(1)} %bitcast.96), kind=kOutput, calls=%fused_computation.6 | convolution fusion | flops 1076363264 | bytes 7864320 | tf_op jit(solution)/shard_map/dot_general | solution.py:110
  248.8 11.2 %all_to_all.91 = bf16[2,16,8,2048]{3,2,1,0:T(8,128)(2,1)S(1)} all-to-all(bf16[2,16,8,2048]{3,2,1,0:T(8,128)(2,1)S(1)} %bitcast.94), channel_id=1, replica_groups=mesh['hist_0'=4,'hist_1'=4,'hist_2'=2,'second'=16] {'hist_2'}, dimensions={0} | all-to-all | bytes 2097152 | tf_op jit(solution)/shard_map/all_to_all | solution.py:40
  260.3 13.3 %all_to_all.92 = bf16[16,8,2048]{2,1,0:T(8,128)(2,1)S(1)} all-to-all(bf16[16,8,2048]{2,1,0:T(8,128)(2,1)S(1)} %reduce_sum.102), channel_id=1, replica_groups=mesh['hist_0'=4,'hist_1'=4,'hist_2'=2,'second'=16] {'hist_0','hist_1'}, dimensions={0} | all-to-all | bytes 1048576 | tf_op jit(solution)/shard_map/all_to_all | solution.py:48
  273.7 12.7 %all_to_all.93 = bf16[16,8,2048]{2,1,0:T(8,128)(2,1)S(1)} all-to-all(bf16[16,8,2048]{2,1,0:T(8,128)(2,1)S(1)} %broadcast_in_dim.106), channel_id=1, replica_groups=mesh['hist_0'=4,'hist_1'=4,'hist_2'=2,'second'=16] {'hist_0','hist_1'}, dimensions={0} | all-to-all | bytes 1048576 | tf_op jit(solution)/shard_map/all_to_all | solution.py:17
  286.6 7.4 %all_to_all.94 = bf16[2,16,8,2048]{3,2,1,0:T(8,128)(2,1)S(1)} all-to-all(bf16[2,16,8,2048]{3,2,1,0:T(8,128)(2,1)S(1)} %broadcast_in_dim.107), channel_id=1, replica_groups=mesh['hist_0'=4,'hist_1'=4,'hist_2'=2,'second'=16] {'hist_2'}, dimensions={0} | all-to-all | bytes 2097152 | tf_op jit(solution)/shard_map/all_to_all | solution.py:17
  294.8 1.1 fusion.21
  295.9 1.1 fusion.6
  297.0 1.0 pad_maximum_fusion
  (48 shorter events, 5.7 us)
Async XLA Ops:
  0.0 1.6 copy-start
  16.5 18.3 %copy-start.4 = (f32[128]{0:T(128)S(1)}, f32[128]{0:T(128)}, u32[]{:S(2)}) copy-start(f32[128]{0:T(128)} %param.10) | copy-start | bytes 1540
  30.6 13.1 %all-to-all-start.2 = ((bf16[16,8,2048]{2,1,0:T(8,128)(2,1)}), bf16[16,8,2048]{2,1,0:T(8,128)(2,1)S(1)}, u32[]{:S(2)}, u32[]{:S(2)}) async-start(bf16[16,8,2048]{2,1,0:T(8,128)(2,1)} %broadcast_in_dim.95), calls=%async_computation.2 | async-start | bytes 1048576 | tf_op jit(solution)/shard_map/all_to_all | solution.py:17
  51.8 1.0 copy-start.3
  52.0 1.0 copy-start.2
  294.8 3.2 %copy-start.1 = (bf16[256,1024]{1,0:T(8,128)(2,1)S(1)}, bf16[256,1024]{1,0:T(8,128)(2,1)}, u32[]{:S(2)}) copy-start(bf16[256,1024]{1,0:T(8,128)(2,1)} %param.7) | copy-start | bytes 1572868
where the time goes:
time: 299 us; the launch traced here: 298 us
  blocking collectives  257 us (86%)
  matrix products  17.6 us (6%)
  waiting for transfers between devices  8.8 us (3%)
  local copies, waits for them, and re-layouts  6.25 us (2%)
  starting transfers between devices  4.19 us (1%)
  other arithmetic  4.11 us (1%)
    all_to_all x7, blocking collectives, sent_to_all(): lax.all_to_all(jnp.broadcast_to(x[None], (devices, *x.shape)), axis, 0, 0...  119 us
    all_to_all x5, blocking collectives, summed_on_arrival(): parts = lax.all_to_all(split_up(x, dim, devices), axis, 0, 0, tiled=True)  97.8 us
    all_to_all x3, blocking collectives, sum_in_two_steps(): lax.all_to_all(own.astype(jnp.bfloat16), far, 0, 0, tiled=True)  39.5 us
    dot_general x3, matrix products, local(): jnp.dot(sigma_rows, masked, preferred_element_type=jnp.float32)  11.2 us
    all_to_all x1, waiting for transfers between devices, sent_to_all(): lax.all_to_all(jnp.broadcast_to(x[None], (devices, *x.shape)), axis, 0, 0...  8.8 us
    dot_general x6, matrix products, advance(): jnp.dot(step_inv, source, precision=lax.Precision.HIGHEST, preferred_elem...  6.44 us
  transfers between devices with their start and end apart: 1, of which 1 were waited for; matrix products, arithmetic and copies ran while one was open for 0% of the time, Pallas kernels for 0%

commit v1 on v0

v1 whole, which is shorter than its diff:
```python
import functools

import jax
import jax.numpy as jnp
from jax import lax
from jax.experimental import pallas as pl
from jax.experimental.pallas import tpu as pltpu
from jax.sharding import Mesh
from jax.sharding import PartitionSpec as P

HIST = ("x", "y", "c")
PLANE = ("x", "y")
ROW_T = 128
HALF = 64
TILE = 256


def low_lanes(shape):
    return lax.broadcasted_iota(jnp.int32, shape, 1) < HALF


def swap_halves(value):
    return pltpu.roll(value, HALF, 1)


def unpack_pair(even, odd):
    low = low_lanes(even.shape)
    return (
        jnp.where(low, even, swap_halves(odd)),
        jnp.where(low, swap_halves(even), odd),
    )


def memory_kernel(block, first_half, from_pieces, where_ref, reach_ref, sigma_ref, hist_ref, out_ref, *scratch):
    rows, cols = hist_ref.shape
    past_loc, tiles = rows // ROW_T, cols // ROW_T
    hist_place, second_place, own = where_ref[0], where_ref[1], where_ref[2]
    half = 1 - own if first_half else own
    step = pl.program_id(0)
    if from_pieces:
        sigma = scratch[0]

        @pl.when(step == 0)
        def _():
            for pair in range(sigma_ref.shape[0] // 2):
                top, bottom = unpack_pair(
                    sigma_ref[2 * pair].astype(jnp.float32), sigma_ref[2 * pair + 1].astype(jnp.float32)
                )
                sigma[:ROW_T, pair * ROW_T : (pair + 1) * ROW_T] = top.astype(jnp.bfloat16)
                sigma[ROW_T:, pair * ROW_T : (pair + 1) * ROW_T] = bottom.astype(jnp.bfloat16)
    else:
        sigma = sigma_ref
    tile_0 = second_place * 16 + half * 8 + step * tiles
    columns = []
    for tile in range(tiles):
        live = reach_ref[block, tile_0 + tile] - hist_place * past_loc
        columns.append(
            jnp.concatenate(
                [
                    jnp.where(
                        past < live,
                        hist_ref[past * ROW_T : (past + 1) * ROW_T, tile * ROW_T : (tile + 1) * ROW_T],
                        jnp.zeros((), hist_ref.dtype),
                    )
                    for past in range(past_loc)
                ],
                0,
            )
        )
    masked = jnp.concatenate(columns, 1)
    term = jnp.dot(sigma[...], masked, preferred_element_type=jnp.float32)
    for tile in range(tiles):
        top = term[:ROW_T, tile * ROW_T : (tile + 1) * ROW_T]
        bottom = term[ROW_T:, tile * ROW_T : (tile + 1) * ROW_T]
        even, odd = unpack_pair(top, bottom)
        out_ref[2 * tile] = even.astype(out_ref.dtype)
        out_ref[2 * tile + 1] = odd.astype(out_ref.dtype)


def memory_terms(block, first_half, where, reach, sigma, history):
    rows, cols = history.shape
    from_pieces = sigma.ndim == 3
    steps = cols // 2 // TILE

    def hist_map(i, where_ref, reach_ref):
        own = where_ref[2]
        return (0, ((1 - own) if first_half else own) * steps + i)

    return pl.pallas_call(
        functools.partial(memory_kernel, block, first_half, from_pieces),
        out_shape=jax.ShapeDtypeStruct((cols // 2 // HALF, ROW_T, ROW_T), jnp.bfloat16),
        grid_spec=pltpu.PrefetchScalarGridSpec(
            num_scalar_prefetch=2,
            grid=(steps,),
            in_specs=[
                pl.BlockSpec(sigma.shape, lambda i, w, r: (0,) * sigma.ndim),
                pl.BlockSpec((rows, TILE), hist_map),
            ],
            out_specs=pl.BlockSpec((TILE // HALF, ROW_T, ROW_T), lambda i, w, r: (i, 0, 0)),
            scratch_shapes=[pltpu.VMEM((2 * ROW_T, rows), jnp.bfloat16)] if from_pieces else [],
        ),
        cost_estimate=pl.CostEstimate(
            flops=2 * 256 * rows * cols // 2, bytes_accessed=rows * cols + 1024 * 1024, transcendentals=0
        ),
        name=f"memory_{block}_{int(first_half)}",
    )(where, reach, sigma, history)


def step_kernel(first, last, where_ref, terms_ref, green_ref, step_ref, weight_ref, *outs):
    integral = terms_ref[0].astype(jnp.float32)
    for piece in range(1, terms_ref.shape[0]):
        integral = integral + terms_ref[piece].astype(jnp.float32)
    low = low_lanes(integral.shape)
    held = green_ref[...].astype(jnp.float32)
    turned = swap_halves(held)
    if first:
        before = jnp.where(where_ref[3] == 0, held, turned)
    else:
        before = turned
    source = integral + jnp.where(low, before, 0.0)
    dot = functools.partial(jnp.dot, precision=lax.Precision.HIGHEST, preferred_element_type=jnp.float32)
    moved = dot(step_ref[...], source)
    further = dot(step_ref[...], jnp.where(low, 0.0, swap_halves(moved)))
    rows = moved + further
    if last:
        piece = rows.astype(jnp.bfloat16)
    else:
        square = rows * rows
        piece = (weight_ref[...] * rows * square / (1.0 + square)).astype(jnp.bfloat16)
        outs[1][...] = rows
    for copy in range(outs[0].shape[0]):
        outs[0][copy] = piece


def advance(first, last, where, terms, green, step_inv, weights):
    whole = pl.BlockSpec(memory_space=pltpu.VMEM)
    shapes = [jax.ShapeDtypeStruct((16, ROW_T, ROW_T), jnp.bfloat16)]
    specs = [pl.BlockSpec((16, ROW_T, ROW_T), lambda i, w: (0, 0, 0))]
    if not last:
        shapes.append(jax.ShapeDtypeStruct((ROW_T, ROW_T), jnp.float32))
        specs.append(pl.BlockSpec((ROW_T, ROW_T), lambda i, w: (0, 0)))
    square = pl.BlockSpec((ROW_T, ROW_T), lambda i, w: (0, 0))
    green_spec = pl.BlockSpec((ROW_T, ROW_T), lambda i, w: (0, w[4])) if first else square
    out = pl.pallas_call(
        functools.partial(step_kernel, first, last),
        out_shape=tuple(shapes),
        grid_spec=pltpu.PrefetchScalarGridSpec(
            num_scalar_prefetch=1,
            grid=(1,),
            in_specs=[pl.BlockSpec(terms.shape, lambda i, w: (0, 0, 0)), green_spec, square, square],
            out_specs=tuple(specs),
        ),
        name=f"advance_{int(first)}{int(last)}",
    )(where, terms, green, step_inv, weights)
    return out[0], (None if last else out[1])


def spread_kernel(where_ref, own_ref, other_ref, out_ref):
    step = pl.program_id(0)
    mine = where_ref[2] == (step >= 8).astype(jnp.int32)

    def write(ref):
        top, bottom = unpack_pair(ref[0].astype(jnp.float32), ref[1].astype(jnp.float32))
        out_ref[:ROW_T] = top.astype(out_ref.dtype)
        out_ref[ROW_T:] = bottom.astype(out_ref.dtype)

    @pl.when(mine)
    def _():
        write(own_ref)

    @pl.when(jnp.logical_not(mine))
    def _():
        write(other_ref)


def spread_out(where, own, other):
    pair = pl.BlockSpec((2, ROW_T, ROW_T), lambda i, w: (lax.rem(i, 8), 0, 0))
    return pl.pallas_call(
        spread_kernel,
        out_shape=jax.ShapeDtypeStruct((2 * ROW_T, 16 * ROW_T), jnp.bfloat16),
        grid_spec=pltpu.PrefetchScalarGridSpec(
            num_scalar_prefetch=1,
            grid=(16,),
            in_specs=[pair, pair],
            out_specs=pl.BlockSpec((2 * ROW_T, ROW_T), lambda i, w: (0, i)),
        ),
        name="spread",
    )(where, own, other)


def exchange(x, axis):
    return lax.all_to_all(x, axis, 0, 0, tiled=True)


def local(history, self_rows, edge_rows, step_inv, coupling, reach):
    place = lax.axis_index(PLANE)
    core = lax.axis_index("c")
    where = jnp.stack(
        [lax.axis_index(HIST), lax.axis_index("z"), core, place % 2, core * 8 + place // 2]
    ).astype(jnp.int32)
    weights = jnp.broadcast_to(coupling[:, None], (ROW_T, ROW_T))
    swap = [(0, 1), (1, 0)]
    sigma, green = self_rows, edge_rows
    blocks = reach.shape[0]
    for block in range(blocks):
        last = block + 1 == blocks
        away = memory_terms(block, True, where, reach, sigma, history)
        arrived = lax.ppermute(away, "c", swap)
        kept = memory_terms(block, False, where, reach, sigma, history)
        pair = (kept.astype(jnp.float32) + arrived.astype(jnp.float32)).astype(jnp.bfloat16)
        terms = exchange(pair, PLANE)
        pieces, green = advance(block == 0, last, where, terms, green, step_inv, weights)
        if last:
            own = exchange(pieces, PLANE)
            return spread_out(where, own, lax.ppermute(own, "c", swap))
        sigma = exchange(exchange(pieces, "z"), PLANE)


def solution(mesh):
    torus = Mesh(mesh.devices.reshape(4, 4, 2, mesh.shape["second"]), ("x", "y", "c", "z"))
    placed = (P(HIST, "z"), P(None, HIST), P(None, "z"), P(), P(), P())
    return jax.shard_map(local, mesh=torus, in_specs=placed, out_specs=P(None, "z"), check_vma=False)
```

time: 299 us -> 242 us (0.81)
  blocking collectives: 257 us -> 146 us
  Pallas kernels: 0 us -> 51.5 us
  starting transfers between devices: 4.19 us -> 34.6 us
  matrix products: 17.6 us -> 0 us
  waiting for transfers between devices: 8.8 us -> 1.52 us
  local copies, waits for them, and re-layouts: 6.25 us -> 2.18 us
    all_to_all x15 -> x8, blocking collectives: 257 us -> 146 us  [exchange(): return lax.all_to_all(x, axis, 0, 0, tiled=True)]
    pallas_call x0 -> x10, Pallas kernels: none -> 51.5 us  [the longest x6 31.8 us: memory_terms(): pl.pallas_call(functools.partial(memory_kernel, block, first_half, from_p...]
    ppermute x0 -> x4, starting transfers between devices: none -> 34.6 us  [the longest x3 29.3 us: local(): arrived = lax.ppermute(away, 'c', swap)]
    dot_general x9 -> x0, matrix products: 17.6 us -> none  [the longest x3 11.2 us: local(): jnp.dot(sigma_rows, masked, preferred_element_type=jnp.float32)]
    all_to_all x1 -> x0, waiting for transfers between devices: 8.8 us -> none  [sent_to_all(): lax.all_to_all(jnp.broadcast_to(x[None], (devices, *x.shape)), axis, 0, 0...]
    all_to_all x1 -> x0, starting transfers between devices: 4.19 us -> none  [sent_to_all(): lax.all_to_all(jnp.broadcast_to(x[None], (devices, *x.shape)), axis, 0, 0...]
  transfers between devices with their start and end apart: 1 -> 4, of which waited for: 1 -> 1; matrix products, arithmetic and copies ran while one was open for 0% -> 0% of each run, Pallas kernels for 0% -> 7%
where the time goes in v1:
time: 242 us; the launch traced here: 240 us
  blocking collectives  146 us (60%)
  Pallas kernels  51.5 us (21%)
  starting transfers between devices  34.6 us (14%)
  other arithmetic  3.55 us (1%)
    all_to_all x8, blocking collectives, exchange(): return lax.all_to_all(x, axis, 0, 0, tiled=True)  146 us
    pallas_call x6, Pallas kernels, memory_terms(): pl.pallas_call(functools.partial(memory_kernel, block, first_half, from_p...  31.8 us
    ppermute x3, starting transfers between devices, local(): arrived = lax.ppermute(away, 'c', swap)  29.3 us
    pallas_call x1, Pallas kernels, spread_out(): pl.pallas_call(spread_kernel, out_shape=jax.ShapeDtypeStruct((2 * ROW_T,...  10.3 us
    pallas_call x3, Pallas kernels, advance(): pl.pallas_call(functools.partial(step_kernel, first, last), out_shape=tup...  9.5 us
    ppermute x1, starting transfers between devices, local(): return spread_out(where, own, lax.ppermute(own, 'c', swap))  5.31 us
  transfers between devices with their start and end apart: 4, of which 1 were waited for; matrix products, arithmetic and copies ran while one was open for 0% of the time, Pallas kernels for 7%

profile of v1, /device:TPU:1, one launch (start us, length us, event | category | flops | bytes accessed | tf_op | source)
XLA Modules:
  0.0 239.9 jit_solution(11676184445379247690)
XLA Ops:
  0.0 0.7 stack.23.where_ref
  0.7 5.1 %memory_0_1.1 = bf16[16,128,128]{2,1,0:T(8,128)(2,1)} custom-call(s32[5]{0:T(128)} %stack.23.where_ref, s32[3,256]{1,0:T(4,128)} %reach_ref.11, bf16[256,1024]{1,0:T(8,128)(2,1)} %sigma_ref.3, bf16[1024,2048]{1,0:T(8,128)(2,1)} %hist_ref.11), custom_call_target="tpu_custom_call" | custom-call | flops 536870912 | bytes 3145728 | tf_op jit(solution)/shard_map/memory_0_1/pallas_call | solution.py:89
  5.8 8.9 %collective-permute-start = (bf16[16,128,128]{2,1,0:T(8,128)(2,1)}, bf16[16,128,128]{2,1,0:T(8,128)(2,1)S(1)}, u32[]{:S(2)}, u32[]{:S(2)}) collective-permute-start(bf16[16,128,128]{2,1,0:T(8,128)(2,1)} %memory_0_1.1), channel_id=1, source_target_pairs={{0,16},{16,0},{1,17},{17,1},{2,18},{18,2},{3,19},{19,3},{4,20},{20... | collective-permute-start | bytes 1572872 | tf_op jit(solution)/shard_map/ppermute | solution.py:208
  14.7 5.1 %memory_0_0.1 = bf16[16,128,128]{2,1,0:T(8,128)(2,1)} custom-call(s32[5]{0:T(128)} %stack.23.where_ref, s32[3,256]{1,0:T(4,128)} %reach_ref.11, bf16[256,1024]{1,0:T(8,128)(2,1)} %sigma_ref.3, bf16[1024,2048]{1,0:T(8,128)(2,1)} %hist_ref.11), custom_call_target="tpu_custom_call" | custom-call | flops 536870912 | bytes 3145728 | tf_op jit(solution)/shard_map/memory_0_0/pallas_call | solution.py:89
  19.8 0.0 collective-permute-done
  19.8 1.2 add_convert_fusion.2
  21.0 13.9 %all_to_all.40.terms_ref = bf16[16,128,128]{2,1,0:T(8,128)(2,1)} all-to-all(bf16[16,128,128]{2,1,0:T(8,128)(2,1)S(1)} %add_convert_fusion.2), channel_id=1, replica_groups=mesh['x'=4,'y'=4,'c'=2,'z'=16] {'x','y'}, dimensions={0} | all-to-all | bytes 1048576 | tf_op jit(solution)/shard_map/all_to_all | solution.py:192
  34.9 0.7 broadcast_in_dim.2.weight_ref
  35.6 3.1 %advance_10.1 = (bf16[16,128,128]{2,1,0:T(8,128)(2,1)}, f32[128,128]{1,0:T(8,128)}) custom-call(s32[5]{0:T(128)} %stack.23.where_ref, bf16[16,128,128]{2,1,0:T(8,128)(2,1)} %all_to_all.40.terms_ref, bf16[128,2048]{1,0:T(8,128)(2,1)} %green_ref.1, f32[128,128]{1,0:T(8,128)} %step_ref.5, f32[128,128]{1,0:T(8,128)} %broadcast_in_dim.2.weight_ref), custom_call_target="tpu_custom_call" | custom-call | tf_op jit(solution)/shard_map/advance_10/pallas_call | solution.py:144
  38.7 33.9 %all_to_all.41 = bf16[16,128,128]{2,1,0:T(8,128)(2,1)S(1)} all-to-all(bf16[16,128,128]{2,1,0:T(8,128)(2,1)} %get-tuple-element.9), channel_id=1, replica_groups=mesh['x'=4,'y'=4,'c'=2,'z'=16] {'z'}, dimensions={0} | all-to-all | bytes 1048576 | tf_op jit(solution)/shard_map/all_to_all | solution.py:192
  72.7 14.7 %all_to_all.42.sigma_ref = bf16[16,128,128]{2,1,0:T(8,128)(2,1)} all-to-all(bf16[16,128,128]{2,1,0:T(8,128)(2,1)S(1)} %all_to_all.41), channel_id=1, replica_groups=mesh['x'=4,'y'=4,'c'=2,'z'=16] {'x','y'}, dimensions={0} | all-to-all | bytes 1048576 | tf_op jit(solution)/shard_map/all_to_all | solution.py:192
  87.4 5.4 %memory_1_1.1 = bf16[16,128,128]{2,1,0:T(8,128)(2,1)} custom-call(s32[5]{0:T(128)} %stack.23.where_ref, s32[3,256]{1,0:T(4,128)} %reach_ref.11, bf16[16,128,128]{2,1,0:T(8,128)(2,1)} %all_to_all.42.sigma_ref, bf16[1024,2048]{1,0:T(8,128)(2,1)} %hist_ref.11), custom_call_target="tpu_custom_call" | custom-call | flops 536870912 | bytes 3145728 | tf_op jit(solution)/shard_map/memory_1_1/pallas_call | solution.py:89
  92.8 10.2 %collective-permute-start.1 = (bf16[16,128,128]{2,1,0:T(8,128)(2,1)}, bf16[16,128,128]{2,1,0:T(8,128)(2,1)S(1)}, u32[]{:S(2)}, u32[]{:S(2)}) collective-permute-start(bf16[16,128,128]{2,1,0:T(8,128)(2,1)} %memory_1_1.1), channel_id=1, source_target_pairs={{0,16},{16,0},{1,17},{17,1},{2,18},{18,2},{3,19},{19,3},{4,20},{20... | collective-permute-start | bytes 1572872 | tf_op jit(solution)/shard_map/ppermute | solution.py:208
  103.0 5.4 %memory_1_0.1 = bf16[16,128,128]{2,1,0:T(8,128)(2,1)} custom-call(s32[5]{0:T(128)} %stack.23.where_ref, s32[3,256]{1,0:T(4,128)} %reach_ref.11, bf16[16,128,128]{2,1,0:T(8,128)(2,1)} %all_to_all.42.sigma_ref, bf16[1024,2048]{1,0:T(8,128)(2,1)} %hist_ref.11), custom_call_target="tpu_custom_call" | custom-call | flops 536870912 | bytes 3145728 | tf_op jit(solution)/shard_map/memory_1_0/pallas_call | solution.py:89
  108.4 0.0 collective-permute-done.1
  108.4 1.2 add_convert_fusion.1
  109.6 13.8 %all_to_all.43.terms_ref = bf16[16,128,128]{2,1,0:T(8,128)(2,1)} all-to-all(bf16[16,128,128]{2,1,0:T(8,128)(2,1)S(1)} %add_convert_fusion.1), channel_id=1, replica_groups=mesh['x'=4,'y'=4,'c'=2,'z'=16] {'x','y'}, dimensions={0} | all-to-all | bytes 1048576 | tf_op jit(solution)/shard_map/all_to_all | solution.py:192
  123.4 3.2 %advance_00.1 = (bf16[16,128,128]{2,1,0:T(8,128)(2,1)}, f32[128,128]{1,0:T(8,128)}) custom-call(s32[5]{0:T(128)} %stack.23.where_ref, bf16[16,128,128]{2,1,0:T(8,128)(2,1)} %all_to_all.43.terms_ref, f32[128,128]{1,0:T(8,128)} %get-tuple-element.10.green_ref, f32[128,128]{1,0:T(8,128)} %step_ref.5, f32[128,128]{1,0:T(8,128)} %broadcast_in_dim.2.weight_ref), custom_call_target="tpu_custom_call" | custom-call | tf_op jit(solution)/shard_map/advance_00/pallas_call | solution.py:144
  126.6 28.8 %all_to_all.44 = bf16[16,128,128]{2,1,0:T(8,128)(2,1)S(1)} all-to-all(bf16[16,128,128]{2,1,0:T(8,128)(2,1)} %get-tuple-element.11), channel_id=1, replica_groups=mesh['x'=4,'y'=4,'c'=2,'z'=16] {'z'}, dimensions={0} | all-to-all | bytes 1048576 | tf_op jit(solution)/shard_map/all_to_all | solution.py:192
  155.4 14.3 %all_to_all.45.sigma_ref = bf16[16,128,128]{2,1,0:T(8,128)(2,1)} all-to-all(bf16[16,128,128]{2,1,0:T(8,128)(2,1)S(1)} %all_to_all.44), channel_id=1, replica_groups=mesh['x'=4,'y'=4,'c'=2,'z'=16] {'x','y'}, dimensions={0} | all-to-all | bytes 1048576 | tf_op jit(solution)/shard_map/all_to_all | solution.py:192
  169.7 5.4 %memory_2_1.1 = bf16[16,128,128]{2,1,0:T(8,128)(2,1)} custom-call(s32[5]{0:T(128)} %stack.23.where_ref, s32[3,256]{1,0:T(4,128)} %reach_ref.11, bf16[16,128,128]{2,1,0:T(8,128)(2,1)} %all_to_all.45.sigma_ref, bf16[1024,2048]{1,0:T(8,128)(2,1)} %hist_ref.11), custom_call_target="tpu_custom_call" | custom-call | flops 536870912 | bytes 3145728 | tf_op jit(solution)/shard_map/memory_2_1/pallas_call | solution.py:89
  175.1 10.2 %collective-permute-start.2 = (bf16[16,128,128]{2,1,0:T(8,128)(2,1)}, bf16[16,128,128]{2,1,0:T(8,128)(2,1)S(1)}, u32[]{:S(2)}, u32[]{:S(2)}) collective-permute-start(bf16[16,128,128]{2,1,0:T(8,128)(2,1)} %memory_2_1.1), channel_id=1, source_target_pairs={{0,16},{16,0},{1,17},{17,1},{2,18},{18,2},{3,19},{19,3},{4,20},{20... | collective-permute-start | bytes 1572872 | tf_op jit(solution)/shard_map/ppermute | solution.py:208
  185.3 5.4 %memory_2_0.1 = bf16[16,128,128]{2,1,0:T(8,128)(2,1)} custom-call(s32[5]{0:T(128)} %stack.23.where_ref, s32[3,256]{1,0:T(4,128)} %reach_ref.11, bf16[16,128,128]{2,1,0:T(8,128)(2,1)} %all_to_all.45.sigma_ref, bf16[1024,2048]{1,0:T(8,128)(2,1)} %hist_ref.11), custom_call_target="tpu_custom_call" | custom-call | flops 536870912 | bytes 3145728 | tf_op jit(solution)/shard_map/memory_2_0/pallas_call | solution.py:89
  190.7 0.0 collective-permute-done.2
  190.7 1.2 add_convert_fusion
  191.9 13.8 %all_to_all.46.terms_ref = bf16[16,128,128]{2,1,0:T(8,128)(2,1)} all-to-all(bf16[16,128,128]{2,1,0:T(8,128)(2,1)S(1)} %add_convert_fusion), channel_id=1, replica_groups=mesh['x'=4,'y'=4,'c'=2,'z'=16] {'x','y'}, dimensions={0} | all-to-all | bytes 1048576 | tf_op jit(solution)/shard_map/all_to_all | solution.py:192
  205.7 3.2 %advance_01.1 = bf16[16,128,128]{2,1,0:T(8,128)(2,1)} custom-call(s32[5]{0:T(128)} %stack.23.where_ref, bf16[16,128,128]{2,1,0:T(8,128)(2,1)} %all_to_all.46.terms_ref, f32[128,128]{1,0:T(8,128)} %get-tuple-element.12.green_ref, f32[128,128]{1,0:T(8,128)} %step_ref.5, f32[128,128]{1,0:T(8,128)} %broadcast_in_dim.2.weight_ref), custom_call_target="tpu_custom_call" | custom-call | tf_op jit(solution)/shard_map/advance_01/pallas_call | solution.py:144
  208.9 13.1 %all_to_all.47.own_ref = bf16[16,128,128]{2,1,0:T(8,128)(2,1)S(1)} all-to-all(bf16[16,128,128]{2,1,0:T(8,128)(2,1)} %advance_01.1), channel_id=1, replica_groups=mesh['x'=4,'y'=4,'c'=2,'z'=16] {'x','y'}, dimensions={0} | all-to-all | bytes 1048576 | tf_op jit(solution)/shard_map/all_to_all | solution.py:192
  222.0 5.3 %collective-permute-start.3 = (bf16[16,128,128]{2,1,0:T(8,128)(2,1)S(1)}, bf16[16,128,128]{2,1,0:T(8,128)(2,1)S(1)}, u32[]{:S(2)}, u32[]{:S(2)}) collective-permute-start(bf16[16,128,128]{2,1,0:T(8,128)(2,1)S(1)} %all_to_all.47.own_ref), channel_id=1, source_target_pairs={{0,16},{16,0},{1,17},{17,1},{2,18},{18,2},{3,19},{19,3},{4,20},{20... | collective-permute-start | bytes 1572872 | tf_op jit(solution)/shard_map/ppermute | solution.py:215
  227.3 1.5 collective-permute-done.3.other_ref
  228.8 0.8 copy-done.1
  229.6 10.3 %spread.1 = bf16[256,2048]{1,0:T(8,128)(2,1)} custom-call(s32[5]{0:T(128)} %stack.23.where_ref, bf16[16,128,128]{2,1,0:T(8,128)(2,1)} %copy-done, bf16[16,128,128]{2,1,0:T(8,128)(2,1)} %copy-done.1), custom_call_target="tpu_custom_call" | custom-call | tf_op jit(solution)/shard_map/spread/pallas_call | solution.py:178
  (5 shorter events, 0.0 us)
Async XLA Ops:
  5.8 29.1 %copy-start.2 = (f32[128]{0:T(128)S(1)}, f32[128]{0:T(128)}, u32[]{:S(2)}) copy-start(f32[128]{0:T(128)} %param.10) | copy-start | bytes 1540
  5.8 14.0 %collective-permute-start = (bf16[16,128,128]{2,1,0:T(8,128)(2,1)}, bf16[16,128,128]{2,1,0:T(8,128)(2,1)S(1)}, u32[]{:S(2)}, u32[]{:S(2)}) collective-permute-start(bf16[16,128,128]{2,1,0:T(8,128)(2,1)} %memory_0_1.1), channel_id=1, source_target_pairs={{0,16},{16,0},{1,17},{17,1},{2,18},{18,2},{3,19},{19,3},{4,20},{20... | collective-permute-start | bytes 1572872 | tf_op jit(solution)/shard_map/ppermute | solution.py:208
  92.8 15.6 %collective-permute-start.1 = (bf16[16,128,128]{2,1,0:T(8,128)(2,1)}, bf16[16,128,128]{2,1,0:T(8,128)(2,1)S(1)}, u32[]{:S(2)}, u32[]{:S(2)}) collective-permute-start(bf16[16,128,128]{2,1,0:T(8,128)(2,1)} %memory_1_1.1), channel_id=1, source_target_pairs={{0,16},{16,0},{1,17},{17,1},{2,18},{18,2},{3,19},{19,3},{4,20},{20... | collective-permute-start | bytes 1572872 | tf_op jit(solution)/shard_map/ppermute | solution.py:208
  175.1 15.6 %collective-permute-start.2 = (bf16[16,128,128]{2,1,0:T(8,128)(2,1)}, bf16[16,128,128]{2,1,0:T(8,128)(2,1)S(1)}, u32[]{:S(2)}, u32[]{:S(2)}) collective-permute-start(bf16[16,128,128]{2,1,0:T(8,128)(2,1)} %memory_2_1.1), channel_id=1, source_target_pairs={{0,16},{16,0},{1,17},{17,1},{2,18},{18,2},{3,19},{19,3},{4,20},{20... | collective-permute-start | bytes 1572872 | tf_op jit(solution)/shard_map/ppermute | solution.py:208
  222.0 6.8 %copy-start = (bf16[16,128,128]{2,1,0:T(8,128)(2,1)}, bf16[16,128,128]{2,1,0:T(8,128)(2,1)S(1)}, u32[]{:S(2)}) copy-start(bf16[16,128,128]{2,1,0:T(8,128)(2,1)S(1)} %all_to_all.47.own_ref) | copy-start | bytes 1572868
  222.0 6.8 %collective-permute-start.3 = (bf16[16,128,128]{2,1,0:T(8,128)(2,1)S(1)}, bf16[16,128,128]{2,1,0:T(8,128)(2,1)S(1)}, u32[]{:S(2)}, u32[]{:S(2)}) collective-permute-start(bf16[16,128,128]{2,1,0:T(8,128)(2,1)S(1)} %all_to_all.47.own_ref), channel_id=1, source_target_pairs={{0,16},{16,0},{1,17},{17,1},{2,18},{18,2},{3,19},{19,3},{4,20},{20... | collective-permute-start | bytes 1572872 | tf_op jit(solution)/shard_map/ppermute | solution.py:215
  228.8 0.8 copy-start.1

commit v2 on v1

v2 whole, which is shorter than its diff:
```python
import functools

import jax
import jax.numpy as jnp
from jax import lax
from jax.experimental import pallas as pl
from jax.experimental.pallas import tpu as pltpu
from jax.sharding import Mesh
from jax.sharding import PartitionSpec as P

HIST = ("x", "y", "c")
PLANE = ("x", "y")
ROW_T = 128
HALF = 64
TILE = 256


def low_lanes(shape):
    return lax.broadcasted_iota(jnp.int32, shape, 1) < HALF


def swap_halves(value):
    return pltpu.roll(value, HALF, 1)


def unpack_pair(even, odd):
    low = low_lanes(even.shape)
    return (
        jnp.where(low, even, swap_halves(odd)),
        jnp.where(low, swap_halves(even), odd),
    )


VMEM = pl.BlockSpec(memory_space=pltpu.VMEM)
SMEM = pl.BlockSpec(memory_space=pltpu.SMEM)
PARAMS = pltpu.CompilerParams(vmem_limit_bytes=16 * 1024 * 1024)


def memory_kernel(block, first_half, from_pieces, reach_ref, sigma_ref, hist_ref, out_ref, *scratch):
    rows = hist_ref.shape[0]
    past_loc, tiles = rows // ROW_T, TILE // ROW_T
    hist_place, second_place, own = lax.axis_index(HIST), lax.axis_index("z"), lax.axis_index("c")
    half = 1 - own if first_half else own
    if from_pieces:
        sigma = scratch[0]
        for pair in range(sigma_ref.shape[0] // 2):
            top, bottom = unpack_pair(
                sigma_ref[2 * pair].astype(jnp.float32), sigma_ref[2 * pair + 1].astype(jnp.float32)
            )
            sigma[:ROW_T, pair * ROW_T : (pair + 1) * ROW_T] = top.astype(jnp.bfloat16)
            sigma[ROW_T:, pair * ROW_T : (pair + 1) * ROW_T] = bottom.astype(jnp.bfloat16)
    else:
        sigma = sigma_ref
    steps = hist_ref.shape[1] // 2 // TILE
    for step in range(steps):
        start = pl.multiple_of((half * steps + step) * TILE, TILE)
        tile_0 = second_place * 16 + half * 8 + step * tiles
        columns = []
        for tile in range(tiles):
            live = reach_ref[block, tile_0 + tile] - hist_place * past_loc
            columns.append(
                jnp.concatenate(
                    [
                        jnp.where(
                            past < live,
                            hist_ref[past * ROW_T : (past + 1) * ROW_T, pl.ds(start + tile * ROW_T, ROW_T)],
                            jnp.zeros((), hist_ref.dtype),
                        )
                        for past in range(past_loc)
                    ],
                    0,
                )
            )
        masked = jnp.concatenate(columns, 1)
        term = jnp.dot(sigma[...], masked, preferred_element_type=jnp.float32)
        for tile in range(tiles):
            top = term[:ROW_T, tile * ROW_T : (tile + 1) * ROW_T]
            bottom = term[ROW_T:, tile * ROW_T : (tile + 1) * ROW_T]
            even, odd = unpack_pair(top, bottom)
            out_ref[(step * tiles + tile) * 2] = even.astype(out_ref.dtype)
            out_ref[(step * tiles + tile) * 2 + 1] = odd.astype(out_ref.dtype)


def memory_terms(block, first_half, reach, sigma, history):
    rows, cols = history.shape
    from_pieces = sigma.ndim == 3
    return pl.pallas_call(
        functools.partial(memory_kernel, block, first_half, from_pieces),
        out_shape=jax.ShapeDtypeStruct((cols // 2 // HALF, ROW_T, ROW_T), jnp.bfloat16),
        in_specs=[SMEM, VMEM, VMEM],
        out_specs=VMEM,
        scratch_shapes=[pltpu.VMEM((2 * ROW_T, rows), jnp.bfloat16)] if from_pieces else [],
        cost_estimate=pl.CostEstimate(
            flops=2 * 256 * rows * cols // 2, bytes_accessed=rows * cols + 1024 * 1024, transcendentals=0
        ),
        compiler_params=PARAMS,
        name=f"memory_{block}_{int(first_half)}",
    )(reach, sigma, history)


def step_kernel(first, last, terms_ref, green_ref, step_ref, coupling_ref, *outs):
    integral = terms_ref[0].astype(jnp.float32)
    for piece in range(1, terms_ref.shape[0]):
        integral = integral + terms_ref[piece].astype(jnp.float32)
    low = low_lanes(integral.shape)
    if first:
        place = lax.axis_index("x") * 4 + lax.axis_index("y")
        tile = pl.multiple_of((lax.axis_index("c") * 8 + place // 2) * ROW_T, ROW_T)
        held = green_ref[:, pl.ds(tile, ROW_T)].astype(jnp.float32)
        before = jnp.where(place % 2 == 0, held, swap_halves(held))
    else:
        before = swap_halves(green_ref[...])
    source = integral + jnp.where(low, before, 0.0)
    dot = functools.partial(jnp.dot, precision=lax.Precision.HIGHEST, preferred_element_type=jnp.float32)
    moved = dot(step_ref[...], source)
    further = dot(step_ref[...], jnp.where(low, 0.0, swap_halves(moved)))
    rows = moved + further
    if last:
        piece = rows.astype(jnp.bfloat16)
    else:
        square = rows * rows
        piece = (coupling_ref[...] * rows * square / (1.0 + square)).astype(jnp.bfloat16)
        outs[1][...] = rows
    for copy in range(outs[0].shape[0]):
        outs[0][copy] = piece


def advance(first, last, terms, green, step_inv, coupling):
    shapes = [jax.ShapeDtypeStruct((16, ROW_T, ROW_T), jnp.bfloat16)]
    if not last:
        shapes.append(jax.ShapeDtypeStruct((ROW_T, ROW_T), jnp.float32))
    out = pl.pallas_call(
        functools.partial(step_kernel, first, last),
        out_shape=tuple(shapes),
        in_specs=[VMEM, VMEM, VMEM, VMEM],
        out_specs=(VMEM,) * len(shapes),
        compiler_params=PARAMS,
        name=f"advance_{int(first)}{int(last)}",
    )(terms, green, step_inv, coupling)
    return out[0], (None if last else out[1])


def spread_kernel(own_ref, other_ref, out_ref):
    def write(ref, half):
        for pair in range(8):
            top, bottom = unpack_pair(ref[2 * pair].astype(jnp.float32), ref[2 * pair + 1].astype(jnp.float32))
            start = pl.multiple_of((half * 8 + pair) * ROW_T, ROW_T)
            out_ref[:ROW_T, pl.ds(start, ROW_T)] = top.astype(out_ref.dtype)
            out_ref[ROW_T:, pl.ds(start, ROW_T)] = bottom.astype(out_ref.dtype)

    core = lax.axis_index("c")
    write(own_ref, core)
    write(other_ref, 1 - core)


def spread_out(own, other):
    return pl.pallas_call(
        spread_kernel,
        out_shape=jax.ShapeDtypeStruct((2 * ROW_T, 16 * ROW_T), jnp.bfloat16),
        in_specs=[VMEM, VMEM],
        out_specs=VMEM,
        compiler_params=PARAMS,
        name="spread",
    )(own, other)


def exchange(x, axis):
    return lax.all_to_all(x, axis, 0, 0, tiled=True)


def local(history, self_rows, edge_rows, step_inv, coupling, reach):
    weights = coupling[:, None]
    swap = [(0, 1), (1, 0)]
    sigma, green = self_rows, edge_rows
    blocks = reach.shape[0]
    for block in range(blocks):
        last = block + 1 == blocks
        away = memory_terms(block, True, reach, sigma, history)
        arrived = lax.ppermute(away, "c", swap)
        kept = memory_terms(block, False, reach, sigma, history)
        pair = (kept.astype(jnp.float32) + arrived.astype(jnp.float32)).astype(jnp.bfloat16)
        terms = exchange(pair, PLANE)
        pieces, green = advance(block == 0, last, terms, green, step_inv, weights)
        if last:
            own = exchange(pieces, PLANE)
            return spread_out(own, lax.ppermute(own, "c", swap))
        sigma = exchange(exchange(pieces, "z"), PLANE)


def solution(mesh):
    torus = Mesh(mesh.devices.reshape(4, 4, 2, mesh.shape["second"]), ("x", "y", "c", "z"))
    placed = (P(HIST, "z"), P(None, HIST), P(None, "z"), P(), P(), P())
    return jax.shard_map(local, mesh=torus, in_specs=placed, out_specs=P(None, "z"), check_vma=False)
```

time: 242 us -> 202 us (0.83)
  Pallas kernels: 51.5 us -> 13.1 us
  blocking collectives: 146 us -> 130 us
  waiting for transfers between devices: 1.52 us -> 11.5 us
  local copies, waits for them, and re-layouts: 2.18 us -> 6.25 us
  starting transfers between devices: 34.6 us -> 38.5 us
    pallas_call x6, Pallas kernels: 31.8 us -> 9.8 us  [memory_terms(): pl.pallas_call(functools.partial(memory_kernel, block, first_half, from_p...]
    all_to_all x8 -> x7, blocking collectives: 146 us -> 130 us  [exchange(): return lax.all_to_all(x, axis, 0, 0, tiled=True)]
    all_to_all x0 -> x1, waiting for transfers between devices: none -> 9.98 us  [exchange(): return lax.all_to_all(x, axis, 0, 0, tiled=True)]
    pallas_call x1, Pallas kernels: 10.3 us -> 1.42 us  [spread_out(): pl.pallas_call(spread_kernel, out_shape=jax.ShapeDtypeStruct((2 * ROW_T,...]
    pallas_call x3, Pallas kernels: 9.5 us -> 1.91 us  [advance(): pl.pallas_call(functools.partial(step_kernel, first, last), out_shape=tup...]
    unnamed x6 -> x18, local copies, waits for them, and re-layouts: 0.81 us -> 6.13 us
    all_to_all x0 -> x1, starting transfers between devices: none -> 3.57 us  [exchange(): return lax.all_to_all(x, axis, 0, 0, tiled=True)]
  transfers between devices with their start and end apart: 4 -> 5, of which waited for: 1 -> 2; matrix products, arithmetic and copies ran while one was open for 0% -> 0% of each run, Pallas kernels for 7% -> 2%
where the time goes in v2:
time: 202 us; the launch traced here: 201 us
  blocking collectives  130 us (64%)
  starting transfers between devices  38.5 us (19%)
  Pallas kernels  13.1 us (6%)
  waiting for transfers between devices  11.5 us (6%)
  local copies, waits for them, and re-layouts  6.25 us (3%)
    all_to_all x7, blocking collectives, exchange(): return lax.all_to_all(x, axis, 0, 0, tiled=True)  130 us
    ppermute x3, starting transfers between devices, local(): arrived = lax.ppermute(away, 'c', swap)  29.6 us
    all_to_all x1, waiting for transfers between devices, exchange(): return lax.all_to_all(x, axis, 0, 0, tiled=True)  9.98 us
    pallas_call x6, Pallas kernels, memory_terms(): pl.pallas_call(functools.partial(memory_kernel, block, first_half, from_p...  9.8 us
    unnamed x18, local copies, waits for them, and re-layouts  6.13 us
    ppermute x1, starting transfers between devices, local(): return spread_out(own, lax.ppermute(own, 'c', swap))  5.38 us
  transfers between devices with their start and end apart: 5, of which 2 were waited for; matrix products, arithmetic and copies ran while one was open for 0% of the time, Pallas kernels for 2%

profile of v2, /device:TPU:1, one launch (start us, length us, event | category | flops | bytes accessed | tf_op | source)
XLA Modules:
  0.0 201.3 jit_solution(1481710817646308463)
XLA Ops:
  0.0 2.2 %copy-done = bf16[1024,2048]{1,0:T(8,128)(2,1)S(1)} copy-done((bf16[1024,2048]{1,0:T(8,128)(2,1)S(1)}, bf16[1024,2048]{1,0:T(8,128)(2,1)}, u32[]{:S(2)}) %copy-start) | copy-done | bytes 4194328
  2.2 1.0 copy-done.3
  3.2 0.7 copy-done.6
  3.9 1.6 memory_0_1.1
  5.5 8.9 %collective-permute-start = (bf16[16,128,128]{2,1,0:T(8,128)(2,1)S(1)}, bf16[16,128,128]{2,1,0:T(8,128)(2,1)S(1)}, u32[]{:S(2)}, u32[]{:S(2)}) collective-permute-start(bf16[16,128,128]{2,1,0:T(8,128)(2,1)S(1)} %memory_0_1.1), channel_id=1, source_target_pairs={{0,16},{16,0},{1,17},{17,1},{2,18},{18,2},{3,19},{19,3},{4,20},{20... | collective-permute-start | bytes 1572872 | tf_op jit(solution)/shard_map/ppermute | solution.py:179
  14.4 1.6 memory_0_0.1
  16.0 0.9 add_convert_fusion.2
  16.9 3.6 %all-to-all-start = ((bf16[16,128,128]{2,1,0:T(8,128)(2,1)}), bf16[16,128,128]{2,1,0:T(8,128)(2,1)S(1)}, u32[]{:S(2)}, u32[]{:S(2)}) async-start(bf16[16,128,128]{2,1,0:T(8,128)(2,1)} %add_convert_fusion.2), calls=%async_computation | async-start | bytes 1048576 | tf_op jit(solution)/shard_map/all_to_all | solution.py:168
  20.5 0.1 copy.7.coupling_ref
  20.6 10.0 %all-to-all-done.terms_ref = bf16[16,128,128]{2,1,0:T(8,128)(2,1)S(1)} async-done(((bf16[16,128,128]{2,1,0:T(8,128)(2,1)}), bf16[16,128,128]{2,1,0:T(8,128)(2,1)S(1)}, u32[]{:S(2)}, u32[]{:S(2)}) %all-to-all-start) | async-done | bytes 524320 | tf_op jit(solution)/shard_map/all_to_all | solution.py:168
  30.6 0.7 advance_10.1
  31.3 35.1 %all_to_all.40 = bf16[16,128,128]{2,1,0:T(8,128)(2,1)S(1)} all-to-all(bf16[16,128,128]{2,1,0:T(8,128)(2,1)S(1)} %get-tuple-element.9), channel_id=1, replica_groups=mesh['x'=4,'y'=4,'c'=2,'z'=16] {'z'}, dimensions={0} | all-to-all | bytes 1048576 | tf_op jit(solution)/shard_map/all_to_all | solution.py:168
  66.4 13.1 %all_to_all.41.sigma_ref = bf16[16,128,128]{2,1,0:T(8,128)(2,1)S(1)} all-to-all(bf16[16,128,128]{2,1,0:T(8,128)(2,1)S(1)} %all_to_all.40), channel_id=1, replica_groups=mesh['x'=4,'y'=4,'c'=2,'z'=16] {'x','y'}, dimensions={0} | all-to-all | bytes 1048576 | tf_op jit(solution)/shard_map/all_to_all | solution.py:168
  79.5 2.2 %copy-done.1 = bf16[1024,2048]{1,0:T(8,128)(2,1)S(1)} copy-done((bf16[1024,2048]{1,0:T(8,128)(2,1)S(1)}, bf16[1024,2048]{1,0:T(8,128)(2,1)}, u32[]{:S(2)}) %copy-start.1) | copy-done | bytes 4194328
  81.7 1.7 memory_1_1.1
  83.4 10.5 %collective-permute-start.1 = (bf16[16,128,128]{2,1,0:T(8,128)(2,1)S(1)}, bf16[16,128,128]{2,1,0:T(8,128)(2,1)S(1)}, u32[]{:S(2)}, u32[]{:S(2)}) collective-permute-start(bf16[16,128,128]{2,1,0:T(8,128)(2,1)S(1)} %memory_1_1.1), channel_id=1, source_target_pairs={{0,16},{16,0},{1,17},{17,1},{2,18},{18,2},{3,19},{19,3},{4,20},{20... | collective-permute-start | bytes 1572872 | tf_op jit(solution)/shard_map/ppermute | solution.py:179
  94.0 1.7 memory_1_0.1
  95.7 0.1 add_convert_fusion.1
  95.8 13.2 %all_to_all.42.terms_ref = bf16[16,128,128]{2,1,0:T(8,128)(2,1)S(1)} all-to-all(bf16[16,128,128]{2,1,0:T(8,128)(2,1)S(1)} %add_convert_fusion.1), channel_id=1, replica_groups=mesh['x'=4,'y'=4,'c'=2,'z'=16] {'x','y'}, dimensions={0} | all-to-all | bytes 1048576 | tf_op jit(solution)/shard_map/all_to_all | solution.py:168
  109.0 0.6 advance_00.1
  109.6 28.8 %all_to_all.43 = bf16[16,128,128]{2,1,0:T(8,128)(2,1)S(1)} all-to-all(bf16[16,128,128]{2,1,0:T(8,128)(2,1)S(1)} %get-tuple-element.11), channel_id=1, replica_groups=mesh['x'=4,'y'=4,'c'=2,'z'=16] {'z'}, dimensions={0} | all-to-all | bytes 1048576 | tf_op jit(solution)/shard_map/all_to_all | solution.py:168
  138.5 14.1 %all_to_all.44.sigma_ref = bf16[16,128,128]{2,1,0:T(8,128)(2,1)S(1)} all-to-all(bf16[16,128,128]{2,1,0:T(8,128)(2,1)S(1)} %all_to_all.43), channel_id=1, replica_groups=mesh['x'=4,'y'=4,'c'=2,'z'=16] {'x','y'}, dimensions={0} | all-to-all | bytes 1048576 | tf_op jit(solution)/shard_map/all_to_all | solution.py:168
  152.6 1.7 memory_2_1.1
  154.3 10.2 %collective-permute-start.2 = (bf16[16,128,128]{2,1,0:T(8,128)(2,1)S(1)}, bf16[16,128,128]{2,1,0:T(8,128)(2,1)S(1)}, u32[]{:S(2)}, u32[]{:S(2)}) collective-permute-start(bf16[16,128,128]{2,1,0:T(8,128)(2,1)S(1)} %memory_2_1.1), channel_id=1, source_target_pairs={{0,16},{16,0},{1,17},{17,1},{2,18},{18,2},{3,19},{19,3},{4,20},{20... | collective-permute-start | bytes 1572872 | tf_op jit(solution)/shard_map/ppermute | solution.py:179
  164.5 1.7 memory_2_0.1
  166.2 0.1 add_convert_fusion
  166.3 13.2 %all_to_all.45.terms_ref = bf16[16,128,128]{2,1,0:T(8,128)(2,1)S(1)} all-to-all(bf16[16,128,128]{2,1,0:T(8,128)(2,1)S(1)} %add_convert_fusion), channel_id=1, replica_groups=mesh['x'=4,'y'=4,'c'=2,'z'=16] {'x','y'}, dimensions={0} | all-to-all | bytes 1048576 | tf_op jit(solution)/shard_map/all_to_all | solution.py:168
  179.5 0.6 advance_01.1
  180.1 12.8 %all_to_all.46.own_ref = bf16[16,128,128]{2,1,0:T(8,128)(2,1)S(1)} all-to-all(bf16[16,128,128]{2,1,0:T(8,128)(2,1)S(1)} %advance_01.1), channel_id=1, replica_groups=mesh['x'=4,'y'=4,'c'=2,'z'=16] {'x','y'}, dimensions={0} | all-to-all | bytes 1048576 | tf_op jit(solution)/shard_map/all_to_all | solution.py:168
  193.0 5.4 %collective-permute-start.3 = (bf16[16,128,128]{2,1,0:T(8,128)(2,1)S(1)}, bf16[16,128,128]{2,1,0:T(8,128)(2,1)S(1)}, u32[]{:S(2)}, u32[]{:S(2)}) collective-permute-start(bf16[16,128,128]{2,1,0:T(8,128)(2,1)S(1)} %all_to_all.46.own_ref), channel_id=1, source_target_pairs={{0,16},{16,0},{1,17},{17,1},{2,18},{18,2},{3,19},{19,3},{4,20},{20... | collective-permute-start | bytes 1572872 | tf_op jit(solution)/shard_map/ppermute | solution.py:186
  198.4 1.5 collective-permute-done.3.other_ref
  199.9 1.4 spread.1
  (17 shorter events, 0.0 us)
Async XLA Ops:
  0.0 2.2 %copy-start = (bf16[1024,2048]{1,0:T(8,128)(2,1)S(1)}, bf16[1024,2048]{1,0:T(8,128)(2,1)}, u32[]{:S(2)}) copy-start(bf16[1024,2048]{1,0:T(8,128)(2,1)} %hist_ref.11) | copy-start | bytes 12582916
  2.2 1.0 copy-start.3
  3.2 0.7 copy-start.6
  5.5 15.0 %copy-start.8 = (f32[128]{0:T(128)S(1)}, f32[128]{0:T(128)}, u32[]{:S(2)}) copy-start(f32[128]{0:T(128)} %param.10) | copy-start | bytes 1540
  5.5 25.1 %copy-start.4 = (f32[128,128]{1,0:T(8,128)S(1)}, f32[128,128]{1,0:T(8,128)}, u32[]{:S(2)}) copy-start(f32[128,128]{1,0:T(8,128)} %step_ref.5) | copy-start | bytes 196612
  5.5 25.1 %copy-start.5 = (bf16[128,2048]{1,0:T(8,128)(2,1)S(1)}, bf16[128,2048]{1,0:T(8,128)(2,1)}, u32[]{:S(2)}) copy-start(bf16[128,2048]{1,0:T(8,128)(2,1)} %green_ref.1) | copy-start | bytes 1572868
  5.5 10.5 %collective-permute-start = (bf16[16,128,128]{2,1,0:T(8,128)(2,1)S(1)}, bf16[16,128,128]{2,1,0:T(8,128)(2,1)S(1)}, u32[]{:S(2)}, u32[]{:S(2)}) collective-permute-start(bf16[16,128,128]{2,1,0:T(8,128)(2,1)S(1)} %memory_0_1.1), channel_id=1, source_target_pairs={{0,16},{16,0},{1,17},{17,1},{2,18},{18,2},{3,19},{19,3},{4,20},{20... | collective-permute-start | bytes 1572872 | tf_op jit(solution)/shard_map/ppermute | solution.py:179
  16.0 63.6 %copy-start.7 = (s32[3,256]{1,0:T(4,128)S(1)}, s32[3,256]{1,0:T(4,128)}, u32[]{:S(2)}) copy-start(s32[3,256]{1,0:T(4,128)} %reach_ref.11) | copy-start | bytes 9220
  16.9 13.7 %all-to-all-start = ((bf16[16,128,128]{2,1,0:T(8,128)(2,1)}), bf16[16,128,128]{2,1,0:T(8,128)(2,1)S(1)}, u32[]{:S(2)}, u32[]{:S(2)}) async-start(bf16[16,128,128]{2,1,0:T(8,128)(2,1)} %add_convert_fusion.2), calls=%async_computation | async-start | bytes 1048576 | tf_op jit(solution)/shard_map/all_to_all | solution.py:168
  79.5 2.2 %copy-start.1 = (bf16[1024,2048]{1,0:T(8,128)(2,1)S(1)}, bf16[1024,2048]{1,0:T(8,128)(2,1)}, u32[]{:S(2)}) copy-start(bf16[1024,2048]{1,0:T(8,128)(2,1)} %hist_ref.11) | copy-start | bytes 12582916
  83.4 69.2 %copy-start.2 = (bf16[1024,2048]{1,0:T(8,128)(2,1)S(1)}, bf16[1024,2048]{1,0:T(8,128)(2,1)}, u32[]{:S(2)}) copy-start(bf16[1024,2048]{1,0:T(8,128)(2,1)} %hist_ref.11) | copy-start | bytes 12582916
  83.4 12.2 %collective-permute-start.1 = (bf16[16,128,128]{2,1,0:T(8,128)(2,1)S(1)}, bf16[16,128,128]{2,1,0:T(8,128)(2,1)S(1)}, u32[]{:S(2)}, u32[]{:S(2)}) collective-permute-start(bf16[16,128,128]{2,1,0:T(8,128)(2,1)S(1)} %memory_1_1.1), channel_id=1, source_target_pairs={{0,16},{16,0},{1,17},{17,1},{2,18},{18,2},{3,19},{19,3},{4,20},{20... | collective-permute-start | bytes 1572872 | tf_op jit(solution)/shard_map/ppermute | solution.py:179
  154.3 11.8 %collective-permute-start.2 = (bf16[16,128,128]{2,1,0:T(8,128)(2,1)S(1)}, bf16[16,128,128]{2,1,0:T(8,128)(2,1)S(1)}, u32[]{:S(2)}, u32[]{:S(2)}) collective-permute-start(bf16[16,128,128]{2,1,0:T(8,128)(2,1)S(1)} %memory_2_1.1), channel_id=1, source_target_pairs={{0,16},{16,0},{1,17},{17,1},{2,18},{18,2},{3,19},{19,3},{4,20},{20... | collective-permute-start | bytes 1572872 | tf_op jit(solution)/shard_map/ppermute | solution.py:179
  193.0 6.9 %collective-permute-start.3 = (bf16[16,128,128]{2,1,0:T(8,128)(2,1)S(1)}, bf16[16,128,128]{2,1,0:T(8,128)(2,1)S(1)}, u32[]{:S(2)}, u32[]{:S(2)}) collective-permute-start(bf16[16,128,128]{2,1,0:T(8,128)(2,1)S(1)} %all_to_all.46.own_ref), channel_id=1, source_target_pairs={{0,16},{16,0},{1,17},{17,1},{2,18},{18,2},{3,19},{19,3},{4,20},{20... | collective-permute-start | bytes 1572872 | tf_op jit(solution)/shard_map/ppermute | solution.py:186

commit v3 on v2

--- a/solution.py
+++ b/solution.py
@@ -9,7 +9,8 @@
 from jax.sharding import PartitionSpec as P
 
 HIST = ("x", "y", "c")
-PLANE = ("x", "y")
+PLANE = ("y", "x")
+SECOND = ("far", "near")
 ROW_T = 128
 HALF = 64
 TILE = 256
@@ -36,10 +37,39 @@
 PARAMS = pltpu.CompilerParams(vmem_limit_bytes=16 * 1024 * 1024)
 
 
+def column_tile(block, half, step, reach_ref, sigma, hist_ref, out_ref):
+    past_loc, tiles = hist_ref.shape[0] // ROW_T, TILE // ROW_T
+    steps = hist_ref.shape[1] // 2 // TILE
+    start = pl.multiple_of((half * steps + step) * TILE, TILE)
+    tile_0 = lax.axis_index(SECOND) * (2 * steps * tiles) + (half * steps + step) * tiles
+    columns = []
+    for tile in range(tiles):
+        live = reach_ref[block, tile_0 + tile] - lax.axis_index(HIST) * past_loc
+        columns.append(
+            jnp.concatenate(
+                [
+                    jnp.where(
+                        past < live,
+                        hist_ref[past * ROW_T : (past + 1) * ROW_T, pl.ds(start + tile * ROW_T, ROW_T)],
+                        jnp.zeros((), hist_ref.dtype),
+                    )
+                    for past in range(past_loc)
+                ],
+                0,
+            )
+        )
+    masked = jnp.concatenate(columns, 1)
+    term = jnp.dot(sigma[...], masked, preferred_element_type=jnp.float32)
+    for tile in range(tiles):
+        top = term[:ROW_T, tile * ROW_T : (tile + 1) * ROW_T]
+        bottom = term[ROW_T:, tile * ROW_T : (tile + 1) * ROW_T]
+        even, odd = unpack_pair(top, bottom)
+        out_ref[(step * tiles + tile) * 2] = even.astype(out_ref.dtype)
+        out_ref[(step * tiles + tile) * 2 + 1] = odd.astype(out_ref.dtype)
+
+
 def memory_kernel(block, first_half, from_pieces, reach_ref, sigma_ref, hist_ref, out_ref, *scratch):
-    rows = hist_ref.shape[0]
-    past_loc, tiles = rows // ROW_T, TILE // ROW_T
-    hist_place, second_place, own = lax.axis_index(HIST), lax.axis_index("z"), lax.axis_index("c")
+    own = lax.axis_index("c")
     half = 1 - own if first_half else own
     if from_pieces:
         sigma = scratch[0]
@@ -51,34 +81,56 @@
             sigma[ROW_T:, pair * ROW_T : (pair + 1) * ROW_T] = bottom.astype(jnp.bfloat16)
     else:
         sigma = sigma_ref
-    steps = hist_ref.shape[1] // 2 // TILE
+    for step in range(hist_ref.shape[1] // 2 // TILE):
+        column_tile(block, half, step, reach_ref, sigma, hist_ref, out_ref)
+
+
+def first_kernel(reach_hbm, sigma_hbm, hist_hbm, out_ref, hist_ref, sigma_ref, reach_ref, sems):
+    steps = hist_hbm.shape[1] // 2 // TILE
+    own = lax.axis_index("c")
+    copies = [
+        pltpu.make_async_copy(reach_hbm, reach_ref, sems.at[0]),
+        pltpu.make_async_copy(sigma_hbm, sigma_ref, sems.at[1]),
+    ]
+    for half in (1 - own, own):
+        for step in range(steps):
+            part = pl.ds(pl.multiple_of((half * steps + step) * TILE, TILE), TILE)
+            copies.append(
+                pltpu.make_async_copy(hist_hbm.at[:, part], hist_ref.at[:, part], sems.at[len(copies)])
+            )
+    for copy in copies:
+        copy.start()
+    copies[0].wait()
+    copies[1].wait()
     for step in range(steps):
-        start = pl.multiple_of((half * steps + step) * TILE, TILE)
-        tile_0 = second_place * 16 + half * 8 + step * tiles
-        columns = []
-        for tile in range(tiles):
-            live = reach_ref[block, tile_0 + tile] - hist_place * past_loc
-            columns.append(
-                jnp.concatenate(
-                    [
-                        jnp.where(
-                            past < live,
-                            hist_ref[past * ROW_T : (past + 1) * ROW_T, pl.ds(start + tile * ROW_T, ROW_T)],
-                            jnp.zeros((), hist_ref.dtype),
-                        )
-                        for past in range(past_loc)
-                    ],
-                    0,
-                )
-            )
-        masked = jnp.concatenate(columns, 1)
-        term = jnp.dot(sigma[...], masked, preferred_element_type=jnp.float32)
-        for tile in range(tiles):
-            top = term[:ROW_T, tile * ROW_T : (tile + 1) * ROW_T]
-            bottom = term[ROW_T:, tile * ROW_T : (tile + 1) * ROW_T]
-            even, odd = unpack_pair(top, bottom)
-            out_ref[(step * tiles + tile) * 2] = even.astype(out_ref.dtype)
-            out_ref[(step * tiles + tile) * 2 + 1] = odd.astype(out_ref.dtype)
+        copies[2 + step].wait()
+        column_tile(0, 1 - own, step, reach_ref, sigma_ref, hist_ref, out_ref)
+    for step in range(steps):
+        copies[2 + steps + step].wait()
+
+
+def first_terms(reach, sigma, history):
+    rows, cols = history.shape
+    there = pl.BlockSpec(memory_space=pltpu.HBM)
+    return pl.pallas_call(
+        first_kernel,
+        out_shape=(
+            jax.ShapeDtypeStruct((cols // 2 // HALF, ROW_T, ROW_T), jnp.bfloat16),
+            jax.ShapeDtypeStruct(history.shape, history.dtype),
+        ),
+        in_specs=[there, there, there],
+        out_specs=(VMEM, VMEM),
+        scratch_shapes=[
+            pltpu.VMEM(sigma.shape, sigma.dtype),
+            pltpu.SMEM(reach.shape, reach.dtype),
+            pltpu.SemaphoreType.DMA((2 + cols // TILE,)),
+        ],
+        cost_estimate=pl.CostEstimate(
+            flops=2 * 256 * rows * cols // 2, bytes_accessed=2 * rows * cols + 1024 * 1024, transcendentals=0
+        ),
+        compiler_params=PARAMS,
+        name="memory_first",
+    )(reach, sigma, history)
 
 
 def memory_terms(block, first_half, reach, sigma, history):
@@ -104,7 +156,7 @@
         integral = integral + terms_ref[piece].astype(jnp.float32)
     low = low_lanes(integral.shape)
     if first:
-        place = lax.axis_index("x") * 4 + lax.axis_index("y")
+        place = lax.axis_index(PLANE)
         tile = pl.multiple_of((lax.axis_index("c") * 8 + place // 2) * ROW_T, ROW_T)
         held = green_ref[:, pl.ds(tile, ROW_T)].astype(jnp.float32)
         before = jnp.where(place % 2 == 0, held, swap_halves(held))
@@ -118,15 +170,16 @@
     if last:
         piece = rows.astype(jnp.bfloat16)
     else:
+        weights = jnp.broadcast_to(coupling_ref[...], rows.shape).T
         square = rows * rows
-        piece = (coupling_ref[...] * rows * square / (1.0 + square)).astype(jnp.bfloat16)
+        piece = (weights * rows * square / (1.0 + square)).astype(jnp.bfloat16)
         outs[1][...] = rows
     for copy in range(outs[0].shape[0]):
         outs[0][copy] = piece
 
 
 def advance(first, last, terms, green, step_inv, coupling):
-    shapes = [jax.ShapeDtypeStruct((16, ROW_T, ROW_T), jnp.bfloat16)]
+    shapes = [jax.ShapeDtypeStruct((16 if last else 4, ROW_T, ROW_T), jnp.bfloat16)]
     if not last:
         shapes.append(jax.ShapeDtypeStruct((ROW_T, ROW_T), jnp.float32))
     out = pl.pallas_call(
@@ -169,25 +222,30 @@
 
 
 def local(history, self_rows, edge_rows, step_inv, coupling, reach):
-    weights = coupling[:, None]
     swap = [(0, 1), (1, 0)]
-    sigma, green = self_rows, edge_rows
+    weights = coupling[None, :]
+    sigma, green, held = self_rows, edge_rows, history
     blocks = reach.shape[0]
     for block in range(blocks):
         last = block + 1 == blocks
-        away = memory_terms(block, True, reach, sigma, history)
+        if block == 0:
+            away, held = first_terms(reach, sigma, history)
+        else:
+            away = memory_terms(block, True, reach, sigma, held)
         arrived = lax.ppermute(away, "c", swap)
-        kept = memory_terms(block, False, reach, sigma, history)
+        kept = memory_terms(block, False, reach, sigma, held)
         pair = (kept.astype(jnp.float32) + arrived.astype(jnp.float32)).astype(jnp.bfloat16)
         terms = exchange(pair, PLANE)
         pieces, green = advance(block == 0, last, terms, green, step_inv, weights)
         if last:
             own = exchange(pieces, PLANE)
             return spread_out(own, lax.ppermute(own, "c", swap))
-        sigma = exchange(exchange(pieces, "z"), PLANE)
+        distant = exchange(pieces, "far")
+        around = jnp.broadcast_to(distant[None], (4, *distant.shape)).reshape(16, ROW_T, ROW_T)
+        sigma = exchange(exchange(around, "near"), PLANE)
 
 
 def solution(mesh):
-    torus = Mesh(mesh.devices.reshape(4, 4, 2, mesh.shape["second"]), ("x", "y", "c", "z"))
-    placed = (P(HIST, "z"), P(None, HIST), P(None, "z"), P(), P(), P())
-    return jax.shard_map(local, mesh=torus, in_specs=placed, out_specs=P(None, "z"), check_vma=False)
+    torus = Mesh(mesh.devices.reshape(4, 4, 2, 4, 4), ("x", "y", "c", "far", "near"))
+    placed = (P(HIST, SECOND), P(None, HIST), P(None, SECOND), P(), P(), P())
+    return jax.shard_map(local, mesh=torus, in_specs=placed, out_specs=P(None, SECOND), check_vma=False)

time: 202 us -> 199 us (0.985)
  blocking collectives: 130 us -> 154 us
  starting transfers between devices: 38.5 us -> 23 us
  waiting for transfers between devices: 11.5 us -> 1.52 us
  local copies, waits for them, and re-layouts: 6.25 us -> 4.13 us
    all_to_all x7 -> x10, blocking collectives: 130 us -> 154 us  [exchange(): return lax.all_to_all(x, axis, 0, 0, tiled=True)]
    ppermute x3, starting transfers between devices: 29.6 us -> 19 us  [local(): arrived = lax.ppermute(away, 'c', swap)]
    all_to_all x1 -> x0, waiting for transfers between devices: 9.98 us -> none  [exchange(): return lax.all_to_all(x, axis, 0, 0, tiled=True)]
    all_to_all x1 -> x0, starting transfers between devices: 3.57 us -> none  [exchange(): return lax.all_to_all(x, axis, 0, 0, tiled=True)]
    pallas_call x0 -> x1, Pallas kernels: none -> 3.23 us  [first_terms(): pl.pallas_call(first_kernel, out_shape=(jax.ShapeDtypeStruct((cols // 2 /...]
    unnamed x18 -> x14, local copies, waits for them, and re-layouts: 6.13 us -> 3.94 us
    pallas_call x6 -> x5, Pallas kernels: 9.8 us -> 8.29 us  [memory_terms(): pl.pallas_call(functools.partial(memory_kernel, block, first_half, from_p...]
  transfers between devices with their start and end apart: 5 -> 4, of which waited for: 2 -> 1; matrix products, arithmetic and copies ran while one was open for 0% -> 0% of each run, Pallas kernels for 2% -> 2%
where the time goes in v3:
time: 199 us; the launch traced here: 198 us
  blocking collectives  154 us (77%)
  starting transfers between devices  23 us (12%)
  Pallas kernels  14.8 us (7%)
  local copies, waits for them, and re-layouts  4.13 us (2%)
    all_to_all x10, blocking collectives, exchange(): return lax.all_to_all(x, axis, 0, 0, tiled=True)  154 us
    ppermute x3, starting transfers between devices, local(): arrived = lax.ppermute(away, 'c', swap)  19 us
    pallas_call x5, Pallas kernels, memory_terms(): pl.pallas_call(functools.partial(memory_kernel, block, first_half, from_p...  8.29 us
    ppermute x1, starting transfers between devices, local(): return spread_out(own, lax.ppermute(own, 'c', swap))  4.03 us
  transfers between devices with their start and end apart: 4, of which 1 were waited for; matrix products, arithmetic and copies ran while one was open for 0% of the time, Pallas kernels for 2%

profile of v3, /device:TPU:1, one launch (start us, length us, event | category | flops | bytes accessed | tf_op | source)
XLA Modules:
  0.0 198.2 jit_solution(386288285896596026)
XLA Ops:
  0.0 2.2 %copy-done = bf16[1024,2048]{1,0:T(8,128)(2,1)S(1)} copy-done((bf16[1024,2048]{1,0:T(8,128)(2,1)S(1)}, bf16[1024,2048]{1,0:T(8,128)(2,1)}, u32[]{:S(2)}) %copy-start) | copy-done | bytes 4194328
  2.2 1.0 copy-done.1
  3.2 0.7 copy-done.4
  3.9 3.2 %memory_first.1 = (bf16[16,128,128]{2,1,0:T(8,128)(2,1)S(1)}, bf16[1024,2048]{1,0:T(8,128)(2,1)S(1)}) custom-call(s32[3,256]{1,0:T(4,128)S(1)} %copy-done.4, bf16[256,1024]{1,0:T(8,128)(2,1)S(1)} %copy-done.1, bf16[1024,2048]{1,0:T(8,128)(2,1)S(1)} %copy-done), custom_call_target="tpu_custom_call" | custom-call | flops 536870912 | bytes 5242880 | tf_op jit(solution)/shard_map/memory_first/pallas_call | solution.py:115
  7.2 8.9 %collective-permute-start = (bf16[16,128,128]{2,1,0:T(8,128)(2,1)S(1)}, bf16[16,128,128]{2,1,0:T(8,128)(2,1)S(1)}, u32[]{:S(2)}, u32[]{:S(2)}) collective-permute-start(bf16[16,128,128]{2,1,0:T(8,128)(2,1)S(1)} %get-tuple-element.12), channel_id=1, source_target_pairs={{0,16},{16,0},{1,17},{17,1},{2,18},{18,2},{3,19},{19,3},{4,20},{20... | collective-permute-start | bytes 1572872 | tf_op jit(solution)/shard_map/ppermute | solution.py:235
  16.1 1.6 memory_0_0.1
  17.7 0.1 add_convert_fusion.2
  17.8 13.7 %all_to_all.50.terms_ref = bf16[16,128,128]{2,1,0:T(8,128)(2,1)S(1)} all-to-all(bf16[16,128,128]{2,1,0:T(8,128)(2,1)S(1)} %add_convert_fusion.2), channel_id=1, replica_groups=mesh['x'=4,'y'=4,'c'=2,'far'=4,'near'=4] {'y','x'}, dimensions={0} | all-to-all | bytes 1048576 | tf_op jit(solution)/shard_map/all_to_all | solution.py:221
  31.6 0.6 advance_10.1
  32.2 25.2 %all_to_all.51 = bf16[4,128,128]{2,1,0:T(8,128)(2,1)S(1)} all-to-all(bf16[4,128,128]{2,1,0:T(8,128)(2,1)S(1)} %get-tuple-element.13), channel_id=1, replica_groups=mesh['x'=4,'y'=4,'c'=2,'far'=4,'near'=4] {'far'}, dimensions={0} | all-to-all | bytes 262144 | tf_op jit(solution)/shard_map/all_to_all | solution.py:221
  57.4 0.1 broadcast_in_dim.7
  57.5 13.4 %all_to_all.52 = bf16[16,128,128]{2,1,0:T(8,128)(2,1)S(1)} all-to-all(bf16[16,128,128]{2,1,0:T(8,128)(2,1)S(1)} %bitcast.6), channel_id=1, replica_groups=mesh['x'=4,'y'=4,'c'=2,'far'=4,'near'=4] {'near'}, dimensions={0} | all-to-all | bytes 1048576 | tf_op jit(solution)/shard_map/all_to_all | solution.py:221
  70.9 16.4 %all_to_all.53.sigma_ref = bf16[16,128,128]{2,1,0:T(8,128)(2,1)S(1)} all-to-all(bf16[16,128,128]{2,1,0:T(8,128)(2,1)S(1)} %all_to_all.52), channel_id=1, replica_groups=mesh['x'=4,'y'=4,'c'=2,'far'=4,'near'=4] {'y','x'}, dimensions={0} | all-to-all | bytes 1048576 | tf_op jit(solution)/shard_map/all_to_all | solution.py:221
  87.3 1.7 memory_1_1.1
  89.0 5.0 %collective-permute-start.1 = (bf16[16,128,128]{2,1,0:T(8,128)(2,1)S(1)}, bf16[16,128,128]{2,1,0:T(8,128)(2,1)S(1)}, u32[]{:S(2)}, u32[]{:S(2)}) collective-permute-start(bf16[16,128,128]{2,1,0:T(8,128)(2,1)S(1)} %memory_1_1.1), channel_id=1, source_target_pairs={{0,16},{16,0},{1,17},{17,1},{2,18},{18,2},{3,19},{19,3},{4,20},{20... | collective-permute-start | bytes 1572872 | tf_op jit(solution)/shard_map/ppermute | solution.py:235
  94.0 1.7 memory_1_0.1
  95.7 0.1 add_convert_fusion.1
  95.8 13.5 %all_to_all.54.terms_ref = bf16[16,128,128]{2,1,0:T(8,128)(2,1)S(1)} all-to-all(bf16[16,128,128]{2,1,0:T(8,128)(2,1)S(1)} %add_convert_fusion.1), channel_id=1, replica_groups=mesh['x'=4,'y'=4,'c'=2,'far'=4,'near'=4] {'y','x'}, dimensions={0} | all-to-all | bytes 1048576 | tf_op jit(solution)/shard_map/all_to_all | solution.py:221
  109.3 0.6 advance_00.1
  109.9 17.4 %all_to_all.55 = bf16[4,128,128]{2,1,0:T(8,128)(2,1)S(1)} all-to-all(bf16[4,128,128]{2,1,0:T(8,128)(2,1)S(1)} %get-tuple-element.15), channel_id=1, replica_groups=mesh['x'=4,'y'=4,'c'=2,'far'=4,'near'=4] {'far'}, dimensions={0} | all-to-all | bytes 262144 | tf_op jit(solution)/shard_map/all_to_all | solution.py:221
  127.4 14.8 %all_to_all.56 = bf16[16,128,128]{2,1,0:T(8,128)(2,1)S(1)} all-to-all(bf16[16,128,128]{2,1,0:T(8,128)(2,1)S(1)} %bitcast.7), channel_id=1, replica_groups=mesh['x'=4,'y'=4,'c'=2,'far'=4,'near'=4] {'near'}, dimensions={0} | all-to-all | bytes 1048576 | tf_op jit(solution)/shard_map/all_to_all | solution.py:221
  142.2 12.7 %all_to_all.57.sigma_ref = bf16[16,128,128]{2,1,0:T(8,128)(2,1)S(1)} all-to-all(bf16[16,128,128]{2,1,0:T(8,128)(2,1)S(1)} %all_to_all.56), channel_id=1, replica_groups=mesh['x'=4,'y'=4,'c'=2,'far'=4,'near'=4] {'y','x'}, dimensions={0} | all-to-all | bytes 1048576 | tf_op jit(solution)/shard_map/all_to_all | solution.py:221
  154.9 1.7 memory_2_1.1
  156.6 5.1 %collective-permute-start.2 = (bf16[16,128,128]{2,1,0:T(8,128)(2,1)S(1)}, bf16[16,128,128]{2,1,0:T(8,128)(2,1)S(1)}, u32[]{:S(2)}, u32[]{:S(2)}) collective-permute-start(bf16[16,128,128]{2,1,0:T(8,128)(2,1)S(1)} %memory_2_1.1), channel_id=1, source_target_pairs={{0,16},{16,0},{1,17},{17,1},{2,18},{18,2},{3,19},{19,3},{4,20},{20... | collective-permute-start | bytes 1572872 | tf_op jit(solution)/shard_map/ppermute | solution.py:235
  161.7 1.7 memory_2_0.1
  163.4 0.1 add_convert_fusion
  163.6 13.6 %all_to_all.58.terms_ref = bf16[16,128,128]{2,1,0:T(8,128)(2,1)S(1)} all-to-all(bf16[16,128,128]{2,1,0:T(8,128)(2,1)S(1)} %add_convert_fusion), channel_id=1, replica_groups=mesh['x'=4,'y'=4,'c'=2,'far'=4,'near'=4] {'y','x'}, dimensions={0} | all-to-all | bytes 1048576 | tf_op jit(solution)/shard_map/all_to_all | solution.py:221
  177.1 0.6 advance_01.1
  177.8 13.5 %all_to_all.59.own_ref = bf16[16,128,128]{2,1,0:T(8,128)(2,1)S(1)} all-to-all(bf16[16,128,128]{2,1,0:T(8,128)(2,1)S(1)} %advance_01.1), channel_id=1, replica_groups=mesh['x'=4,'y'=4,'c'=2,'far'=4,'near'=4] {'y','x'}, dimensions={0} | all-to-all | bytes 1048576 | tf_op jit(solution)/shard_map/all_to_all | solution.py:221
  191.2 4.0 %collective-permute-start.3 = (bf16[16,128,128]{2,1,0:T(8,128)(2,1)S(1)}, bf16[16,128,128]{2,1,0:T(8,128)(2,1)S(1)}, u32[]{:S(2)}, u32[]{:S(2)}) collective-permute-start(bf16[16,128,128]{2,1,0:T(8,128)(2,1)S(1)} %all_to_all.59.own_ref), channel_id=1, source_target_pairs={{0,16},{16,0},{1,17},{17,1},{2,18},{18,2},{3,19},{19,3},{4,20},{20... | collective-permute-start | bytes 1572872 | tf_op jit(solution)/shard_map/ppermute | solution.py:242
  195.3 1.5 collective-permute-done.3.other_ref
  196.8 1.4 spread.1
  (15 shorter events, 0.1 us)
Async XLA Ops:
  0.0 2.2 %copy-start = (bf16[1024,2048]{1,0:T(8,128)(2,1)S(1)}, bf16[1024,2048]{1,0:T(8,128)(2,1)}, u32[]{:S(2)}) copy-start(bf16[1024,2048]{1,0:T(8,128)(2,1)} %hist_hbm.1) | copy-start | bytes 12582916
  2.2 1.0 copy-start.1
  3.2 0.7 copy-start.4
  7.2 24.4 %copy-start.2 = (f32[128,128]{1,0:T(8,128)S(1)}, f32[128,128]{1,0:T(8,128)}, u32[]{:S(2)}) copy-start(f32[128,128]{1,0:T(8,128)} %step_ref.5) | copy-start | bytes 196612
  7.2 24.4 %copy-start.3 = (bf16[128,2048]{1,0:T(8,128)(2,1)S(1)}, bf16[128,2048]{1,0:T(8,128)(2,1)}, u32[]{:S(2)}) copy-start(bf16[128,2048]{1,0:T(8,128)(2,1)} %green_ref.1) | copy-start | bytes 1572868
  7.2 24.4 %copy-start.6 = (f32[128]{0:T(128)S(1)}, f32[128]{0:T(128)}, u32[]{:S(2)}) copy-start(f32[128]{0:T(128)} %param.10) | copy-start | bytes 1540
  7.2 10.5 %collective-permute-start = (bf16[16,128,128]{2,1,0:T(8,128)(2,1)S(1)}, bf16[16,128,128]{2,1,0:T(8,128)(2,1)S(1)}, u32[]{:S(2)}, u32[]{:S(2)}) collective-permute-start(bf16[16,128,128]{2,1,0:T(8,128)(2,1)S(1)} %get-tuple-element.12), channel_id=1, source_target_pairs={{0,16},{16,0},{1,17},{17,1},{2,18},{18,2},{3,19},{19,3},{4,20},{20... | collective-permute-start | bytes 1572872 | tf_op jit(solution)/shard_map/ppermute | solution.py:235
  17.7 69.6 %copy-start.5 = (s32[3,256]{1,0:T(4,128)S(1)}, s32[3,256]{1,0:T(4,128)}, u32[]{:S(2)}) copy-start(s32[3,256]{1,0:T(4,128)} %reach_ref.9) | copy-start | bytes 9220
  89.0 6.7 %collective-permute-start.1 = (bf16[16,128,128]{2,1,0:T(8,128)(2,1)S(1)}, bf16[16,128,128]{2,1,0:T(8,128)(2,1)S(1)}, u32[]{:S(2)}, u32[]{:S(2)}) collective-permute-start(bf16[16,128,128]{2,1,0:T(8,128)(2,1)S(1)} %memory_1_1.1), channel_id=1, source_target_pairs={{0,16},{16,0},{1,17},{17,1},{2,18},{18,2},{3,19},{19,3},{4,20},{20... | collective-permute-start | bytes 1572872 | tf_op jit(solution)/shard_map/ppermute | solution.py:235
  156.6 6.8 %collective-permute-start.2 = (bf16[16,128,128]{2,1,0:T(8,128)(2,1)S(1)}, bf16[16,128,128]{2,1,0:T(8,128)(2,1)S(1)}, u32[]{:S(2)}, u32[]{:S(2)}) collective-permute-start(bf16[16,128,128]{2,1,0:T(8,128)(2,1)S(1)} %memory_2_1.1), channel_id=1, source_target_pairs={{0,16},{16,0},{1,17},{17,1},{2,18},{18,2},{3,19},{19,3},{4,20},{20... | collective-permute-start | bytes 1572872 | tf_op jit(solution)/shard_map/ppermute | solution.py:235
  191.2 5.6 %collective-permute-start.3 = (bf16[16,128,128]{2,1,0:T(8,128)(2,1)S(1)}, bf16[16,128,128]{2,1,0:T(8,128)(2,1)S(1)}, u32[]{:S(2)}, u32[]{:S(2)}) collective-permute-start(bf16[16,128,128]{2,1,0:T(8,128)(2,1)S(1)} %all_to_all.59.own_ref), channel_id=1, source_target_pairs={{0,16},{16,0},{1,17},{17,1},{2,18},{18,2},{3,19},{19,3},{4,20},{20... | collective-permute-start | bytes 1572872 | tf_op jit(solution)/shard_map/ppermute | solution.py:242

commit v4 on v3

v4 whole, which is shorter than its diff:
```python
import functools

import jax
import jax.numpy as jnp
from jax import lax
from jax.experimental import pallas as pl
from jax.experimental.pallas import tpu as pltpu
from jax.sharding import Mesh
from jax.sharding import PartitionSpec as P

HIST = ("x", "y_high", "y_low", "c")
PLANE = ("y_low", "x", "y_high")
SECOND = ("z_high", "z_low")
ROW_T = 128
HALF = 64
TILE = 256


def low_lanes(shape):
    return lax.broadcasted_iota(jnp.int32, shape, 1) < HALF


def swap_halves(value):
    return pltpu.roll(value, HALF, 1)


def unpack_pair(even, odd):
    low = low_lanes(even.shape)
    return (
        jnp.where(low, even, swap_halves(odd)),
        jnp.where(low, swap_halves(even), odd),
    )


VMEM = pl.BlockSpec(memory_space=pltpu.VMEM)
SMEM = pl.BlockSpec(memory_space=pltpu.SMEM)
PARAMS = pltpu.CompilerParams(vmem_limit_bytes=16 * 1024 * 1024)


def column_tile(block, half, step, reach_ref, sigma, hist_ref, out_ref):
    past_loc, tiles, steps = hist_ref.shape[0] // ROW_T, TILE // ROW_T, hist_ref.shape[1] // TILE
    tile_0 = (lax.axis_index(SECOND) * 2 + half) * steps * tiles + step * tiles
    columns = []
    for tile in range(tiles):
        live = reach_ref[block, tile_0 + tile] - lax.axis_index(HIST) * past_loc
        start = step * TILE + tile * ROW_T
        columns.append(
            jnp.concatenate(
                [
                    jnp.where(
                        past < live,
                        hist_ref[past * ROW_T : (past + 1) * ROW_T, start : start + ROW_T],
                        jnp.zeros((), hist_ref.dtype),
                    )
                    for past in range(past_loc)
                ],
                0,
            )
        )
    masked = jnp.concatenate(columns, 1)
    term = jnp.dot(sigma[...], masked, preferred_element_type=jnp.float32)
    for tile in range(tiles):
        top = term[:ROW_T, tile * ROW_T : (tile + 1) * ROW_T]
        bottom = term[ROW_T:, tile * ROW_T : (tile + 1) * ROW_T]
        even, odd = unpack_pair(top, bottom)
        out_ref[(step * tiles + tile) * 2] = even.astype(out_ref.dtype)
        out_ref[(step * tiles + tile) * 2 + 1] = odd.astype(out_ref.dtype)


def away_kernel(block, reach_in, sigma_in, hist_hbm, out_ref, kept_ref, sigma_out, away_ref, reach_own, sems):
    width = hist_hbm.shape[1] // 2
    steps = width // TILE
    own = lax.axis_index("c")
    copies = []
    for half, buffer in ((1 - own, away_ref), (own, kept_ref)):
        for step in range(steps):
            there = hist_hbm.at[:, pl.ds(pl.multiple_of(half * width + step * TILE, TILE), TILE)]
            here = buffer.at[:, step * TILE : (step + 1) * TILE]
            copies.append(pltpu.make_async_copy(there, here, sems.at[len(copies)]))
    if block == 0:
        inputs = [
            pltpu.make_async_copy(reach_in, reach_own, sems.at[2 * steps]),
            pltpu.make_async_copy(sigma_in, sigma_out, sems.at[2 * steps + 1]),
        ]
        for copy in inputs:
            copy.start()
    for copy in copies:
        copy.start()
    if block == 0:
        for copy in inputs:
            copy.wait()
        reach_ref = reach_own
    else:
        reach_ref = reach_in
        for pair in range(sigma_in.shape[0] // 2):
            top, bottom = unpack_pair(sigma_in[2 * pair].astype(jnp.float32), sigma_in[2 * pair + 1].astype(jnp.float32))
            sigma_out[:ROW_T, pair * ROW_T : (pair + 1) * ROW_T] = top.astype(jnp.bfloat16)
            sigma_out[ROW_T:, pair * ROW_T : (pair + 1) * ROW_T] = bottom.astype(jnp.bfloat16)
    for step in range(steps):
        copies[step].wait()
        column_tile(block, 1 - own, step, reach_ref, sigma_out, away_ref, out_ref)
    for step in range(steps):
        copies[steps + step].wait()


def own_kernel(block, reach_ref, sigma_ref, hist_ref, out_ref):
    for step in range(hist_ref.shape[1] // TILE):
        column_tile(block, lax.axis_index("c"), step, reach_ref, sigma_ref, hist_ref, out_ref)


def product_cost(rows, cols):
    return pl.CostEstimate(flops=512 * rows * cols, bytes_accessed=4 * rows * cols, transcendentals=0)


def away_terms(block, reach, sigma, history):
    rows, cols = history.shape
    hbm = pl.BlockSpec(memory_space=pltpu.HBM)
    history = pltpu.with_memory_space_constraint(history, pltpu.HBM)
    if block == 0:
        reach, sigma = (pltpu.with_memory_space_constraint(value, pltpu.HBM) for value in (reach, sigma))
    return pl.pallas_call(
        functools.partial(away_kernel, block),
        out_shape=(
            jax.ShapeDtypeStruct((cols // 2 // HALF, ROW_T, ROW_T), jnp.bfloat16),
            jax.ShapeDtypeStruct((rows, cols // 2), history.dtype),
            jax.ShapeDtypeStruct((2 * ROW_T, rows), jnp.bfloat16),
        ),
        in_specs=[hbm, hbm, hbm] if block == 0 else [SMEM, VMEM, hbm],
        out_specs=(VMEM, VMEM, VMEM),
        scratch_shapes=[
            pltpu.VMEM((rows, cols // 2), history.dtype),
            pltpu.SMEM(reach.shape, reach.dtype),
            pltpu.SemaphoreType.DMA((2 + cols // TILE,)),
        ],
        cost_estimate=product_cost(rows, cols // 2),
        compiler_params=PARAMS,
        name=f"away_{block}",
    )(reach, sigma, history)


def own_terms(block, reach, sigma, kept):
    return pl.pallas_call(
        functools.partial(own_kernel, block),
        out_shape=jax.ShapeDtypeStruct((kept.shape[1] // HALF, ROW_T, ROW_T), jnp.bfloat16),
        in_specs=[SMEM, VMEM, VMEM],
        out_specs=VMEM,
        cost_estimate=product_cost(*kept.shape),
        compiler_params=PARAMS,
        name=f"own_{block}",
    )(reach, sigma, kept)


def step_kernel(first, last, terms_ref, green_ref, step_ref, coupling_ref, *outs):
    integral = terms_ref[0].astype(jnp.float32)
    for piece in range(1, terms_ref.shape[0]):
        integral = integral + terms_ref[piece].astype(jnp.float32)
    low = low_lanes(integral.shape)
    if first:
        place = lax.axis_index(PLANE)
        tile = pl.multiple_of((lax.axis_index("c") * 8 + place // 2) * ROW_T, ROW_T)
        held = green_ref[:, pl.ds(tile, ROW_T)].astype(jnp.float32)
        before = jnp.where(place % 2 == 0, held, swap_halves(held))
    else:
        before = swap_halves(green_ref[...])
    source = integral + jnp.where(low, before, 0.0)
    dot = functools.partial(jnp.dot, precision=lax.Precision.HIGHEST, preferred_element_type=jnp.float32)
    moved = dot(step_ref[...], source)
    further = dot(step_ref[...], jnp.where(low, 0.0, swap_halves(moved)))
    rows = moved + further
    if last:
        piece = rows.astype(jnp.bfloat16)
    else:
        weights = jnp.broadcast_to(coupling_ref[...], rows.shape).T
        square = rows * rows
        piece = (weights * rows * square / (1.0 + square)).astype(jnp.bfloat16)
        outs[1][...] = rows
    for copy in range(outs[0].shape[0]):
        outs[0][copy] = piece


def advance(first, last, terms, green, step_inv, coupling):
    shapes = [jax.ShapeDtypeStruct((16 if last else 8, ROW_T, ROW_T), jnp.bfloat16)]
    if not last:
        shapes.append(jax.ShapeDtypeStruct((ROW_T, ROW_T), jnp.float32))
    out = pl.pallas_call(
        functools.partial(step_kernel, first, last),
        out_shape=tuple(shapes),
        in_specs=[VMEM, VMEM, VMEM, VMEM],
        out_specs=(VMEM,) * len(shapes),
        compiler_params=PARAMS,
        name=f"advance_{int(first)}{int(last)}",
    )(terms, green, step_inv, coupling)
    return out[0], (None if last else out[1])


def spread_kernel(own_ref, other_ref, out_ref):
    def write(ref, half):
        for pair in range(8):
            top, bottom = unpack_pair(ref[2 * pair].astype(jnp.float32), ref[2 * pair + 1].astype(jnp.float32))
            start = pl.multiple_of((half * 8 + pair) * ROW_T, ROW_T)
            out_ref[:ROW_T, pl.ds(start, ROW_T)] = top.astype(out_ref.dtype)
            out_ref[ROW_T:, pl.ds(start, ROW_T)] = bottom.astype(out_ref.dtype)

    core = lax.axis_index("c")
    write(own_ref, core)
    write(other_ref, 1 - core)


def spread_out(own, other):
    return pl.pallas_call(
        spread_kernel,
        out_shape=jax.ShapeDtypeStruct((2 * ROW_T, 16 * ROW_T), jnp.bfloat16),
        in_specs=[VMEM, VMEM],
        out_specs=VMEM,
        compiler_params=PARAMS,
        name="spread",
    )(own, other)


def exchange(x, axis):
    return lax.all_to_all(x, axis, 0, 0, tiled=True)


def gathered_over_second(copies):
    size = lax.axis_size(SECOND)
    ring = [(place, (place + 1) % size) for place in range(size)]
    mine = exchange(copies, "z_high")
    below = lax.ppermute(mine[: size // 4], SECOND, ring)
    above = lax.ppermute(mine[size // 4 :], SECOND, [(there, here) for here, there in ring])
    even = lax.axis_index("z_low") == 0
    return jnp.where(even, jnp.concatenate([mine, below, above]), jnp.concatenate([below, above, mine]))


def local(history, self_rows, edge_rows, step_inv, coupling, reach):
    swap = [(0, 1), (1, 0)]
    weights = coupling[None, :]
    sigma, green = self_rows, edge_rows
    blocks = reach.shape[0]
    for block in range(blocks):
        last = block + 1 == blocks
        away, kept, rows = away_terms(block, reach, sigma, history)
        arrived = lax.ppermute(away, "c", swap)
        mine = own_terms(block, reach, rows, kept)
        pair = (mine.astype(jnp.float32) + arrived.astype(jnp.float32)).astype(jnp.bfloat16)
        terms = exchange(pair, PLANE)
        pieces, green = advance(block == 0, last, terms, green, step_inv, weights)
        if last:
            own = exchange(pieces, PLANE)
            return spread_out(own, lax.ppermute(own, "c", swap))
        sigma = exchange(gathered_over_second(pieces), PLANE)


def solution(mesh):
    torus = Mesh(mesh.devices.reshape(4, 2, 2, 2, 8, 2), HIST + SECOND)
    placed = (P(HIST, SECOND), P(None, HIST), P(None, SECOND), P(), P(), P())
    return jax.shard_map(local, mesh=torus, in_specs=placed, out_specs=P(None, SECOND), check_vma=False)
```

time: 199 us -> 202 us (1.015)
  blocking collectives: 154 us -> 131 us
  starting transfers between devices: 23 us -> 42.8 us
  waiting for transfers between devices: 1.52 us -> 7.35 us
  local copies, waits for them, and re-layouts: 4.13 us -> 0.06 us
  Pallas kernels: 14.8 us -> 18.8 us
    all_to_all x10 -> x8, blocking collectives: 154 us -> 131 us  [exchange(): return lax.all_to_all(x, axis, 0, 0, tiled=True)]
    ppermute x0 -> x4, starting transfers between devices: none -> 13.5 us  [the longest x2 7.54 us: gathered_over_second(): below = lax.ppermute(mine[:size // 4], SECOND, ring)]
    ppermute x0 -> x4, waiting for transfers between devices: none -> 5.7 us  [the longest x2 5.28 us: gathered_over_second(): lax.ppermute(mine[size // 4:], SECOND, [(there, here) for here, there in...]
    ppermute x3, starting transfers between devices: 19 us -> 24.7 us  [local(): arrived = lax.ppermute(away, 'c', swap)]
    pallas_call x6, Pallas kernels: 11.5 us -> 15.5 us  [the longest x3 11.2 us: away_terms(): pl.pallas_call(functools.partial(away_kernel, block), out_shape=(jax.Shap...]
    unnamed x14 -> x8, local copies, waits for them, and re-layouts: 3.94 us -> 0.02 us
  transfers between devices with their start and end apart: 4 -> 8, of which waited for: 1 -> 6; matrix products, arithmetic and copies ran while one was open for 0% -> 0% of each run, Pallas kernels for 2% -> 2%
where the time goes in v4:
time: 202 us; the launch traced here: 201 us
  blocking collectives  131 us (65%)
  starting transfers between devices  42.8 us (21%)
  Pallas kernels  18.8 us (9%)
  waiting for transfers between devices  7.35 us (4%)
    all_to_all x8, blocking collectives, exchange(): return lax.all_to_all(x, axis, 0, 0, tiled=True)  131 us
    ppermute x3, starting transfers between devices, local(): arrived = lax.ppermute(away, 'c', swap)  24.7 us
    pallas_call x3, Pallas kernels, away_terms(): pl.pallas_call(functools.partial(away_kernel, block), out_shape=(jax.Shap...  11.2 us
    ppermute x2, starting transfers between devices, gathered_over_second(): below = lax.ppermute(mine[:size // 4], SECOND, ring)  7.54 us
    ppermute x2, starting transfers between devices, gathered_over_second(): lax.ppermute(mine[size // 4:], SECOND, [(there, here) for here, there in...  5.96 us
    ppermute x2, waiting for transfers between devices, gathered_over_second(): lax.ppermute(mine[size // 4:], SECOND, [(there, here) for here, there in...  5.28 us
    ppermute x1, starting transfers between devices, local(): return spread_out(own, lax.ppermute(own, 'c', swap))  4.67 us
    pallas_call x3, Pallas kernels, own_terms(): pl.pallas_call(functools.partial(own_kernel, block), out_shape=jax.ShapeD...  4.34 us
  transfers between devices with their start and end apart: 8, of which 6 were waited for; matrix products, arithmetic and copies ran while one was open for 0% of the time, Pallas kernels for 2%

profile of v4, /device:TPU:1, one launch (start us, length us, event | category | flops | bytes accessed | tf_op | source)
XLA Modules:
  0.0 201.1 jit_solution(879748291663831377)
XLA Ops:
  0.0 3.3 %away_0.1 = (bf16[16,128,128]{2,1,0:T(8,128)(2,1)S(1)}, bf16[1024,1024]{1,0:T(8,128)(2,1)S(1)}, bf16[256,1024]{1,0:T(8,128)(2,1)S(1)}) custom-call(s32[3,256]{1,0:T(4,128)} %reach_ref.5, bf16[256,1024]{1,0:T(8,128)(2,1)} %sigma_in.1, bf16[1024,2048]{1,0:T(8,128)(2,1)} %hist_hbm.5), custom_call_target="tpu_custom_call" | custom-call | flops 536870912 | bytes 4194304 | tf_op jit(solution)/shard_map/away_0/pallas_call | solution.py:121
  3.3 8.7 %collective-permute-start = (bf16[16,128,128]{2,1,0:T(8,128)(2,1)S(1)}, bf16[16,128,128]{2,1,0:T(8,128)(2,1)S(1)}, u32[]{:S(2)}, u32[]{:S(2)}) collective-permute-start(bf16[16,128,128]{2,1,0:T(8,128)(2,1)S(1)} %get-tuple-element.20), channel_id=1, source_target_pairs={{0,16},{16,0},{1,17},{17,1},{2,18},{18,2},{3,19},{19,3},{4,20},{20... | collective-permute-start | bytes 1572872 | tf_op jit(solution)/shard_map/ppermute | solution.py:242
  12.1 1.5 own_0.1
  13.8 13.8 %all_to_all.40.terms_ref = bf16[16,128,128]{2,1,0:T(8,128)(2,1)S(1)} all-to-all(bf16[16,128,128]{2,1,0:T(8,128)(2,1)S(1)} %add_convert_fusion.2), channel_id=1, replica_groups=mesh['x'=4,'y_high'=2,'y_low'=2,'c'=2,'z_high'=8,'z_low'=2] {'y_low','x'..., dimensions={0} | all-to-all | bytes 1048576 | tf_op jit(solution)/shard_map/all_to_all | solution.py:221
  27.6 0.6 advance_10.1
  28.2 29.9 %all_to_all.41 = bf16[8,128,128]{2,1,0:T(8,128)(2,1)S(1)} all-to-all(bf16[8,128,128]{2,1,0:T(8,128)(2,1)S(1)} %get-tuple-element.21), channel_id=1, replica_groups=mesh['x'=4,'y_high'=2,'y_low'=2,'c'=2,'z_high'=8,'z_low'=2] {'z_high'}, dimensions={0} | all-to-all | bytes 524288 | tf_op jit(solution)/shard_map/all_to_all | solution.py:221
  58.2 2.5 %collective-permute-start.1 = (bf16[4,128,128]{2,1,0:T(8,128)(2,1)S(1)}, bf16[4,128,128]{2,1,0:T(8,128)(2,1)S(1)}, u32[]{:S(2)}, u32[]{:S(2)}) collective-permute-start(bf16[4,128,128]{2,1,0:T(8,128)(2,1)S(1)} %get-tuple-element.33), channel_id=1, source_target_pairs={{0,1},{1,2},{2,3},{3,4},{4,5},{5,6},{6,7},{7,8},{8,9},{9,10},{10,1... | collective-permute-start | bytes 393224 | tf_op jit(solution)/shard_map/ppermute | solution.py:228
  60.6 4.0 %collective-permute-start.2 = (bf16[4,128,128]{2,1,0:T(8,128)(2,1)S(1)}, bf16[4,128,128]{2,1,0:T(8,128)(2,1)S(1)}, u32[]{:S(2)}, u32[]{:S(2)}) collective-permute-start(bf16[4,128,128]{2,1,0:T(8,128)(2,1)S(1)} %get-tuple-element.34), channel_id=1, source_target_pairs={{1,0},{2,1},{3,2},{4,3},{5,4},{6,5},{7,6},{8,7},{9,8},{10,9},{11,1... | collective-permute-start | bytes 393224 | tf_op jit(solution)/shard_map/ppermute | solution.py:229
  64.7 0.4 collective-permute-done.1
  65.1 1.5 collective-permute-done.2
  66.7 14.3 %all_to_all.42.sigma_in = bf16[16,128,128]{2,1,0:T(8,128)(2,1)S(1)} all-to-all(bf16[16,128,128]{2,1,0:T(8,128)(2,1)S(1)} %maximum_select_fusion), channel_id=1, replica_groups=mesh['x'=4,'y_high'=2,'y_low'=2,'c'=2,'z_high'=8,'z_low'=2] {'y_low','x'..., dimensions={0} | all-to-all | bytes 1048576 | tf_op jit(solution)/shard_map/all_to_all | solution.py:221
  81.0 3.9 %away_1.1 = (bf16[16,128,128]{2,1,0:T(8,128)(2,1)S(1)}, bf16[1024,1024]{1,0:T(8,128)(2,1)S(1)}, bf16[256,1024]{1,0:T(8,128)(2,1)S(1)}) custom-call(s32[3,256]{1,0:T(4,128)S(1)} %copy-done.2, bf16[16,128,128]{2,1,0:T(8,128)(2,1)S(1)} %all_to_all.42.sigma_in, bf16[1024,2048]{1,0:T(8,128)(2,1)} %hist_hbm.5), custom_call_target="tpu_custom_call" | custom-call | flops 536870912 | bytes 4194304 | tf_op jit(solution)/shard_map/away_1/pallas_call | solution.py:121
  85.0 7.7 %collective-permute-start.3 = (bf16[16,128,128]{2,1,0:T(8,128)(2,1)S(1)}, bf16[16,128,128]{2,1,0:T(8,128)(2,1)S(1)}, u32[]{:S(2)}, u32[]{:S(2)}) collective-permute-start(bf16[16,128,128]{2,1,0:T(8,128)(2,1)S(1)} %get-tuple-element.24), channel_id=1, source_target_pairs={{0,16},{16,0},{1,17},{17,1},{2,18},{18,2},{3,19},{19,3},{4,20},{20... | collective-permute-start | bytes 1572872 | tf_op jit(solution)/shard_map/ppermute | solution.py:242
  92.7 1.4 own_1.1
  94.2 0.1 add_convert_fusion.1
  94.4 13.3 %all_to_all.43.terms_ref = bf16[16,128,128]{2,1,0:T(8,128)(2,1)S(1)} all-to-all(bf16[16,128,128]{2,1,0:T(8,128)(2,1)S(1)} %add_convert_fusion.1), channel_id=1, replica_groups=mesh['x'=4,'y_high'=2,'y_low'=2,'c'=2,'z_high'=8,'z_low'=2] {'y_low','x'..., dimensions={0} | all-to-all | bytes 1048576 | tf_op jit(solution)/shard_map/all_to_all | solution.py:221
  107.7 0.6 advance_00.1
  108.3 19.7 %all_to_all.44 = bf16[8,128,128]{2,1,0:T(8,128)(2,1)S(1)} all-to-all(bf16[8,128,128]{2,1,0:T(8,128)(2,1)S(1)} %get-tuple-element.26), channel_id=1, replica_groups=mesh['x'=4,'y_high'=2,'y_low'=2,'c'=2,'z_high'=8,'z_low'=2] {'z_high'}, dimensions={0} | all-to-all | bytes 524288 | tf_op jit(solution)/shard_map/all_to_all | solution.py:221
  128.0 5.1 %collective-permute-start.4 = (bf16[4,128,128]{2,1,0:T(8,128)(2,1)S(1)}, bf16[4,128,128]{2,1,0:T(8,128)(2,1)S(1)}, u32[]{:S(2)}, u32[]{:S(2)}) collective-permute-start(bf16[4,128,128]{2,1,0:T(8,128)(2,1)S(1)} %get-tuple-element.31), channel_id=1, source_target_pairs={{0,1},{1,2},{2,3},{3,4},{4,5},{5,6},{6,7},{7,8},{8,9},{9,10},{10,1... | collective-permute-start | bytes 393224 | tf_op jit(solution)/shard_map/ppermute | solution.py:228
  133.1 1.9 collective-permute-start.5
  135.1 3.8 %collective-permute-done.5 = bf16[4,128,128]{2,1,0:T(8,128)(2,1)S(1)} collective-permute-done((bf16[4,128,128]{2,1,0:T(8,128)(2,1)S(1)}, bf16[4,128,128]{2,1,0:T(8,128)(2,1)S(1)}, u32[]{:S(2)}, u32[]{:S(2)}) %collective-permute-start.5) | collective-permute-done | bytes 131104 | tf_op jit(solution)/shard_map/ppermute | solution.py:229
  139.0 13.2 %all_to_all.45.sigma_in = bf16[16,128,128]{2,1,0:T(8,128)(2,1)S(1)} all-to-all(bf16[16,128,128]{2,1,0:T(8,128)(2,1)S(1)} %maximum_select_fusion.1), channel_id=1, replica_groups=mesh['x'=4,'y_high'=2,'y_low'=2,'c'=2,'z_high'=8,'z_low'=2] {'y_low','x'..., dimensions={0} | all-to-all | bytes 1048576 | tf_op jit(solution)/shard_map/all_to_all | solution.py:221
  152.2 3.9 %away_2.1 = (bf16[16,128,128]{2,1,0:T(8,128)(2,1)S(1)}, bf16[1024,1024]{1,0:T(8,128)(2,1)S(1)}, bf16[256,1024]{1,0:T(8,128)(2,1)S(1)}) custom-call(s32[3,256]{1,0:T(4,128)S(1)} %copy-done.2, bf16[16,128,128]{2,1,0:T(8,128)(2,1)S(1)} %all_to_all.45.sigma_in, bf16[1024,2048]{1,0:T(8,128)(2,1)} %hist_hbm.5), custom_call_target="tpu_custom_call" | custom-call | flops 536870912 | bytes 4194304 | tf_op jit(solution)/shard_map/away_2/pallas_call | solution.py:121
  156.1 8.2 %collective-permute-start.6 = (bf16[16,128,128]{2,1,0:T(8,128)(2,1)S(1)}, bf16[16,128,128]{2,1,0:T(8,128)(2,1)S(1)}, u32[]{:S(2)}, u32[]{:S(2)}) collective-permute-start(bf16[16,128,128]{2,1,0:T(8,128)(2,1)S(1)} %get-tuple-element.29), channel_id=1, source_target_pairs={{0,16},{16,0},{1,17},{17,1},{2,18},{18,2},{3,19},{19,3},{4,20},{20... | collective-permute-start | bytes 1572872 | tf_op jit(solution)/shard_map/ppermute | solution.py:242
  164.3 1.4 own_2.1
  165.8 0.1 add_convert_fusion
  166.0 13.3 %all_to_all.46.terms_ref = bf16[16,128,128]{2,1,0:T(8,128)(2,1)S(1)} all-to-all(bf16[16,128,128]{2,1,0:T(8,128)(2,1)S(1)} %add_convert_fusion), channel_id=1, replica_groups=mesh['x'=4,'y_high'=2,'y_low'=2,'c'=2,'z_high'=8,'z_low'=2] {'y_low','x'..., dimensions={0} | all-to-all | bytes 1048576 | tf_op jit(solution)/shard_map/all_to_all | solution.py:221
  179.3 0.6 advance_01.1
  180.0 13.6 %all_to_all.47.own_ref = bf16[16,128,128]{2,1,0:T(8,128)(2,1)S(1)} all-to-all(bf16[16,128,128]{2,1,0:T(8,128)(2,1)S(1)} %advance_01.1), channel_id=1, replica_groups=mesh['x'=4,'y_high'=2,'y_low'=2,'c'=2,'z_high'=8,'z_low'=2] {'y_low','x'..., dimensions={0} | all-to-all | bytes 1048576 | tf_op jit(solution)/shard_map/all_to_all | solution.py:221
  193.5 4.7 %collective-permute-start.7 = (bf16[16,128,128]{2,1,0:T(8,128)(2,1)S(1)}, bf16[16,128,128]{2,1,0:T(8,128)(2,1)S(1)}, u32[]{:S(2)}, u32[]{:S(2)}) collective-permute-start(bf16[16,128,128]{2,1,0:T(8,128)(2,1)S(1)} %all_to_all.47.own_ref), channel_id=1, source_target_pairs={{0,16},{16,0},{1,17},{17,1},{2,18},{18,2},{3,19},{19,3},{4,20},{20... | collective-permute-start | bytes 1572872 | tf_op jit(solution)/shard_map/ppermute | solution.py:249
  198.2 1.5 collective-permute-done.7.other_ref
  199.7 1.4 spread.1
  (17 shorter events, 0.6 us)
Async XLA Ops:
  0.0 12.1 %copy-start.2 = (s32[3,256]{1,0:T(4,128)S(1)}, s32[3,256]{1,0:T(4,128)}, u32[]{:S(2)}) copy-start(s32[3,256]{1,0:T(4,128)} %reach_ref.5) | copy-start | bytes 9220
  3.3 10.3 %collective-permute-start = (bf16[16,128,128]{2,1,0:T(8,128)(2,1)S(1)}, bf16[16,128,128]{2,1,0:T(8,128)(2,1)S(1)}, u32[]{:S(2)}, u32[]{:S(2)}) collective-permute-start(bf16[16,128,128]{2,1,0:T(8,128)(2,1)S(1)} %get-tuple-element.20), channel_id=1, source_target_pairs={{0,16},{16,0},{1,17},{17,1},{2,18},{18,2},{3,19},{19,3},{4,20},{20... | collective-permute-start | bytes 1572872 | tf_op jit(solution)/shard_map/ppermute | solution.py:242
  13.6 14.0 %copy-start = (f32[128,128]{1,0:T(8,128)S(1)}, f32[128,128]{1,0:T(8,128)}, u32[]{:S(2)}) copy-start(f32[128,128]{1,0:T(8,128)} %step_ref.5) | copy-start | bytes 196612
  13.6 14.0 %copy-start.1 = (bf16[128,2048]{1,0:T(8,128)(2,1)S(1)}, bf16[128,2048]{1,0:T(8,128)(2,1)}, u32[]{:S(2)}) copy-start(bf16[128,2048]{1,0:T(8,128)(2,1)} %green_ref.1) | copy-start | bytes 1572868
  13.6 14.0 %copy-start.3 = (f32[128]{0:T(128)S(1)}, f32[128]{0:T(128)}, u32[]{:S(2)}) copy-start(f32[128]{0:T(128)} %param.10) | copy-start | bytes 1540
  58.2 6.9 %collective-permute-start.1 = (bf16[4,128,128]{2,1,0:T(8,128)(2,1)S(1)}, bf16[4,128,128]{2,1,0:T(8,128)(2,1)S(1)}, u32[]{:S(2)}, u32[]{:S(2)}) collective-permute-start(bf16[4,128,128]{2,1,0:T(8,128)(2,1)S(1)} %get-tuple-element.33), channel_id=1, source_target_pairs={{0,1},{1,2},{2,3},{3,4},{4,5},{5,6},{6,7},{7,8},{8,9},{9,10},{10,1... | collective-permute-start | bytes 393224 | tf_op jit(solution)/shard_map/ppermute | solution.py:228
  60.6 6.0 %collective-permute-start.2 = (bf16[4,128,128]{2,1,0:T(8,128)(2,1)S(1)}, bf16[4,128,128]{2,1,0:T(8,128)(2,1)S(1)}, u32[]{:S(2)}, u32[]{:S(2)}) collective-permute-start(bf16[4,128,128]{2,1,0:T(8,128)(2,1)S(1)} %get-tuple-element.34), channel_id=1, source_target_pairs={{1,0},{2,1},{3,2},{4,3},{5,4},{6,5},{7,6},{8,7},{9,8},{10,9},{11,1... | collective-permute-start | bytes 393224 | tf_op jit(solution)/shard_map/ppermute | solution.py:229
  85.0 9.3 %collective-permute-start.3 = (bf16[16,128,128]{2,1,0:T(8,128)(2,1)S(1)}, bf16[16,128,128]{2,1,0:T(8,128)(2,1)S(1)}, u32[]{:S(2)}, u32[]{:S(2)}) collective-permute-start(bf16[16,128,128]{2,1,0:T(8,128)(2,1)S(1)} %get-tuple-element.24), channel_id=1, source_target_pairs={{0,16},{16,0},{1,17},{17,1},{2,18},{18,2},{3,19},{19,3},{4,20},{20... | collective-permute-start | bytes 1572872 | tf_op jit(solution)/shard_map/ppermute | solution.py:242
  128.0 7.0 %collective-permute-start.4 = (bf16[4,128,128]{2,1,0:T(8,128)(2,1)S(1)}, bf16[4,128,128]{2,1,0:T(8,128)(2,1)S(1)}, u32[]{:S(2)}, u32[]{:S(2)}) collective-permute-start(bf16[4,128,128]{2,1,0:T(8,128)(2,1)S(1)} %get-tuple-element.31), channel_id=1, source_target_pairs={{0,1},{1,2},{2,3},{3,4},{4,5},{5,6},{6,7},{7,8},{8,9},{9,10},{10,1... | collective-permute-start | bytes 393224 | tf_op jit(solution)/shard_map/ppermute | solution.py:228
  133.1 5.7 %collective-permute-start.5 = (bf16[4,128,128]{2,1,0:T(8,128)(2,1)S(1)}, bf16[4,128,128]{2,1,0:T(8,128)(2,1)S(1)}, u32[]{:S(2)}, u32[]{:S(2)}) collective-permute-start(bf16[4,128,128]{2,1,0:T(8,128)(2,1)S(1)} %get-tuple-element.32), channel_id=1, source_target_pairs={{1,0},{2,1},{3,2},{4,3},{5,4},{6,5},{7,6},{8,7},{9,8},{10,9},{11,1... | collective-permute-start | bytes 393224 | tf_op jit(solution)/shard_map/ppermute | solution.py:229
  156.1 9.7 %collective-permute-start.6 = (bf16[16,128,128]{2,1,0:T(8,128)(2,1)S(1)}, bf16[16,128,128]{2,1,0:T(8,128)(2,1)S(1)}, u32[]{:S(2)}, u32[]{:S(2)}) collective-permute-start(bf16[16,128,128]{2,1,0:T(8,128)(2,1)S(1)} %get-tuple-element.29), channel_id=1, source_target_pairs={{0,16},{16,0},{1,17},{17,1},{2,18},{18,2},{3,19},{19,3},{4,20},{20... | collective-permute-start | bytes 1572872 | tf_op jit(solution)/shard_map/ppermute | solution.py:242
  193.5 6.2 %collective-permute-start.7 = (bf16[16,128,128]{2,1,0:T(8,128)(2,1)S(1)}, bf16[16,128,128]{2,1,0:T(8,128)(2,1)S(1)}, u32[]{:S(2)}, u32[]{:S(2)}) collective-permute-start(bf16[16,128,128]{2,1,0:T(8,128)(2,1)S(1)} %all_to_all.47.own_ref), channel_id=1, source_target_pairs={{0,16},{16,0},{1,17},{17,1},{2,18},{18,2},{3,19},{19,3},{4,20},{20... | collective-permute-start | bytes 1572872 | tf_op jit(solution)/shard_map/ppermute | solution.py:249

commit v5 on v3

v5 whole, which is shorter than its diff:
```python
import functools

import jax
import jax.numpy as jnp
from jax import lax
from jax.experimental import pallas as pl
from jax.experimental.pallas import tpu as pltpu
from jax.sharding import Mesh
from jax.sharding import PartitionSpec as P

HIST = ("x", "y", "c")
SECOND = ("z_high", "z_low")
MIX = ("z_low", "x", "y")
ROW_T = 128
HALF = 64
QUARTER = 32
TILE = 256

VMEM = pl.BlockSpec(memory_space=pltpu.VMEM)
SMEM = pl.BlockSpec(memory_space=pltpu.SMEM)
PARAMS = pltpu.CompilerParams(vmem_limit_bytes=16 * 1024 * 1024)


def lower_lanes(shape, width):
    return (lax.broadcasted_iota(jnp.int32, shape, 1) // width) % 2 == 0


def swapped(first, second, width):
    low = lower_lanes(first.shape, width)
    return (
        jnp.where(low, first, pltpu.roll(second, width, 1)),
        jnp.where(low, pltpu.roll(first, ROW_T - width, 1), second),
    )


def lane_blocks_transposed(tiles):
    a0, a2 = swapped(tiles[0], tiles[2], HALF)
    a1, a3 = swapped(tiles[1], tiles[3], HALF)
    return (*swapped(a0, a1, QUARTER), *swapped(a2, a3, QUARTER))


PLACES = (0, ROW_T, HALF, ROW_T + HALF)


def tile_from_pieces(ref, group):
    return lane_blocks_transposed([ref[4 * group + piece].astype(jnp.float32) for piece in range(4)])


def column_tile(block, half, step, reach_ref, sigma, hist_ref, out_ref, edge_ref=None):
    past_loc, tiles = hist_ref.shape[0] // ROW_T, TILE // ROW_T
    steps = hist_ref.shape[1] // 2 // TILE
    start = pl.multiple_of((half * steps + step) * TILE, TILE)
    tile_0 = (lax.axis_index(SECOND) * 2 * steps + half * steps + step) * tiles
    columns = []
    for tile in range(tiles):
        live = reach_ref[block, tile_0 + tile] - lax.axis_index(HIST) * past_loc
        columns.append(
            jnp.concatenate(
                [
                    jnp.where(
                        past < live,
                        hist_ref[past * ROW_T : (past + 1) * ROW_T, pl.ds(start + tile * ROW_T, ROW_T)],
                        jnp.zeros((), hist_ref.dtype),
                    )
                    for past in range(past_loc)
                ],
                0,
            )
        )
    masked = jnp.concatenate(columns, 1)
    term = jnp.dot(sigma[...], masked, preferred_element_type=jnp.float32)
    for tile in range(tiles):
        parts = [term[at : at + HALF, tile * ROW_T : (tile + 1) * ROW_T] for at in PLACES]
        if edge_ref is not None:
            adds = lax.axis_index(("x", "y")) == 0
            for part in (0, 2):
                edge = edge_ref[PLACES[part] : PLACES[part] + HALF, pl.ds(start + tile * ROW_T, ROW_T)]
                parts[part] = parts[part] + jnp.where(adds, edge.astype(jnp.float32), 0.0)
        for piece, value in enumerate(lane_blocks_transposed(parts)):
            out_ref[(step * tiles + tile) * 4 + piece] = value.astype(out_ref.dtype)


def memory_kernel(block, first_half, from_pieces, with_edge, reach_ref, sigma_ref, hist_ref, *rest):
    own = lax.axis_index("c")
    half = 1 - own if first_half else own
    edge_ref = rest[0] if with_edge else None
    out_ref = rest[1] if with_edge else rest[0]
    sigma = sigma_ref
    if from_pieces:
        sigma = rest[-1]
        for group in range(sigma_ref.shape[0] // 4):
            for at, value in zip(PLACES, tile_from_pieces(sigma_ref, group)):
                sigma[at : at + HALF, group * ROW_T : (group + 1) * ROW_T] = value.astype(sigma.dtype)
    for step in range(hist_ref.shape[1] // 2 // TILE):
        column_tile(block, half, step, reach_ref, sigma, hist_ref, out_ref, edge_ref)


def product_cost(rows, cols):
    return pl.CostEstimate(flops=512 * rows * cols, bytes_accessed=4 * rows * cols, transcendentals=0)


def pieces_shape(cols):
    return jax.ShapeDtypeStruct((cols // QUARTER, HALF, ROW_T), jnp.bfloat16)


def memory_terms(block, first_half, reach, sigma, history, edge=None):
    rows, cols = history.shape
    from_pieces = sigma.ndim == 3
    extra = () if edge is None else (edge,)
    return pl.pallas_call(
        functools.partial(memory_kernel, block, first_half, from_pieces, edge is not None),
        out_shape=pieces_shape(cols // 2),
        in_specs=[SMEM, VMEM, VMEM] + [VMEM] * len(extra),
        out_specs=VMEM,
        scratch_shapes=[pltpu.VMEM((2 * ROW_T, rows), jnp.bfloat16)] if from_pieces else [],
        cost_estimate=product_cost(rows, cols // 2),
        compiler_params=PARAMS,
        name=f"memory_{block}_{int(first_half)}",
    )(reach, sigma, history, *extra)


def first_kernel(reach_hbm, sigma_hbm, hist_hbm, out_ref, hist_ref, sigma_ref, reach_ref, sems):
    steps = hist_hbm.shape[1] // 2 // TILE
    own = lax.axis_index("c")
    copies = [
        pltpu.make_async_copy(reach_hbm, reach_ref, sems.at[0]),
        pltpu.make_async_copy(sigma_hbm, sigma_ref, sems.at[1]),
    ]
    for half in (1 - own, own):
        for step in range(steps):
            part = pl.ds(pl.multiple_of((half * steps + step) * TILE, TILE), TILE)
            copies.append(
                pltpu.make_async_copy(hist_hbm.at[:, part], hist_ref.at[:, part], sems.at[len(copies)])
            )
    for copy in copies:
        copy.start()
    copies[0].wait()
    copies[1].wait()
    for step in range(steps):
        copies[2 + step].wait()
        column_tile(0, 1 - own, step, reach_ref, sigma_ref, hist_ref, out_ref)
    for step in range(steps):
        copies[2 + steps + step].wait()


def first_terms(reach, sigma, history):
    rows, cols = history.shape
    there = pl.BlockSpec(memory_space=pltpu.HBM)
    return pl.pallas_call(
        first_kernel,
        out_shape=(
            pieces_shape(cols // 2),
            jax.ShapeDtypeStruct(history.shape, history.dtype),
            jax.ShapeDtypeStruct(sigma.shape, sigma.dtype),
        ),
        in_specs=[there, there, there],
        out_specs=(VMEM, VMEM, VMEM),
        scratch_shapes=[
            pltpu.SMEM(reach.shape, reach.dtype),
            pltpu.SemaphoreType.DMA((2 + cols // TILE,)),
        ],
        cost_estimate=product_cost(rows, cols // 2),
        compiler_params=PARAMS,
        name="memory_first",
    )(*(pltpu.with_memory_space_constraint(value, pltpu.HBM) for value in (reach, sigma, history)))


def step_kernel(first, last, terms_ref, step_ref, coupling_ref, *refs):
    count = terms_ref.shape[0] // 2
    sums = []
    for plane in range(2):
        total = terms_ref[plane * count].astype(jnp.float32)
        for place in range(1, count):
            total = total + terms_ref[plane * count + place].astype(jnp.float32)
        sums.append(total)
    source = jnp.concatenate(swapped(*sums, HALF), 0)
    step_0 = lower_lanes(source.shape, QUARTER)
    outs = refs
    if not first:
        source = source + jnp.where(step_0, pltpu.roll(refs[0][...], ROW_T - QUARTER, 1), 0.0)
        outs = refs[1:]
    dot = functools.partial(jnp.dot, precision=lax.Precision.HIGHEST, preferred_element_type=jnp.float32)
    moved = dot(step_ref[...], source)
    rows = moved + dot(step_ref[...], jnp.where(step_0, 0.0, pltpu.roll(moved, QUARTER, 1)))
    result = rows
    if not last:
        weights = jnp.broadcast_to(coupling_ref[...], rows.shape).T
        square = rows * rows
        result = weights * rows * square / (1.0 + square)
        outs[1][...] = rows
    planes = [value.astype(jnp.bfloat16) for value in swapped(result[:HALF], result[HALF:], HALF)]
    for plane in range(2):
        for copy in range(outs[0].shape[1 if last else 0]):
            if last:
                outs[0][plane, copy] = planes[plane]
            else:
                outs[0][copy, plane] = planes[plane]


def advance(first, last, terms, green, step_inv, coupling):
    copies = (2, 16) if last else (8, 2)
    shapes = [jax.ShapeDtypeStruct((*copies, HALF, ROW_T), jnp.bfloat16)]
    if not last:
        shapes.append(jax.ShapeDtypeStruct((ROW_T, ROW_T), jnp.float32))
    args = (terms, step_inv, coupling) + (() if first else (green,))
    out = pl.pallas_call(
        functools.partial(step_kernel, first, last),
        out_shape=tuple(shapes),
        in_specs=[VMEM] * len(args),
        out_specs=(VMEM,) * len(shapes),
        compiler_params=PARAMS,
        name=f"advance_{int(first)}{int(last)}",
    )(*args)
    return out[0], (None if last else out[1])


def spread_kernel(own_ref, other_ref, out_ref):
    core = lax.axis_index("c")
    for ref, half in ((own_ref, core), (other_ref, 1 - core)):
        groups = ref.shape[0] // 4
        for group in range(groups):
            part = pl.ds(pl.multiple_of((half * groups + group) * ROW_T, ROW_T), ROW_T)
            for at, value in zip(PLACES, tile_from_pieces(ref, group)):
                out_ref[at : at + HALF, part] = value.astype(out_ref.dtype)


def spread_out(own, other):
    return pl.pallas_call(
        spread_kernel,
        out_shape=jax.ShapeDtypeStruct((2 * ROW_T, 2 * own.shape[0] * QUARTER), jnp.bfloat16),
        in_specs=[VMEM, VMEM],
        out_specs=VMEM,
        compiler_params=PARAMS,
        name="spread",
    )(own, other)


def exchange(x, axis):
    return lax.all_to_all(x, axis, 0, 0, tiled=True)


def local(history, self_rows, edge_rows, step_inv, coupling, reach):
    swap = [(0, 1), (1, 0)]
    weights = coupling[None, :]
    green, blocks = None, reach.shape[0]
    for block in range(blocks):
        last = block + 1 == blocks
        if block == 0:
            away, held, rows = first_terms(reach, self_rows, history)
        else:
            away = memory_terms(block, True, reach, rows, held)
        arrived = lax.ppermute(away, "c", swap)
        mine = memory_terms(block, False, reach, rows, held, edge_rows if block == 0 else None)
        pair = (mine.astype(jnp.float32) + arrived.astype(jnp.float32)).astype(jnp.bfloat16)
        terms = exchange(pair, MIX)
        pieces, green = advance(block == 0, last, terms, green, step_inv, weights)
        if last:
            own = exchange(pieces.reshape(-1, HALF, ROW_T), MIX)
            return spread_out(own, lax.ppermute(own, "c", swap))
        places = exchange(pieces, "z_high").reshape(16, HALF, ROW_T)
        rows = exchange(jnp.concatenate([places, places]), MIX)


def solution(mesh):
    torus = Mesh(mesh.devices.reshape(4, 4, 2, 8, 2), HIST + SECOND)
    placed = (P(HIST, SECOND), P(None, HIST), P(None, SECOND), P(), P(), P())
    return jax.shard_map(local, mesh=torus, in_specs=placed, out_specs=P(None, SECOND), check_vma=False)
```

time: 199 us -> 186 us (0.935)
  blocking collectives: 154 us -> 138 us
  Pallas kernels: 14.8 us -> 19 us
  local copies, waits for them, and re-layouts: 4.13 us -> 0.02 us
  starting transfers between devices: 23 us -> 26 us
    all_to_all x10 -> x8, blocking collectives: 154 us -> 138 us  [exchange(): return lax.all_to_all(x, axis, 0, 0, tiled=True)]
    unnamed x14 -> x8, local copies, waits for them, and re-layouts: 3.94 us -> 0.02 us
    pallas_call x5, Pallas kernels: 8.29 us -> 10.6 us  [memory_terms(): pl.pallas_call(functools.partial(memory_kernel, block, first_half, from_p...]
    ppermute x3, starting transfers between devices: 19 us -> 21 us  [local(): arrived = lax.ppermute(away, 'c', swap)]
  transfers between devices with their start and end apart: 4 -> 4, of which waited for: 1 -> 1; matrix products, arithmetic and copies ran while one was open for 0% -> 0% of each run, Pallas kernels for 2% -> 3%
where the time goes in v5:
time: 186 us
  blocking collectives  138 us (74%)
  starting transfers between devices  26 us (14%)
  Pallas kernels  19 us (10%)
    all_to_all x8, blocking collectives, exchange(): return lax.all_to_all(x, axis, 0, 0, tiled=True)  138 us
    ppermute x3, starting transfers between devices, local(): arrived = lax.ppermute(away, 'c', swap)  21 us
    pallas_call x5, Pallas kernels, memory_terms(): pl.pallas_call(functools.partial(memory_kernel, block, first_half, from_p...  10.6 us
    ppermute x1, starting transfers between devices, local(): return spread_out(own, lax.ppermute(own, 'c', swap))  5.03 us
  transfers between devices with their start and end apart: 4, of which 1 were waited for; matrix products, arithmetic and copies ran while one was open for 0% of the time, Pallas kernels for 3%

profile of v5, /device:TPU:1, one launch (start us, length us, event | category | flops | bytes accessed | tf_op | source)
XLA Modules:
  0.0 185.5 jit_solution(5192950730044502237)
XLA Ops:
  0.0 3.7 %memory_first.1 = (bf16[32,64,128]{2,1,0:T(8,128)(2,1)S(1)}, bf16[1024,2048]{1,0:T(8,128)(2,1)S(1)}, bf16[256,1024]{1,0:T(8,128)(2,1)S(1)}) custom-call(s32[3,256]{1,0:T(4,128)} %reach_ref.9, bf16[256,1024]{1,0:T(8,128)(2,1)} %sigma_hbm.1, bf16[1024,2048]{1,0:T(8,128)(2,1)} %hist_hbm.1), custom_call_target="tpu_custom_call" | custom-call | flops 536870912 | bytes 4194304 | tf_op jit(solution)/shard_map/memory_first/pallas_call | solution.py:149
  3.7 8.7 %collective-permute-start = (bf16[32,64,128]{2,1,0:T(8,128)(2,1)S(1)}, bf16[32,64,128]{2,1,0:T(8,128)(2,1)S(1)}, u32[]{:S(2)}, u32[]{:S(2)}) collective-permute-start(bf16[32,64,128]{2,1,0:T(8,128)(2,1)S(1)} %get-tuple-element.14), channel_id=1, source_target_pairs={{0,16},{16,0},{1,17},{17,1},{2,18},{18,2},{3,19},{19,3},{4,20},{20... | collective-permute-start | bytes 1572872 | tf_op jit(solution)/shard_map/ppermute | solution.py:252
  12.5 0.0 copy-done.2
  12.5 0.0 copy-start
  12.5 0.0 copy-start.3
  12.5 1.7 memory_0_0.1
  14.2 0.0 collective-permute-done
  14.2 0.2 add_convert_fusion.2
  14.4 13.4 %all_to_all.40.terms_ref = bf16[32,64,128]{2,1,0:T(8,128)(2,1)S(1)} all-to-all(bf16[32,64,128]{2,1,0:T(8,128)(2,1)S(1)} %add_convert_fusion.2), channel_id=1, replica_groups=mesh['x'=4,'y'=4,'c'=2,'z_high'=8,'z_low'=2] {'z_low','x','y'}, dimensions={0} | all-to-all | bytes 1048576 | tf_op jit(solution)/shard_map/all_to_all | solution.py:239
  27.9 0.7 advance_10.1
  28.6 30.9 %all_to_all.41 = bf16[8,2,64,128]{3,2,1,0:T(8,128)(2,1)S(1)} all-to-all(bf16[8,2,64,128]{3,2,1,0:T(8,128)(2,1)S(1)} %get-tuple-element.15), channel_id=1, replica_groups=mesh['x'=4,'y'=4,'c'=2,'z_high'=8,'z_low'=2] {'z_high'}, dimensions={0} | all-to-all | bytes 524288 | tf_op jit(solution)/shard_map/all_to_all | solution.py:239
  59.6 15.1 %all_to_all.42.sigma_ref = bf16[32,64,128]{2,1,0:T(8,128)(2,1)S(1)} all-to-all(bf16[32,64,128]{2,1,0:T(8,128)(2,1)S(1)} %pad_maximum_fusion), channel_id=1, replica_groups=mesh['x'=4,'y'=4,'c'=2,'z_high'=8,'z_low'=2] {'z_low','x','y'}, dimensions={0} | all-to-all | bytes 1048576 | tf_op jit(solution)/shard_map/all_to_all | solution.py:239
  74.7 2.2 %memory_1_1.1 = bf16[32,64,128]{2,1,0:T(8,128)(2,1)S(1)} custom-call(s32[3,256]{1,0:T(4,128)S(1)} %copy-done.2, bf16[32,64,128]{2,1,0:T(8,128)(2,1)S(1)} %all_to_all.42.sigma_ref, bf16[1024,2048]{1,0:T(8,128)(2,1)S(1)} %get-tuple-element.13.hist_ref), custom_call_target="tpu_custom_call" | custom-call | flops 536870912 | bytes 4194304 | tf_op jit(solution)/shard_map/memory_1_1/pallas_call | solution.py:110
  76.9 5.9 %collective-permute-start.1 = (bf16[32,64,128]{2,1,0:T(8,128)(2,1)S(1)}, bf16[32,64,128]{2,1,0:T(8,128)(2,1)S(1)}, u32[]{:S(2)}, u32[]{:S(2)}) collective-permute-start(bf16[32,64,128]{2,1,0:T(8,128)(2,1)S(1)} %memory_1_1.1), channel_id=1, source_target_pairs={{0,16},{16,0},{1,17},{17,1},{2,18},{18,2},{3,19},{19,3},{4,20},{20... | collective-permute-start | bytes 1572872 | tf_op jit(solution)/shard_map/ppermute | solution.py:252
  82.8 2.2 %memory_1_0.1 = bf16[32,64,128]{2,1,0:T(8,128)(2,1)S(1)} custom-call(s32[3,256]{1,0:T(4,128)S(1)} %copy-done.2, bf16[32,64,128]{2,1,0:T(8,128)(2,1)S(1)} %all_to_all.42.sigma_ref, bf16[1024,2048]{1,0:T(8,128)(2,1)S(1)} %get-tuple-element.13.hist_ref), custom_call_target="tpu_custom_call" | custom-call | flops 536870912 | bytes 4194304 | tf_op jit(solution)/shard_map/memory_1_0/pallas_call | solution.py:110
  85.1 0.0 collective-permute-done.1
  85.1 0.2 add_convert_fusion.1
  85.3 14.1 %all_to_all.43.terms_ref = bf16[32,64,128]{2,1,0:T(8,128)(2,1)S(1)} all-to-all(bf16[32,64,128]{2,1,0:T(8,128)(2,1)S(1)} %add_convert_fusion.1), channel_id=1, replica_groups=mesh['x'=4,'y'=4,'c'=2,'z_high'=8,'z_low'=2] {'z_low','x','y'}, dimensions={0} | all-to-all | bytes 1048576 | tf_op jit(solution)/shard_map/all_to_all | solution.py:239
  99.4 0.7 advance_00.1
  100.1 21.7 %all_to_all.44 = bf16[8,2,64,128]{3,2,1,0:T(8,128)(2,1)S(1)} all-to-all(bf16[8,2,64,128]{3,2,1,0:T(8,128)(2,1)S(1)} %get-tuple-element.17), channel_id=1, replica_groups=mesh['x'=4,'y'=4,'c'=2,'z_high'=8,'z_low'=2] {'z_high'}, dimensions={0} | all-to-all | bytes 524288 | tf_op jit(solution)/shard_map/all_to_all | solution.py:239
  121.8 14.9 %all_to_all.45.sigma_ref = bf16[32,64,128]{2,1,0:T(8,128)(2,1)S(1)} all-to-all(bf16[32,64,128]{2,1,0:T(8,128)(2,1)S(1)} %pad_maximum_fusion.1), channel_id=1, replica_groups=mesh['x'=4,'y'=4,'c'=2,'z_high'=8,'z_low'=2] {'z_low','x','y'}, dimensions={0} | all-to-all | bytes 1048576 | tf_op jit(solution)/shard_map/all_to_all | solution.py:239
  136.7 2.2 %memory_2_1.1 = bf16[32,64,128]{2,1,0:T(8,128)(2,1)S(1)} custom-call(s32[3,256]{1,0:T(4,128)S(1)} %copy-done.2, bf16[32,64,128]{2,1,0:T(8,128)(2,1)S(1)} %all_to_all.45.sigma_ref, bf16[1024,2048]{1,0:T(8,128)(2,1)S(1)} %get-tuple-element.13.hist_ref), custom_call_target="tpu_custom_call" | custom-call | flops 536870912 | bytes 4194304 | tf_op jit(solution)/shard_map/memory_2_1/pallas_call | solution.py:110
  139.0 6.4 %collective-permute-start.2 = (bf16[32,64,128]{2,1,0:T(8,128)(2,1)S(1)}, bf16[32,64,128]{2,1,0:T(8,128)(2,1)S(1)}, u32[]{:S(2)}, u32[]{:S(2)}) collective-permute-start(bf16[32,64,128]{2,1,0:T(8,128)(2,1)S(1)} %memory_2_1.1), channel_id=1, source_target_pairs={{0,16},{16,0},{1,17},{17,1},{2,18},{18,2},{3,19},{19,3},{4,20},{20... | collective-permute-start | bytes 1572872 | tf_op jit(solution)/shard_map/ppermute | solution.py:252
  145.3 2.2 %memory_2_0.1 = bf16[32,64,128]{2,1,0:T(8,128)(2,1)S(1)} custom-call(s32[3,256]{1,0:T(4,128)S(1)} %copy-done.2, bf16[32,64,128]{2,1,0:T(8,128)(2,1)S(1)} %all_to_all.45.sigma_ref, bf16[1024,2048]{1,0:T(8,128)(2,1)S(1)} %get-tuple-element.13.hist_ref), custom_call_target="tpu_custom_call" | custom-call | flops 536870912 | bytes 4194304 | tf_op jit(solution)/shard_map/memory_2_0/pallas_call | solution.py:110
  147.6 0.0 collective-permute-done.2
  147.6 0.2 add_convert_fusion
  147.8 14.1 %all_to_all.46.terms_ref = bf16[32,64,128]{2,1,0:T(8,128)(2,1)S(1)} all-to-all(bf16[32,64,128]{2,1,0:T(8,128)(2,1)S(1)} %add_convert_fusion), channel_id=1, replica_groups=mesh['x'=4,'y'=4,'c'=2,'z_high'=8,'z_low'=2] {'z_low','x','y'}, dimensions={0} | all-to-all | bytes 1048576 | tf_op jit(solution)/shard_map/all_to_all | solution.py:239
  161.9 0.8 advance_01.1
  162.7 13.8 %all_to_all.47.own_ref = bf16[32,64,128]{2,1,0:T(8,128)(2,1)S(1)} all-to-all(bf16[32,64,128]{2,1,0:T(8,128)(2,1)S(1)} %bitcast.4), channel_id=1, replica_groups=mesh['x'=4,'y'=4,'c'=2,'z_high'=8,'z_low'=2] {'z_low','x','y'}, dimensions={0} | all-to-all | bytes 1048576 | tf_op jit(solution)/shard_map/all_to_all | solution.py:239
  176.5 5.0 %collective-permute-start.3 = (bf16[32,64,128]{2,1,0:T(8,128)(2,1)S(1)}, bf16[32,64,128]{2,1,0:T(8,128)(2,1)S(1)}, u32[]{:S(2)}, u32[]{:S(2)}) collective-permute-start(bf16[32,64,128]{2,1,0:T(8,128)(2,1)S(1)} %all_to_all.47.own_ref), channel_id=1, source_target_pairs={{0,16},{16,0},{1,17},{17,1},{2,18},{18,2},{3,19},{19,3},{4,20},{20... | collective-permute-start | bytes 1572872 | tf_op jit(solution)/shard_map/ppermute | solution.py:259
  181.5 1.5 collective-permute-done.3.other_ref
  183.0 2.5 %spread.1 = bf16[256,2048]{1,0:T(8,128)(2,1)} custom-call(bf16[32,64,128]{2,1,0:T(8,128)(2,1)S(1)} %all_to_all.47.own_ref, bf16[32,64,128]{2,1,0:T(8,128)(2,1)S(1)} %collective-permute-done.3.other_ref), custom_call_target="tpu_custom_call" | custom-call | tf_op jit(solution)/shard_map/spread/pallas_call | solution.py:228
  (7 shorter events, 0.1 us)
Async XLA Ops:
  0.0 12.5 %copy-start.2 = (s32[3,256]{1,0:T(4,128)S(1)}, s32[3,256]{1,0:T(4,128)}, u32[]{:S(2)}) copy-start(s32[3,256]{1,0:T(4,128)} %reach_ref.9) | copy-start | bytes 9220
  0.0 12.5 %copy-start.1 = (bf16[128,2048]{1,0:T(8,128)(2,1)S(1)}, bf16[128,2048]{1,0:T(8,128)(2,1)}, u32[]{:S(2)}) copy-start(bf16[128,2048]{1,0:T(8,128)(2,1)} %rest_0_.1) | copy-start | bytes 1572868
  3.7 10.5 %collective-permute-start = (bf16[32,64,128]{2,1,0:T(8,128)(2,1)S(1)}, bf16[32,64,128]{2,1,0:T(8,128)(2,1)S(1)}, u32[]{:S(2)}, u32[]{:S(2)}) collective-permute-start(bf16[32,64,128]{2,1,0:T(8,128)(2,1)S(1)} %get-tuple-element.14), channel_id=1, source_target_pairs={{0,16},{16,0},{1,17},{17,1},{2,18},{18,2},{3,19},{19,3},{4,20},{20... | collective-permute-start | bytes 1572872 | tf_op jit(solution)/shard_map/ppermute | solution.py:252
  12.5 15.3 %copy-start = (f32[128,128]{1,0:T(8,128)S(1)}, f32[128,128]{1,0:T(8,128)}, u32[]{:S(2)}) copy-start(f32[128,128]{1,0:T(8,128)} %step_ref.5) | copy-start | bytes 196612
  12.5 15.3 %copy-start.3 = (f32[128]{0:T(128)S(1)}, f32[128]{0:T(128)}, u32[]{:S(2)}) copy-start(f32[128]{0:T(128)} %param.10) | copy-start | bytes 1540
  76.9 8.2 %collective-permute-start.1 = (bf16[32,64,128]{2,1,0:T(8,128)(2,1)S(1)}, bf16[32,64,128]{2,1,0:T(8,128)(2,1)S(1)}, u32[]{:S(2)}, u32[]{:S(2)}) collective-permute-start(bf16[32,64,128]{2,1,0:T(8,128)(2,1)S(1)} %memory_1_1.1), channel_id=1, source_target_pairs={{0,16},{16,0},{1,17},{17,1},{2,18},{18,2},{3,19},{19,3},{4,20},{20... | collective-permute-start | bytes 1572872 | tf_op jit(solution)/shard_map/ppermute | solution.py:252
  139.0 8.6 %collective-permute-start.2 = (bf16[32,64,128]{2,1,0:T(8,128)(2,1)S(1)}, bf16[32,64,128]{2,1,0:T(8,128)(2,1)S(1)}, u32[]{:S(2)}, u32[]{:S(2)}) collective-permute-start(bf16[32,64,128]{2,1,0:T(8,128)(2,1)S(1)} %memory_2_1.1), channel_id=1, source_target_pairs={{0,16},{16,0},{1,17},{17,1},{2,18},{18,2},{3,19},{19,3},{4,20},{20... | collective-permute-start | bytes 1572872 | tf_op jit(solution)/shard_map/ppermute | solution.py:252
  176.5 6.6 %collective-permute-start.3 = (bf16[32,64,128]{2,1,0:T(8,128)(2,1)S(1)}, bf16[32,64,128]{2,1,0:T(8,128)(2,1)S(1)}, u32[]{:S(2)}, u32[]{:S(2)}) collective-permute-start(bf16[32,64,128]{2,1,0:T(8,128)(2,1)S(1)} %all_to_all.47.own_ref), channel_id=1, source_target_pairs={{0,16},{16,0},{1,17},{17,1},{2,18},{18,2},{3,19},{19,3},{4,20},{20... | collective-permute-start | bytes 1572872 | tf_op jit(solution)/shard_map/ppermute | solution.py:259

commit v6 on v5

--- a/solution.py
+++ b/solution.py
@@ -8,13 +8,14 @@
 from jax.sharding import Mesh
 from jax.sharding import PartitionSpec as P
 
-HIST = ("x", "y", "c")
-SECOND = ("z_high", "z_low")
-MIX = ("z_low", "x", "y")
+HIST = ("x_high", "x_low", "y_high", "y_low", "c")
+SECOND = ("z_3", "z_2", "z_1", "z_0")
+FAR = ("z_3", "z_1", "z_2")
+MIX = ("z_0", "x_high", "y_high", "x_low", "y_low")
 ROW_T = 128
 HALF = 64
 QUARTER = 32
-TILE = 256
+TILE = 512
 
 VMEM = pl.BlockSpec(memory_space=pltpu.VMEM)
 SMEM = pl.BlockSpec(memory_space=pltpu.SMEM)
@@ -43,7 +44,7 @@
 
 
 def tile_from_pieces(ref, group):
-    return lane_blocks_transposed([ref[4 * group + piece].astype(jnp.float32) for piece in range(4)])
+    return lane_blocks_transposed([ref[4 * group + piece] for piece in range(4)])
 
 
 def column_tile(block, half, step, reach_ref, sigma, hist_ref, out_ref, edge_ref=None):
@@ -54,45 +55,37 @@
     columns = []
     for tile in range(tiles):
         live = reach_ref[block, tile_0 + tile] - lax.axis_index(HIST) * past_loc
-        columns.append(
-            jnp.concatenate(
-                [
-                    jnp.where(
-                        past < live,
-                        hist_ref[past * ROW_T : (past + 1) * ROW_T, pl.ds(start + tile * ROW_T, ROW_T)],
-                        jnp.zeros((), hist_ref.dtype),
-                    )
-                    for past in range(past_loc)
-                ],
-                0,
-            )
-        )
+        parts = []
+        for past in range(past_loc):
+            keep = jnp.full((1, ROW_T), jnp.where(past < live, 1.0, 0.0), jnp.float32).astype(hist_ref.dtype)
+            part = hist_ref[past * ROW_T : (past + 1) * ROW_T, pl.ds(start + tile * ROW_T, ROW_T)]
+            parts.append(part * keep)
+        columns.append(jnp.concatenate(parts, 0))
     masked = jnp.concatenate(columns, 1)
     term = jnp.dot(sigma[...], masked, preferred_element_type=jnp.float32)
     for tile in range(tiles):
         parts = [term[at : at + HALF, tile * ROW_T : (tile + 1) * ROW_T] for at in PLACES]
         if edge_ref is not None:
-            adds = lax.axis_index(("x", "y")) == 0
+            adds = lax.axis_index(HIST[:4]) == 0
             for part in (0, 2):
                 edge = edge_ref[PLACES[part] : PLACES[part] + HALF, pl.ds(start + tile * ROW_T, ROW_T)]
                 parts[part] = parts[part] + jnp.where(adds, edge.astype(jnp.float32), 0.0)
-        for piece, value in enumerate(lane_blocks_transposed(parts)):
+        for piece, value in enumerate(lane_blocks_transposed([part.astype(out_ref.dtype) for part in parts])):
             out_ref[(step * tiles + tile) * 4 + piece] = value.astype(out_ref.dtype)
 
 
-def memory_kernel(block, first_half, from_pieces, with_edge, reach_ref, sigma_ref, hist_ref, *rest):
+def memory_kernel(block, first_half, with_edge, reach_ref, sigma_ref, hist_ref, *rest):
     own = lax.axis_index("c")
     half = 1 - own if first_half else own
-    edge_ref = rest[0] if with_edge else None
-    out_ref = rest[1] if with_edge else rest[0]
+    edge_ref, outs = (rest[0], rest[1:]) if with_edge else (None, rest)
     sigma = sigma_ref
-    if from_pieces:
-        sigma = rest[-1]
+    if first_half:
+        sigma = outs[1]
         for group in range(sigma_ref.shape[0] // 4):
             for at, value in zip(PLACES, tile_from_pieces(sigma_ref, group)):
                 sigma[at : at + HALF, group * ROW_T : (group + 1) * ROW_T] = value.astype(sigma.dtype)
     for step in range(hist_ref.shape[1] // 2 // TILE):
-        column_tile(block, half, step, reach_ref, sigma, hist_ref, out_ref, edge_ref)
+        column_tile(block, half, step, reach_ref, sigma, hist_ref, outs[0], edge_ref)
 
 
 def product_cost(rows, cols):
@@ -105,14 +98,13 @@
 
 def memory_terms(block, first_half, reach, sigma, history, edge=None):
     rows, cols = history.shape
-    from_pieces = sigma.ndim == 3
     extra = () if edge is None else (edge,)
+    joined = (jax.ShapeDtypeStruct((2 * ROW_T, rows), jnp.bfloat16),) if first_half else ()
     return pl.pallas_call(
-        functools.partial(memory_kernel, block, first_half, from_pieces, edge is not None),
-        out_shape=pieces_shape(cols // 2),
+        functools.partial(memory_kernel, block, first_half, edge is not None),
+        out_shape=(pieces_shape(cols // 2), *joined),
         in_specs=[SMEM, VMEM, VMEM] + [VMEM] * len(extra),
-        out_specs=VMEM,
-        scratch_shapes=[pltpu.VMEM((2 * ROW_T, rows), jnp.bfloat16)] if from_pieces else [],
+        out_specs=(VMEM,) * (1 + len(joined)),
         cost_estimate=product_cost(rows, cols // 2),
         compiler_params=PARAMS,
         name=f"memory_{block}_{int(first_half)}",
@@ -214,25 +206,39 @@
     return out[0], (None if last else out[1])
 
 
-def spread_kernel(own_ref, other_ref, out_ref):
+def spread_kernel(first, pieces_ref, *refs):
+    out_hbm, tile_ref, sems = refs[-3:]
     core = lax.axis_index("c")
-    for ref, half in ((own_ref, core), (other_ref, 1 - core)):
-        groups = ref.shape[0] // 4
-        for group in range(groups):
-            part = pl.ds(pl.multiple_of((half * groups + group) * ROW_T, ROW_T), ROW_T)
-            for at, value in zip(PLACES, tile_from_pieces(ref, group)):
-                out_ref[at : at + HALF, part] = value.astype(out_ref.dtype)
-
-
-def spread_out(own, other):
+    half = core if first else 1 - core
+    groups = pieces_ref.shape[0] // 4
+    copies = []
+    for group in range(groups):
+        for at, value in zip(PLACES, tile_from_pieces(pieces_ref, group)):
+            tile_ref[at : at + HALF, group * ROW_T : (group + 1) * ROW_T] = value.astype(tile_ref.dtype)
+        if group % 2:
+            here = tile_ref.at[:, (group - 1) * ROW_T : (group + 1) * ROW_T]
+            start = pl.multiple_of((half * groups + group - 1) * ROW_T, 2 * ROW_T)
+            copies.append(pltpu.make_async_copy(here, out_hbm.at[:, pl.ds(start, 2 * ROW_T)], sems.at[group // 2]))
+            copies[-1].start()
+    for copy in copies:
+        copy.wait()
+
+
+def spread_out(pieces, result=None):
+    width = pieces.shape[0] * QUARTER
+    first = result is None
+    hbm = pl.BlockSpec(memory_space=pltpu.HBM)
     return pl.pallas_call(
-        spread_kernel,
-        out_shape=jax.ShapeDtypeStruct((2 * ROW_T, 2 * own.shape[0] * QUARTER), jnp.bfloat16),
-        in_specs=[VMEM, VMEM],
-        out_specs=VMEM,
-        compiler_params=PARAMS,
-        name="spread",
-    )(own, other)
+        functools.partial(spread_kernel, first),
+        out_shape=jax.ShapeDtypeStruct((2 * ROW_T, 2 * width), jnp.bfloat16),
+        in_specs=[VMEM] if first else [VMEM, hbm],
+        out_specs=hbm,
+        scratch_shapes=[pltpu.VMEM((2 * ROW_T, width), jnp.bfloat16), pltpu.SemaphoreType.DMA((width // (2 * ROW_T),))],
+        input_output_aliases={} if first else {1: 0},
+        cost_estimate=pl.CostEstimate(flops=0, bytes_accessed=8 * ROW_T * width, transcendentals=0),
+        compiler_params=PARAMS,
+        name=f"spread_{int(first)}",
+    )(*((pieces,) if first else (pieces, result)))
 
 
 def exchange(x, axis):
@@ -248,20 +254,21 @@
         if block == 0:
             away, held, rows = first_terms(reach, self_rows, history)
         else:
-            away = memory_terms(block, True, reach, rows, held)
+            away, rows = memory_terms(block, True, reach, rows, held)
         arrived = lax.ppermute(away, "c", swap)
-        mine = memory_terms(block, False, reach, rows, held, edge_rows if block == 0 else None)
+        (mine,) = memory_terms(block, False, reach, rows, held, edge_rows if block == 0 else None)
         pair = (mine.astype(jnp.float32) + arrived.astype(jnp.float32)).astype(jnp.bfloat16)
         terms = exchange(pair, MIX)
         pieces, green = advance(block == 0, last, terms, green, step_inv, weights)
         if last:
             own = exchange(pieces.reshape(-1, HALF, ROW_T), MIX)
-            return spread_out(own, lax.ppermute(own, "c", swap))
-        places = exchange(pieces, "z_high").reshape(16, HALF, ROW_T)
+            other = lax.ppermute(own, "c", swap)
+            return spread_out(other, spread_out(own))
+        places = exchange(pieces, FAR).reshape(16, HALF, ROW_T)
         rows = exchange(jnp.concatenate([places, places]), MIX)
 
 
 def solution(mesh):
-    torus = Mesh(mesh.devices.reshape(4, 4, 2, 8, 2), HIST + SECOND)
+    torus = Mesh(mesh.devices.reshape((2,) * 9), HIST + SECOND)
     placed = (P(HIST, SECOND), P(None, HIST), P(None, SECOND), P(), P(), P())
     return jax.shard_map(local, mesh=torus, in_specs=placed, out_specs=P(None, SECOND), check_vma=False)

time: 186 us -> 183 us (0.984)
  blocking collectives: 138 us -> 140 us
  Pallas kernels: 19 us -> 17.1 us
    pallas_call x6 -> x7, Pallas kernels: 13.1 us -> 12.1 us  [the longest x5 9.32 us: memory_terms(): pl.pallas_call(functools.partial(memory_kernel, block, first_half, edge i...]
  transfers between devices with their start and end apart: 4 -> 4, of which waited for: 1 -> 1; matrix products, arithmetic and copies ran while one was open for 0% -> 0% of each run, Pallas kernels for 3% -> 4%
where the time goes in v6:
time: 183 us; the launch traced here: 182 us
  blocking collectives  140 us (77%)
  starting transfers between devices  24.3 us (13%)
  Pallas kernels  17.1 us (9%)
    all_to_all x8, blocking collectives, exchange(): return lax.all_to_all(x, axis, 0, 0, tiled=True)  140 us
    ppermute x3, starting transfers between devices, local(): arrived = lax.ppermute(away, 'c', swap)  19.4 us
    pallas_call x5, Pallas kernels, memory_terms(): pl.pallas_call(functools.partial(memory_kernel, block, first_half, edge i...  9.32 us
    ppermute x1, starting transfers between devices, local(): other = lax.ppermute(own, 'c', swap)  4.9 us
  transfers between devices with their start and end apart: 4, of which 1 were waited for; matrix products, arithmetic and copies ran while one was open for 0% of the time, Pallas kernels for 4%

profile of v6, /device:TPU:1, one launch (start us, length us, event | category | flops | bytes accessed | tf_op | source)
XLA Modules:
  0.0 182.1 jit_solution(15117543079990662876)
XLA Ops:
  0.0 2.9 %memory_first.1 = (bf16[32,64,128]{2,1,0:T(8,128)(2,1)S(1)}, bf16[1024,2048]{1,0:T(8,128)(2,1)S(1)}, bf16[256,1024]{1,0:T(8,128)(2,1)S(1)}) custom-call(s32[3,256]{1,0:T(4,128)} %reach_ref.9, bf16[256,1024]{1,0:T(8,128)(2,1)} %sigma_hbm.1, bf16[1024,2048]{1,0:T(8,128)(2,1)} %hist_hbm.1), custom_call_target="tpu_custom_call" | custom-call | flops 536870912 | bytes 4194304 | tf_op jit(solution)/shard_map/memory_first/pallas_call | solution.py:141
  2.9 8.7 %collective-permute-start = (bf16[32,64,128]{2,1,0:T(8,128)(2,1)S(1)}, bf16[32,64,128]{2,1,0:T(8,128)(2,1)S(1)}, u32[]{:S(2)}, u32[]{:S(2)}) collective-permute-start(bf16[32,64,128]{2,1,0:T(8,128)(2,1)S(1)} %get-tuple-element.18), channel_id=1, source_target_pairs={{0,16},{16,0},{1,17},{17,1},{2,18},{18,2},{3,19},{19,3},{4,20},{20... | collective-permute-start | bytes 1572872 | tf_op jit(solution)/shard_map/ppermute | solution.py:258
  11.6 0.0 copy-start
  11.7 0.0 copy-start.3
  11.7 1.7 memory_0_0.1
  13.4 0.0 collective-permute-done
  13.4 0.2 add_convert_fusion.2
  13.6 14.4 %all_to_all.40.terms_ref = bf16[32,64,128]{2,1,0:T(8,128)(2,1)S(1)} all-to-all(bf16[32,64,128]{2,1,0:T(8,128)(2,1)S(1)} %add_convert_fusion.2), channel_id=1, replica_groups=mesh['x_high'=2,'x_low'=2,'y_high'=2,'y_low'=2,'c'=2,'z_3'=2,'z_2'=2,'z_..., dimensions={0} | all-to-all | bytes 1048576 | tf_op jit(solution)/shard_map/all_to_all | solution.py:245
  28.0 0.7 advance_10.1
  28.8 30.5 %all_to_all.41 = bf16[8,2,64,128]{3,2,1,0:T(8,128)(2,1)S(1)} all-to-all(bf16[8,2,64,128]{3,2,1,0:T(8,128)(2,1)S(1)} %get-tuple-element.19), channel_id=1, replica_groups=mesh['x_high'=2,'x_low'=2,'y_high'=2,'y_low'=2,'c'=2,'z_3'=2,'z_2'=2,'z_..., dimensions={0} | all-to-all | bytes 524288 | tf_op jit(solution)/shard_map/all_to_all | solution.py:245
  59.3 15.8 %all_to_all.42.sigma_ref = bf16[32,64,128]{2,1,0:T(8,128)(2,1)S(1)} all-to-all(bf16[32,64,128]{2,1,0:T(8,128)(2,1)S(1)} %pad_maximum_fusion), channel_id=1, replica_groups=mesh['x_high'=2,'x_low'=2,'y_high'=2,'y_low'=2,'c'=2,'z_3'=2,'z_2'=2,'z_..., dimensions={0} | all-to-all | bytes 1048576 | tf_op jit(solution)/shard_map/all_to_all | solution.py:245
  75.2 2.1 %memory_1_1.1 = (bf16[32,64,128]{2,1,0:T(8,128)(2,1)S(1)}, bf16[256,1024]{1,0:T(8,128)(2,1)S(1)}) custom-call(s32[3,256]{1,0:T(4,128)S(1)} %copy-done.2, bf16[32,64,128]{2,1,0:T(8,128)(2,1)S(1)} %all_to_all.42.sigma_ref, bf16[1024,2048]{1,0:T(8,128)(2,1)S(1)} %get-tuple-element.17.hist_ref), custom_call_target="tpu_custom_call" | custom-call | flops 536870912 | bytes 4194304 | tf_op jit(solution)/shard_map/memory_1_1/pallas_call | solution.py:103
  77.2 5.2 %collective-permute-start.1 = (bf16[32,64,128]{2,1,0:T(8,128)(2,1)S(1)}, bf16[32,64,128]{2,1,0:T(8,128)(2,1)S(1)}, u32[]{:S(2)}, u32[]{:S(2)}) collective-permute-start(bf16[32,64,128]{2,1,0:T(8,128)(2,1)S(1)} %get-tuple-element.21), channel_id=1, source_target_pairs={{0,16},{16,0},{1,17},{17,1},{2,18},{18,2},{3,19},{19,3},{4,20},{20... | collective-permute-start | bytes 1572872 | tf_op jit(solution)/shard_map/ppermute | solution.py:258
  82.5 1.7 memory_1_0.1
  84.2 0.0 collective-permute-done.1
  84.2 0.2 add_convert_fusion.1
  84.4 14.6 %all_to_all.43.terms_ref = bf16[32,64,128]{2,1,0:T(8,128)(2,1)S(1)} all-to-all(bf16[32,64,128]{2,1,0:T(8,128)(2,1)S(1)} %add_convert_fusion.1), channel_id=1, replica_groups=mesh['x_high'=2,'x_low'=2,'y_high'=2,'y_low'=2,'c'=2,'z_3'=2,'z_2'=2,'z_..., dimensions={0} | all-to-all | bytes 1048576 | tf_op jit(solution)/shard_map/all_to_all | solution.py:245
  99.0 0.7 advance_00.1
  99.7 20.9 %all_to_all.44 = bf16[8,2,64,128]{3,2,1,0:T(8,128)(2,1)S(1)} all-to-all(bf16[8,2,64,128]{3,2,1,0:T(8,128)(2,1)S(1)} %get-tuple-element.23), channel_id=1, replica_groups=mesh['x_high'=2,'x_low'=2,'y_high'=2,'y_low'=2,'c'=2,'z_3'=2,'z_2'=2,'z_..., dimensions={0} | all-to-all | bytes 524288 | tf_op jit(solution)/shard_map/all_to_all | solution.py:245
  120.7 15.4 %all_to_all.45.sigma_ref = bf16[32,64,128]{2,1,0:T(8,128)(2,1)S(1)} all-to-all(bf16[32,64,128]{2,1,0:T(8,128)(2,1)S(1)} %pad_maximum_fusion.1), channel_id=1, replica_groups=mesh['x_high'=2,'x_low'=2,'y_high'=2,'y_low'=2,'c'=2,'z_3'=2,'z_2'=2,'z_..., dimensions={0} | all-to-all | bytes 1048576 | tf_op jit(solution)/shard_map/all_to_all | solution.py:245
  136.1 2.1 %memory_2_1.1 = (bf16[32,64,128]{2,1,0:T(8,128)(2,1)S(1)}, bf16[256,1024]{1,0:T(8,128)(2,1)S(1)}) custom-call(s32[3,256]{1,0:T(4,128)S(1)} %copy-done.2, bf16[32,64,128]{2,1,0:T(8,128)(2,1)S(1)} %all_to_all.45.sigma_ref, bf16[1024,2048]{1,0:T(8,128)(2,1)S(1)} %get-tuple-element.17.hist_ref), custom_call_target="tpu_custom_call" | custom-call | flops 536870912 | bytes 4194304 | tf_op jit(solution)/shard_map/memory_2_1/pallas_call | solution.py:103
  138.2 5.4 %collective-permute-start.2 = (bf16[32,64,128]{2,1,0:T(8,128)(2,1)S(1)}, bf16[32,64,128]{2,1,0:T(8,128)(2,1)S(1)}, u32[]{:S(2)}, u32[]{:S(2)}) collective-permute-start(bf16[32,64,128]{2,1,0:T(8,128)(2,1)S(1)} %get-tuple-element.25), channel_id=1, source_target_pairs={{0,16},{16,0},{1,17},{17,1},{2,18},{18,2},{3,19},{19,3},{4,20},{20... | collective-permute-start | bytes 1572872 | tf_op jit(solution)/shard_map/ppermute | solution.py:258
  143.6 1.7 memory_2_0.1
  145.3 0.0 collective-permute-done.2
  145.3 0.2 add_convert_fusion
  145.5 14.5 %all_to_all.46.terms_ref = bf16[32,64,128]{2,1,0:T(8,128)(2,1)S(1)} all-to-all(bf16[32,64,128]{2,1,0:T(8,128)(2,1)S(1)} %add_convert_fusion), channel_id=1, replica_groups=mesh['x_high'=2,'x_low'=2,'y_high'=2,'y_low'=2,'c'=2,'z_3'=2,'z_2'=2,'z_..., dimensions={0} | all-to-all | bytes 1048576 | tf_op jit(solution)/shard_map/all_to_all | solution.py:245
  160.1 0.8 advance_01.1
  160.8 13.5 %all_to_all.47.pieces_ref = bf16[32,64,128]{2,1,0:T(8,128)(2,1)S(1)} all-to-all(bf16[32,64,128]{2,1,0:T(8,128)(2,1)S(1)} %bitcast.4), channel_id=1, replica_groups=mesh['x_high'=2,'x_low'=2,'y_high'=2,'y_low'=2,'c'=2,'z_3'=2,'z_2'=2,'z_..., dimensions={0} | all-to-all | bytes 1048576 | tf_op jit(solution)/shard_map/all_to_all | solution.py:245
  174.3 4.9 %collective-permute-start.3 = (bf16[32,64,128]{2,1,0:T(8,128)(2,1)S(1)}, bf16[32,64,128]{2,1,0:T(8,128)(2,1)S(1)}, u32[]{:S(2)}, u32[]{:S(2)}) collective-permute-start(bf16[32,64,128]{2,1,0:T(8,128)(2,1)S(1)} %all_to_all.47.pieces_ref), channel_id=1, source_target_pairs={{0,16},{16,0},{1,17},{17,1},{2,18},{18,2},{3,19},{19,3},{4,20},{20... | collective-permute-start | bytes 1572872 | tf_op jit(solution)/shard_map/ppermute | solution.py:265
  179.2 1.4 spread_1.1.refs_0_
  180.6 0.1 collective-permute-done.3.pieces_ref
  180.8 1.4 spread_0.1
  (8 shorter events, 0.1 us)
Async XLA Ops:
  0.0 11.6 %copy-start.2 = (s32[3,256]{1,0:T(4,128)S(1)}, s32[3,256]{1,0:T(4,128)}, u32[]{:S(2)}) copy-start(s32[3,256]{1,0:T(4,128)} %reach_ref.9) | copy-start | bytes 9220
  0.0 11.6 %copy-start.1 = (bf16[128,2048]{1,0:T(8,128)(2,1)S(1)}, bf16[128,2048]{1,0:T(8,128)(2,1)}, u32[]{:S(2)}) copy-start(bf16[128,2048]{1,0:T(8,128)(2,1)} %rest_0_.1) | copy-start | bytes 1572868
  2.9 10.5 %collective-permute-start = (bf16[32,64,128]{2,1,0:T(8,128)(2,1)S(1)}, bf16[32,64,128]{2,1,0:T(8,128)(2,1)S(1)}, u32[]{:S(2)}, u32[]{:S(2)}) collective-permute-start(bf16[32,64,128]{2,1,0:T(8,128)(2,1)S(1)} %get-tuple-element.18), channel_id=1, source_target_pairs={{0,16},{16,0},{1,17},{17,1},{2,18},{18,2},{3,19},{19,3},{4,20},{20... | collective-permute-start | bytes 1572872 | tf_op jit(solution)/shard_map/ppermute | solution.py:258
  11.6 16.4 %copy-start = (f32[128,128]{1,0:T(8,128)S(1)}, f32[128,128]{1,0:T(8,128)}, u32[]{:S(2)}) copy-start(f32[128,128]{1,0:T(8,128)} %step_ref.5) | copy-start | bytes 196612
  11.7 16.4 %copy-start.3 = (f32[128]{0:T(128)S(1)}, f32[128]{0:T(128)}, u32[]{:S(2)}) copy-start(f32[128]{0:T(128)} %param.10) | copy-start | bytes 1540
  77.2 7.0 %collective-permute-start.1 = (bf16[32,64,128]{2,1,0:T(8,128)(2,1)S(1)}, bf16[32,64,128]{2,1,0:T(8,128)(2,1)S(1)}, u32[]{:S(2)}, u32[]{:S(2)}) collective-permute-start(bf16[32,64,128]{2,1,0:T(8,128)(2,1)S(1)} %get-tuple-element.21), channel_id=1, source_target_pairs={{0,16},{16,0},{1,17},{17,1},{2,18},{18,2},{3,19},{19,3},{4,20},{20... | collective-permute-start | bytes 1572872 | tf_op jit(solution)/shard_map/ppermute | solution.py:258
  138.2 7.2 %collective-permute-start.2 = (bf16[32,64,128]{2,1,0:T(8,128)(2,1)S(1)}, bf16[32,64,128]{2,1,0:T(8,128)(2,1)S(1)}, u32[]{:S(2)}, u32[]{:S(2)}) collective-permute-start(bf16[32,64,128]{2,1,0:T(8,128)(2,1)S(1)} %get-tuple-element.25), channel_id=1, source_target_pairs={{0,16},{16,0},{1,17},{17,1},{2,18},{18,2},{3,19},{19,3},{4,20},{20... | collective-permute-start | bytes 1572872 | tf_op jit(solution)/shard_map/ppermute | solution.py:258
  174.3 6.4 %collective-permute-start.3 = (bf16[32,64,128]{2,1,0:T(8,128)(2,1)S(1)}, bf16[32,64,128]{2,1,0:T(8,128)(2,1)S(1)}, u32[]{:S(2)}, u32[]{:S(2)}) collective-permute-start(bf16[32,64,128]{2,1,0:T(8,128)(2,1)S(1)} %all_to_all.47.pieces_ref), channel_id=1, source_target_pairs={{0,16},{16,0},{1,17},{17,1},{2,18},{18,2},{3,19},{19,3},{4,20},{20... | collective-permute-start | bytes 1572872 | tf_op jit(solution)/shard_map/ppermute | solution.py:265

commit v7 on v6

--- a/solution.py
+++ b/solution.py
@@ -10,8 +10,8 @@
 
 HIST = ("x_high", "x_low", "y_high", "y_low", "c")
 SECOND = ("z_3", "z_2", "z_1", "z_0")
-FAR = ("z_3", "z_1", "z_2")
-MIX = ("z_0", "x_high", "y_high", "x_low", "y_low")
+FAR = ("z_1", "z_3", "z_2")
+MIX = ("z_0", "y_high", "x_high", "x_low", "y_low")
 ROW_T = 128
 HALF = 64
 QUARTER = 32
@@ -157,6 +157,17 @@
     )(*(pltpu.with_memory_space_constraint(value, pltpu.HBM) for value in (reach, sigma, history)))
 
 
+def in_two(value):
+    high = value.astype(jnp.bfloat16)
+    return high, (value - high.astype(jnp.float32)).astype(jnp.bfloat16)
+
+
+def product(left, value):
+    right = in_two(value)
+    dot = functools.partial(jnp.dot, preferred_element_type=jnp.float32)
+    return dot(left[0], right[0]) + (dot(left[0], right[1]) + dot(left[1], right[0]))
+
+
 def step_kernel(first, last, terms_ref, step_ref, coupling_ref, *refs):
     count = terms_ref.shape[0] // 2
     sums = []
@@ -171,9 +182,9 @@
     if not first:
         source = source + jnp.where(step_0, pltpu.roll(refs[0][...], ROW_T - QUARTER, 1), 0.0)
         outs = refs[1:]
-    dot = functools.partial(jnp.dot, precision=lax.Precision.HIGHEST, preferred_element_type=jnp.float32)
-    moved = dot(step_ref[...], source)
-    rows = moved + dot(step_ref[...], jnp.where(step_0, 0.0, pltpu.roll(moved, QUARTER, 1)))
+    operator = in_two(step_ref[...])
+    moved = product(operator, source)
+    rows = moved + product(operator, jnp.where(step_0, 0.0, pltpu.roll(moved, QUARTER, 1)))
     result = rows
     if not last:
         weights = jnp.broadcast_to(coupling_ref[...], rows.shape).T

time: 183 us -> 183 us (level)
  blocking collectives: 140 us -> 143 us
    all_to_all x8, blocking collectives: 140 us -> 143 us  [exchange(): return lax.all_to_all(x, axis, 0, 0, tiled=True)]
where the time goes in v7:
time: 183 us
  blocking collectives  143 us (78%)
  starting transfers between devices  22.5 us (12%)
  Pallas kernels  16.8 us (9%)
    all_to_all x8, blocking collectives, exchange(): return lax.all_to_all(x, axis, 0, 0, tiled=True)  143 us
    ppermute x3, starting transfers between devices, local(): arrived = lax.ppermute(away, 'c', swap)  18.4 us
    pallas_call x5, Pallas kernels, memory_terms(): pl.pallas_call(functools.partial(memory_kernel, block, first_half, edge i...  9.31 us
    ppermute x1, starting transfers between devices, local(): other = lax.ppermute(own, 'c', swap)  4.11 us
  transfers between devices with their start and end apart: 4, of which 1 were waited for; matrix products, arithmetic and copies ran while one was open for 0% of the time, Pallas kernels for 4%

profile of v7, /device:TPU:1, one launch (start us, length us, event | category | flops | bytes accessed | tf_op | source)
XLA Modules:
  0.0 182.9 jit_solution(3959054875332472514)
XLA Ops:
  0.0 2.9 %memory_first.1 = (bf16[32,64,128]{2,1,0:T(8,128)(2,1)S(1)}, bf16[1024,2048]{1,0:T(8,128)(2,1)S(1)}, bf16[256,1024]{1,0:T(8,128)(2,1)S(1)}) custom-call(s32[3,256]{1,0:T(4,128)} %reach_ref.9, bf16[256,1024]{1,0:T(8,128)(2,1)} %sigma_hbm.1, bf16[1024,2048]{1,0:T(8,128)(2,1)} %hist_hbm.1), custom_call_target="tpu_custom_call" | custom-call | flops 536870912 | bytes 4194304 | tf_op jit(solution)/shard_map/memory_first/pallas_call | solution.py:141
  2.9 8.7 %collective-permute-start = (bf16[32,64,128]{2,1,0:T(8,128)(2,1)S(1)}, bf16[32,64,128]{2,1,0:T(8,128)(2,1)S(1)}, u32[]{:S(2)}, u32[]{:S(2)}) collective-permute-start(bf16[32,64,128]{2,1,0:T(8,128)(2,1)S(1)} %get-tuple-element.18), channel_id=1, source_target_pairs={{0,16},{16,0},{1,17},{17,1},{2,18},{18,2},{3,19},{19,3},{4,20},{20... | collective-permute-start | bytes 1572872 | tf_op jit(solution)/shard_map/ppermute | solution.py:269
  11.6 0.0 copy-start
  11.7 0.0 copy-start.3
  11.7 1.7 memory_0_0.1
  13.4 0.0 collective-permute-done
  13.4 0.2 add_convert_fusion.2
  13.6 14.4 %all_to_all.40.terms_ref = bf16[32,64,128]{2,1,0:T(8,128)(2,1)S(1)} all-to-all(bf16[32,64,128]{2,1,0:T(8,128)(2,1)S(1)} %add_convert_fusion.2), channel_id=1, replica_groups=mesh['x_high'=2,'x_low'=2,'y_high'=2,'y_low'=2,'c'=2,'z_3'=2,'z_2'=2,'z_..., dimensions={0} | all-to-all | bytes 1048576 | tf_op jit(solution)/shard_map/all_to_all | solution.py:256
  28.0 0.6 advance_10.1
  28.7 26.8 %all_to_all.41 = bf16[8,2,64,128]{3,2,1,0:T(8,128)(2,1)S(1)} all-to-all(bf16[8,2,64,128]{3,2,1,0:T(8,128)(2,1)S(1)} %get-tuple-element.19), channel_id=1, replica_groups=mesh['x_high'=2,'x_low'=2,'y_high'=2,'y_low'=2,'c'=2,'z_3'=2,'z_2'=2,'z_..., dimensions={0} | all-to-all | bytes 524288 | tf_op jit(solution)/shard_map/all_to_all | solution.py:256
  55.5 20.2 %all_to_all.42.sigma_ref = bf16[32,64,128]{2,1,0:T(8,128)(2,1)S(1)} all-to-all(bf16[32,64,128]{2,1,0:T(8,128)(2,1)S(1)} %pad_maximum_fusion), channel_id=1, replica_groups=mesh['x_high'=2,'x_low'=2,'y_high'=2,'y_low'=2,'c'=2,'z_3'=2,'z_2'=2,'z_..., dimensions={0} | all-to-all | bytes 1048576 | tf_op jit(solution)/shard_map/all_to_all | solution.py:256
  75.7 2.1 %memory_1_1.1 = (bf16[32,64,128]{2,1,0:T(8,128)(2,1)S(1)}, bf16[256,1024]{1,0:T(8,128)(2,1)S(1)}) custom-call(s32[3,256]{1,0:T(4,128)S(1)} %copy-done.2, bf16[32,64,128]{2,1,0:T(8,128)(2,1)S(1)} %all_to_all.42.sigma_ref, bf16[1024,2048]{1,0:T(8,128)(2,1)S(1)} %get-tuple-element.17.hist_ref), custom_call_target="tpu_custom_call" | custom-call | flops 536870912 | bytes 4194304 | tf_op jit(solution)/shard_map/memory_1_1/pallas_call | solution.py:103
  77.8 4.5 %collective-permute-start.1 = (bf16[32,64,128]{2,1,0:T(8,128)(2,1)S(1)}, bf16[32,64,128]{2,1,0:T(8,128)(2,1)S(1)}, u32[]{:S(2)}, u32[]{:S(2)}) collective-permute-start(bf16[32,64,128]{2,1,0:T(8,128)(2,1)S(1)} %get-tuple-element.21), channel_id=1, source_target_pairs={{0,16},{16,0},{1,17},{17,1},{2,18},{18,2},{3,19},{19,3},{4,20},{20... | collective-permute-start | bytes 1572872 | tf_op jit(solution)/shard_map/ppermute | solution.py:269
  82.3 1.7 memory_1_0.1
  84.0 0.0 collective-permute-done.1
  84.0 0.2 add_convert_fusion.1
  84.2 14.6 %all_to_all.43.terms_ref = bf16[32,64,128]{2,1,0:T(8,128)(2,1)S(1)} all-to-all(bf16[32,64,128]{2,1,0:T(8,128)(2,1)S(1)} %add_convert_fusion.1), channel_id=1, replica_groups=mesh['x_high'=2,'x_low'=2,'y_high'=2,'y_low'=2,'c'=2,'z_3'=2,'z_2'=2,'z_..., dimensions={0} | all-to-all | bytes 1048576 | tf_op jit(solution)/shard_map/all_to_all | solution.py:256
  98.8 0.6 advance_00.1
  99.4 17.7 %all_to_all.44 = bf16[8,2,64,128]{3,2,1,0:T(8,128)(2,1)S(1)} all-to-all(bf16[8,2,64,128]{3,2,1,0:T(8,128)(2,1)S(1)} %get-tuple-element.23), channel_id=1, replica_groups=mesh['x_high'=2,'x_low'=2,'y_high'=2,'y_low'=2,'c'=2,'z_3'=2,'z_2'=2,'z_..., dimensions={0} | all-to-all | bytes 524288 | tf_op jit(solution)/shard_map/all_to_all | solution.py:256
  117.2 19.2 %all_to_all.45.sigma_ref = bf16[32,64,128]{2,1,0:T(8,128)(2,1)S(1)} all-to-all(bf16[32,64,128]{2,1,0:T(8,128)(2,1)S(1)} %pad_maximum_fusion.1), channel_id=1, replica_groups=mesh['x_high'=2,'x_low'=2,'y_high'=2,'y_low'=2,'c'=2,'z_3'=2,'z_2'=2,'z_..., dimensions={0} | all-to-all | bytes 1048576 | tf_op jit(solution)/shard_map/all_to_all | solution.py:256
  136.4 2.1 %memory_2_1.1 = (bf16[32,64,128]{2,1,0:T(8,128)(2,1)S(1)}, bf16[256,1024]{1,0:T(8,128)(2,1)S(1)}) custom-call(s32[3,256]{1,0:T(4,128)S(1)} %copy-done.2, bf16[32,64,128]{2,1,0:T(8,128)(2,1)S(1)} %all_to_all.45.sigma_ref, bf16[1024,2048]{1,0:T(8,128)(2,1)S(1)} %get-tuple-element.17.hist_ref), custom_call_target="tpu_custom_call" | custom-call | flops 536870912 | bytes 4194304 | tf_op jit(solution)/shard_map/memory_2_1/pallas_call | solution.py:103
  138.5 5.2 %collective-permute-start.2 = (bf16[32,64,128]{2,1,0:T(8,128)(2,1)S(1)}, bf16[32,64,128]{2,1,0:T(8,128)(2,1)S(1)}, u32[]{:S(2)}, u32[]{:S(2)}) collective-permute-start(bf16[32,64,128]{2,1,0:T(8,128)(2,1)S(1)} %get-tuple-element.25), channel_id=1, source_target_pairs={{0,16},{16,0},{1,17},{17,1},{2,18},{18,2},{3,19},{19,3},{4,20},{20... | collective-permute-start | bytes 1572872 | tf_op jit(solution)/shard_map/ppermute | solution.py:269
  143.7 1.7 memory_2_0.1
  145.4 0.0 collective-permute-done.2
  145.4 0.2 add_convert_fusion
  145.6 14.6 %all_to_all.46.terms_ref = bf16[32,64,128]{2,1,0:T(8,128)(2,1)S(1)} all-to-all(bf16[32,64,128]{2,1,0:T(8,128)(2,1)S(1)} %add_convert_fusion), channel_id=1, replica_groups=mesh['x_high'=2,'x_low'=2,'y_high'=2,'y_low'=2,'c'=2,'z_3'=2,'z_2'=2,'z_..., dimensions={0} | all-to-all | bytes 1048576 | tf_op jit(solution)/shard_map/all_to_all | solution.py:256
  160.2 0.7 advance_01.1
  160.9 15.0 %all_to_all.47.pieces_ref = bf16[32,64,128]{2,1,0:T(8,128)(2,1)S(1)} all-to-all(bf16[32,64,128]{2,1,0:T(8,128)(2,1)S(1)} %bitcast.4), channel_id=1, replica_groups=mesh['x_high'=2,'x_low'=2,'y_high'=2,'y_low'=2,'c'=2,'z_3'=2,'z_2'=2,'z_..., dimensions={0} | all-to-all | bytes 1048576 | tf_op jit(solution)/shard_map/all_to_all | solution.py:256
  175.9 4.1 %collective-permute-start.3 = (bf16[32,64,128]{2,1,0:T(8,128)(2,1)S(1)}, bf16[32,64,128]{2,1,0:T(8,128)(2,1)S(1)}, u32[]{:S(2)}, u32[]{:S(2)}) collective-permute-start(bf16[32,64,128]{2,1,0:T(8,128)(2,1)S(1)} %all_to_all.47.pieces_ref), channel_id=1, source_target_pairs={{0,16},{16,0},{1,17},{17,1},{2,18},{18,2},{3,19},{19,3},{4,20},{20... | collective-permute-start | bytes 1572872 | tf_op jit(solution)/shard_map/ppermute | solution.py:276
  180.0 1.4 spread_1.1.refs_0_
  181.4 0.1 collective-permute-done.3.pieces_ref
  181.5 1.4 spread_0.1
  (8 shorter events, 0.1 us)
Async XLA Ops:
  0.0 11.6 %copy-start.2 = (s32[3,256]{1,0:T(4,128)S(1)}, s32[3,256]{1,0:T(4,128)}, u32[]{:S(2)}) copy-start(s32[3,256]{1,0:T(4,128)} %reach_ref.9) | copy-start | bytes 9220
  0.0 11.6 %copy-start.1 = (bf16[128,2048]{1,0:T(8,128)(2,1)S(1)}, bf16[128,2048]{1,0:T(8,128)(2,1)}, u32[]{:S(2)}) copy-start(bf16[128,2048]{1,0:T(8,128)(2,1)} %rest_0_.1) | copy-start | bytes 1572868
  2.9 10.5 %collective-permute-start = (bf16[32,64,128]{2,1,0:T(8,128)(2,1)S(1)}, bf16[32,64,128]{2,1,0:T(8,128)(2,1)S(1)}, u32[]{:S(2)}, u32[]{:S(2)}) collective-permute-start(bf16[32,64,128]{2,1,0:T(8,128)(2,1)S(1)} %get-tuple-element.18), channel_id=1, source_target_pairs={{0,16},{16,0},{1,17},{17,1},{2,18},{18,2},{3,19},{19,3},{4,20},{20... | collective-permute-start | bytes 1572872 | tf_op jit(solution)/shard_map/ppermute | solution.py:269
  11.6 16.4 %copy-start = (f32[128,128]{1,0:T(8,128)S(1)}, f32[128,128]{1,0:T(8,128)}, u32[]{:S(2)}) copy-start(f32[128,128]{1,0:T(8,128)} %step_ref.5) | copy-start | bytes 196612
  11.7 16.4 %copy-start.3 = (f32[128]{0:T(128)S(1)}, f32[128]{0:T(128)}, u32[]{:S(2)}) copy-start(f32[128]{0:T(128)} %param.10) | copy-start | bytes 1540
  77.8 6.2 %collective-permute-start.1 = (bf16[32,64,128]{2,1,0:T(8,128)(2,1)S(1)}, bf16[32,64,128]{2,1,0:T(8,128)(2,1)S(1)}, u32[]{:S(2)}, u32[]{:S(2)}) collective-permute-start(bf16[32,64,128]{2,1,0:T(8,128)(2,1)S(1)} %get-tuple-element.21), channel_id=1, source_target_pairs={{0,16},{16,0},{1,17},{17,1},{2,18},{18,2},{3,19},{19,3},{4,20},{20... | collective-permute-start | bytes 1572872 | tf_op jit(solution)/shard_map/ppermute | solution.py:269
  138.5 6.9 %collective-permute-start.2 = (bf16[32,64,128]{2,1,0:T(8,128)(2,1)S(1)}, bf16[32,64,128]{2,1,0:T(8,128)(2,1)S(1)}, u32[]{:S(2)}, u32[]{:S(2)}) collective-permute-start(bf16[32,64,128]{2,1,0:T(8,128)(2,1)S(1)} %get-tuple-element.25), channel_id=1, source_target_pairs={{0,16},{16,0},{1,17},{17,1},{2,18},{18,2},{3,19},{19,3},{4,20},{20... | collective-permute-start | bytes 1572872 | tf_op jit(solution)/shard_map/ppermute | solution.py:269
  175.9 5.6 %collective-permute-start.3 = (bf16[32,64,128]{2,1,0:T(8,128)(2,1)S(1)}, bf16[32,64,128]{2,1,0:T(8,128)(2,1)S(1)}, u32[]{:S(2)}, u32[]{:S(2)}) collective-permute-start(bf16[32,64,128]{2,1,0:T(8,128)(2,1)S(1)} %all_to_all.47.pieces_ref), channel_id=1, source_target_pairs={{0,16},{16,0},{1,17},{17,1},{2,18},{18,2},{3,19},{19,3},{4,20},{20... | collective-permute-start | bytes 1572872 | tf_op jit(solution)/shard_map/ppermute | solution.py:276

commit v8 on v7

--- a/solution.py
+++ b/solution.py
@@ -11,7 +11,7 @@
 HIST = ("x_high", "x_low", "y_high", "y_low", "c")
 SECOND = ("z_3", "z_2", "z_1", "z_0")
 FAR = ("z_1", "z_3", "z_2")
-MIX = ("z_0", "y_high", "x_high", "x_low", "y_low")
+MIX = ("z_0", "x_high", "y_high", "x_low", "y_low")
 ROW_T = 128
 HALF = 64
 QUARTER = 32
@@ -275,7 +275,7 @@
             own = exchange(pieces.reshape(-1, HALF, ROW_T), MIX)
             other = lax.ppermute(own, "c", swap)
             return spread_out(other, spread_out(own))
-        places = exchange(pieces, FAR).reshape(16, HALF, ROW_T)
+        places = exchange(pieces, FAR).reshape(2, 2, -1, HALF, ROW_T).swapaxes(0, 1).reshape(16, HALF, ROW_T)
         rows = exchange(jnp.concatenate([places, places]), MIX)
 
 

time: 183 us -> 181 us (0.989)
  blocking collectives: 143 us -> 139 us
    all_to_all x8, blocking collectives: 143 us -> 139 us  [exchange(): return lax.all_to_all(x, axis, 0, 0, tiled=True)]
where the time goes in v8:
time: 181 us
  blocking collectives  139 us (77%)
  starting transfers between devices  24.2 us (13%)
  Pallas kernels  16.8 us (9%)
    all_to_all x8, blocking collectives, exchange(): return lax.all_to_all(x, axis, 0, 0, tiled=True)  139 us
    ppermute x3, starting transfers between devices, local(): arrived = lax.ppermute(away, 'c', swap)  19.1 us
    pallas_call x5, Pallas kernels, memory_terms(): pl.pallas_call(functools.partial(memory_kernel, block, first_half, edge i...  9.31 us
    ppermute x1, starting transfers between devices, local(): other = lax.ppermute(own, 'c', swap)  5.02 us
  transfers between devices with their start and end apart: 4, of which 1 were waited for; matrix products, arithmetic and copies ran while one was open for 0% of the time, Pallas kernels for 4%

profile of v8, /device:TPU:1, one launch (start us, length us, event | category | flops | bytes accessed | tf_op | source)
XLA Modules:
  0.0 180.6 jit_solution(2337443510540512902)
XLA Ops:
  0.0 2.9 %memory_first.1 = (bf16[32,64,128]{2,1,0:T(8,128)(2,1)S(1)}, bf16[1024,2048]{1,0:T(8,128)(2,1)S(1)}, bf16[256,1024]{1,0:T(8,128)(2,1)S(1)}) custom-call(s32[3,256]{1,0:T(4,128)} %reach_ref.9, bf16[256,1024]{1,0:T(8,128)(2,1)} %sigma_hbm.1, bf16[1024,2048]{1,0:T(8,128)(2,1)} %hist_hbm.1), custom_call_target="tpu_custom_call" | custom-call | flops 536870912 | bytes 4194304 | tf_op jit(solution)/shard_map/memory_first/pallas_call | solution.py:141
  2.9 8.7 %collective-permute-start = (bf16[32,64,128]{2,1,0:T(8,128)(2,1)S(1)}, bf16[32,64,128]{2,1,0:T(8,128)(2,1)S(1)}, u32[]{:S(2)}, u32[]{:S(2)}) collective-permute-start(bf16[32,64,128]{2,1,0:T(8,128)(2,1)S(1)} %get-tuple-element.18), channel_id=1, source_target_pairs={{0,16},{16,0},{1,17},{17,1},{2,18},{18,2},{3,19},{19,3},{4,20},{20... | collective-permute-start | bytes 1572872 | tf_op jit(solution)/shard_map/ppermute | solution.py:269
  11.6 0.0 copy-start
  11.7 0.0 copy-start.3
  11.7 1.7 memory_0_0.1
  13.4 0.0 collective-permute-done
  13.4 0.2 add_convert_fusion.2
  13.6 14.4 %all_to_all.40.terms_ref = bf16[32,64,128]{2,1,0:T(8,128)(2,1)S(1)} all-to-all(bf16[32,64,128]{2,1,0:T(8,128)(2,1)S(1)} %add_convert_fusion.2), channel_id=1, replica_groups=mesh['x_high'=2,'x_low'=2,'y_high'=2,'y_low'=2,'c'=2,'z_3'=2,'z_2'=2,'z_..., dimensions={0} | all-to-all | bytes 1048576 | tf_op jit(solution)/shard_map/all_to_all | solution.py:256
  28.0 0.6 advance_10.1
  28.7 26.8 %all_to_all.41 = bf16[8,2,64,128]{3,2,1,0:T(8,128)(2,1)S(1)} all-to-all(bf16[8,2,64,128]{3,2,1,0:T(8,128)(2,1)S(1)} %get-tuple-element.19), channel_id=1, replica_groups=mesh['x_high'=2,'x_low'=2,'y_high'=2,'y_low'=2,'c'=2,'z_3'=2,'z_2'=2,'z_..., dimensions={0} | all-to-all | bytes 524288 | tf_op jit(solution)/shard_map/all_to_all | solution.py:256
  55.6 18.4 %all_to_all.42.sigma_ref = bf16[32,64,128]{2,1,0:T(8,128)(2,1)S(1)} all-to-all(bf16[32,64,128]{2,1,0:T(8,128)(2,1)S(1)} %pad_maximum_fusion), channel_id=1, replica_groups=mesh['x_high'=2,'x_low'=2,'y_high'=2,'y_low'=2,'c'=2,'z_3'=2,'z_2'=2,'z_..., dimensions={0} | all-to-all | bytes 1048576 | tf_op jit(solution)/shard_map/all_to_all | solution.py:256
  73.9 2.1 %memory_1_1.1 = (bf16[32,64,128]{2,1,0:T(8,128)(2,1)S(1)}, bf16[256,1024]{1,0:T(8,128)(2,1)S(1)}) custom-call(s32[3,256]{1,0:T(4,128)S(1)} %copy-done.2, bf16[32,64,128]{2,1,0:T(8,128)(2,1)S(1)} %all_to_all.42.sigma_ref, bf16[1024,2048]{1,0:T(8,128)(2,1)S(1)} %get-tuple-element.17.hist_ref), custom_call_target="tpu_custom_call" | custom-call | flops 536870912 | bytes 4194304 | tf_op jit(solution)/shard_map/memory_1_1/pallas_call | solution.py:103
  76.0 5.2 %collective-permute-start.1 = (bf16[32,64,128]{2,1,0:T(8,128)(2,1)S(1)}, bf16[32,64,128]{2,1,0:T(8,128)(2,1)S(1)}, u32[]{:S(2)}, u32[]{:S(2)}) collective-permute-start(bf16[32,64,128]{2,1,0:T(8,128)(2,1)S(1)} %get-tuple-element.21), channel_id=1, source_target_pairs={{0,16},{16,0},{1,17},{17,1},{2,18},{18,2},{3,19},{19,3},{4,20},{20... | collective-permute-start | bytes 1572872 | tf_op jit(solution)/shard_map/ppermute | solution.py:269
  81.2 1.7 memory_1_0.1
  82.9 0.0 collective-permute-done.1
  82.9 0.2 add_convert_fusion.1
  83.1 14.6 %all_to_all.43.terms_ref = bf16[32,64,128]{2,1,0:T(8,128)(2,1)S(1)} all-to-all(bf16[32,64,128]{2,1,0:T(8,128)(2,1)S(1)} %add_convert_fusion.1), channel_id=1, replica_groups=mesh['x_high'=2,'x_low'=2,'y_high'=2,'y_low'=2,'c'=2,'z_3'=2,'z_2'=2,'z_..., dimensions={0} | all-to-all | bytes 1048576 | tf_op jit(solution)/shard_map/all_to_all | solution.py:256
  97.7 0.6 advance_00.1
  98.3 18.3 %all_to_all.44 = bf16[8,2,64,128]{3,2,1,0:T(8,128)(2,1)S(1)} all-to-all(bf16[8,2,64,128]{3,2,1,0:T(8,128)(2,1)S(1)} %get-tuple-element.23), channel_id=1, replica_groups=mesh['x_high'=2,'x_low'=2,'y_high'=2,'y_low'=2,'c'=2,'z_3'=2,'z_2'=2,'z_..., dimensions={0} | all-to-all | bytes 524288 | tf_op jit(solution)/shard_map/all_to_all | solution.py:256
  116.7 18.1 %all_to_all.45.sigma_ref = bf16[32,64,128]{2,1,0:T(8,128)(2,1)S(1)} all-to-all(bf16[32,64,128]{2,1,0:T(8,128)(2,1)S(1)} %pad_maximum_fusion.1), channel_id=1, replica_groups=mesh['x_high'=2,'x_low'=2,'y_high'=2,'y_low'=2,'c'=2,'z_3'=2,'z_2'=2,'z_..., dimensions={0} | all-to-all | bytes 1048576 | tf_op jit(solution)/shard_map/all_to_all | solution.py:256
  134.8 2.1 %memory_2_1.1 = (bf16[32,64,128]{2,1,0:T(8,128)(2,1)S(1)}, bf16[256,1024]{1,0:T(8,128)(2,1)S(1)}) custom-call(s32[3,256]{1,0:T(4,128)S(1)} %copy-done.2, bf16[32,64,128]{2,1,0:T(8,128)(2,1)S(1)} %all_to_all.45.sigma_ref, bf16[1024,2048]{1,0:T(8,128)(2,1)S(1)} %get-tuple-element.17.hist_ref), custom_call_target="tpu_custom_call" | custom-call | flops 536870912 | bytes 4194304 | tf_op jit(solution)/shard_map/memory_2_1/pallas_call | solution.py:103
  136.9 5.2 %collective-permute-start.2 = (bf16[32,64,128]{2,1,0:T(8,128)(2,1)S(1)}, bf16[32,64,128]{2,1,0:T(8,128)(2,1)S(1)}, u32[]{:S(2)}, u32[]{:S(2)}) collective-permute-start(bf16[32,64,128]{2,1,0:T(8,128)(2,1)S(1)} %get-tuple-element.25), channel_id=1, source_target_pairs={{0,16},{16,0},{1,17},{17,1},{2,18},{18,2},{3,19},{19,3},{4,20},{20... | collective-permute-start | bytes 1572872 | tf_op jit(solution)/shard_map/ppermute | solution.py:269
  142.1 1.7 memory_2_0.1
  143.9 0.0 collective-permute-done.2
  143.9 0.2 add_convert_fusion
  144.1 14.6 %all_to_all.46.terms_ref = bf16[32,64,128]{2,1,0:T(8,128)(2,1)S(1)} all-to-all(bf16[32,64,128]{2,1,0:T(8,128)(2,1)S(1)} %add_convert_fusion), channel_id=1, replica_groups=mesh['x_high'=2,'x_low'=2,'y_high'=2,'y_low'=2,'c'=2,'z_3'=2,'z_2'=2,'z_..., dimensions={0} | all-to-all | bytes 1048576 | tf_op jit(solution)/shard_map/all_to_all | solution.py:256
  158.6 0.7 advance_01.1
  159.3 13.4 %all_to_all.47.pieces_ref = bf16[32,64,128]{2,1,0:T(8,128)(2,1)S(1)} all-to-all(bf16[32,64,128]{2,1,0:T(8,128)(2,1)S(1)} %bitcast.10), channel_id=1, replica_groups=mesh['x_high'=2,'x_low'=2,'y_high'=2,'y_low'=2,'c'=2,'z_3'=2,'z_2'=2,'z_..., dimensions={0} | all-to-all | bytes 1048576 | tf_op jit(solution)/shard_map/all_to_all | solution.py:256
  172.7 5.0 %collective-permute-start.3 = (bf16[32,64,128]{2,1,0:T(8,128)(2,1)S(1)}, bf16[32,64,128]{2,1,0:T(8,128)(2,1)S(1)}, u32[]{:S(2)}, u32[]{:S(2)}) collective-permute-start(bf16[32,64,128]{2,1,0:T(8,128)(2,1)S(1)} %all_to_all.47.pieces_ref), channel_id=1, source_target_pairs={{0,16},{16,0},{1,17},{17,1},{2,18},{18,2},{3,19},{19,3},{4,20},{20... | collective-permute-start | bytes 1572872 | tf_op jit(solution)/shard_map/ppermute | solution.py:276
  177.7 1.4 spread_1.1.refs_0_
  179.1 0.1 collective-permute-done.3.pieces_ref
  179.2 1.4 spread_0.1
  (10 shorter events, 0.1 us)
Async XLA Ops:
  0.0 11.6 %copy-start.2 = (s32[3,256]{1,0:T(4,128)S(1)}, s32[3,256]{1,0:T(4,128)}, u32[]{:S(2)}) copy-start(s32[3,256]{1,0:T(4,128)} %reach_ref.9) | copy-start | bytes 9220
  0.0 11.6 %copy-start.1 = (bf16[128,2048]{1,0:T(8,128)(2,1)S(1)}, bf16[128,2048]{1,0:T(8,128)(2,1)}, u32[]{:S(2)}) copy-start(bf16[128,2048]{1,0:T(8,128)(2,1)} %rest_0_.1) | copy-start | bytes 1572868
  2.9 10.5 %collective-permute-start = (bf16[32,64,128]{2,1,0:T(8,128)(2,1)S(1)}, bf16[32,64,128]{2,1,0:T(8,128)(2,1)S(1)}, u32[]{:S(2)}, u32[]{:S(2)}) collective-permute-start(bf16[32,64,128]{2,1,0:T(8,128)(2,1)S(1)} %get-tuple-element.18), channel_id=1, source_target_pairs={{0,16},{16,0},{1,17},{17,1},{2,18},{18,2},{3,19},{19,3},{4,20},{20... | collective-permute-start | bytes 1572872 | tf_op jit(solution)/shard_map/ppermute | solution.py:269
  11.6 16.4 %copy-start = (f32[128,128]{1,0:T(8,128)S(1)}, f32[128,128]{1,0:T(8,128)}, u32[]{:S(2)}) copy-start(f32[128,128]{1,0:T(8,128)} %step_ref.5) | copy-start | bytes 196612
  11.7 16.4 %copy-start.3 = (f32[128]{0:T(128)S(1)}, f32[128]{0:T(128)}, u32[]{:S(2)}) copy-start(f32[128]{0:T(128)} %param.10) | copy-start | bytes 1540
  76.0 6.9 %collective-permute-start.1 = (bf16[32,64,128]{2,1,0:T(8,128)(2,1)S(1)}, bf16[32,64,128]{2,1,0:T(8,128)(2,1)S(1)}, u32[]{:S(2)}, u32[]{:S(2)}) collective-permute-start(bf16[32,64,128]{2,1,0:T(8,128)(2,1)S(1)} %get-tuple-element.21), channel_id=1, source_target_pairs={{0,16},{16,0},{1,17},{17,1},{2,18},{18,2},{3,19},{19,3},{4,20},{20... | collective-permute-start | bytes 1572872 | tf_op jit(solution)/shard_map/ppermute | solution.py:269
  136.9 7.0 %collective-permute-start.2 = (bf16[32,64,128]{2,1,0:T(8,128)(2,1)S(1)}, bf16[32,64,128]{2,1,0:T(8,128)(2,1)S(1)}, u32[]{:S(2)}, u32[]{:S(2)}) collective-permute-start(bf16[32,64,128]{2,1,0:T(8,128)(2,1)S(1)} %get-tuple-element.25), channel_id=1, source_target_pairs={{0,16},{16,0},{1,17},{17,1},{2,18},{18,2},{3,19},{19,3},{4,20},{20... | collective-permute-start | bytes 1572872 | tf_op jit(solution)/shard_map/ppermute | solution.py:269
  172.7 6.5 %collective-permute-start.3 = (bf16[32,64,128]{2,1,0:T(8,128)(2,1)S(1)}, bf16[32,64,128]{2,1,0:T(8,128)(2,1)S(1)}, u32[]{:S(2)}, u32[]{:S(2)}) collective-permute-start(bf16[32,64,128]{2,1,0:T(8,128)(2,1)S(1)} %all_to_all.47.pieces_ref), channel_id=1, source_target_pairs={{0,16},{16,0},{1,17},{17,1},{2,18},{18,2},{3,19},{19,3},{4,20},{20... | collective-permute-start | bytes 1572872 | tf_op jit(solution)/shard_map/ppermute | solution.py:276

commit v9 on v8

--- a/solution.py
+++ b/solution.py
@@ -16,6 +16,7 @@
 HALF = 64
 QUARTER = 32
 TILE = 512
+STAGGER = 1500
 
 VMEM = pl.BlockSpec(memory_space=pltpu.VMEM)
 SMEM = pl.BlockSpec(memory_space=pltpu.SMEM)
@@ -191,6 +192,12 @@
         square = rows * rows
         result = weights * rows * square / (1.0 + square)
         outs[1][...] = rows
+    if not last:
+
+        @pl.when(lax.axis_index("c") == 1)
+        def _():
+            pl.delay(STAGGER)
+
     planes = [value.astype(jnp.bfloat16) for value in swapped(result[:HALF], result[HALF:], HALF)]
     for plane in range(2):
         for copy in range(outs[0].shape[1 if last else 0]):

time: 181 us -> 186 us (1.028)
  blocking collectives: 139 us -> 143 us
  starting transfers between devices: 24.2 us -> 21 us
  Pallas kernels: 16.8 us -> 19.9 us
    all_to_all x8, blocking collectives: 139 us -> 143 us  [exchange(): return lax.all_to_all(x, axis, 0, 0, tiled=True)]
    ppermute x3, starting transfers between devices: 19.1 us -> 16 us  [local(): arrived = lax.ppermute(away, 'c', swap)]
    pallas_call x3, Pallas kernels: 1.92 us -> 4.94 us  [advance(): pl.pallas_call(functools.partial(step_kernel, first, last), out_shape=tup...]
where the time goes in v9:
time: 186 us; the launch traced here: 185 us
  blocking collectives  143 us (77%)
  starting transfers between devices  21 us (11%)
  Pallas kernels  19.9 us (11%)
    all_to_all x8, blocking collectives, exchange(): return lax.all_to_all(x, axis, 0, 0, tiled=True)  143 us
    ppermute x3, starting transfers between devices, local(): arrived = lax.ppermute(away, 'c', swap)  16 us
    pallas_call x5, Pallas kernels, memory_terms(): pl.pallas_call(functools.partial(memory_kernel, block, first_half, edge i...  9.31 us
    ppermute x1, starting transfers between devices, local(): other = lax.ppermute(own, 'c', swap)  5.02 us
    pallas_call x3, Pallas kernels, advance(): pl.pallas_call(functools.partial(step_kernel, first, last), out_shape=tup...  4.94 us
  transfers between devices with their start and end apart: 4, of which 1 were waited for; matrix products, arithmetic and copies ran while one was open for 0% of the time, Pallas kernels for 4%

profile of v9, /device:TPU:1, one launch (start us, length us, event | category | flops | bytes accessed | tf_op | source)
XLA Modules:
  0.0 185.1 jit_solution(4805929350629600191)
XLA Ops:
  0.0 2.9 %memory_first.1 = (bf16[32,64,128]{2,1,0:T(8,128)(2,1)S(1)}, bf16[1024,2048]{1,0:T(8,128)(2,1)S(1)}, bf16[256,1024]{1,0:T(8,128)(2,1)S(1)}) custom-call(s32[3,256]{1,0:T(4,128)} %reach_ref.9, bf16[256,1024]{1,0:T(8,128)(2,1)} %sigma_hbm.1, bf16[1024,2048]{1,0:T(8,128)(2,1)} %hist_hbm.1), custom_call_target="tpu_custom_call" | custom-call | flops 536870912 | bytes 4194304 | tf_op jit(solution)/shard_map/memory_first/pallas_call | solution.py:142
  2.9 8.7 %collective-permute-start = (bf16[32,64,128]{2,1,0:T(8,128)(2,1)S(1)}, bf16[32,64,128]{2,1,0:T(8,128)(2,1)S(1)}, u32[]{:S(2)}, u32[]{:S(2)}) collective-permute-start(bf16[32,64,128]{2,1,0:T(8,128)(2,1)S(1)} %get-tuple-element.18), channel_id=1, source_target_pairs={{0,16},{16,0},{1,17},{17,1},{2,18},{18,2},{3,19},{19,3},{4,20},{20... | collective-permute-start | bytes 1572872 | tf_op jit(solution)/shard_map/ppermute | solution.py:276
  11.6 0.0 copy-start
  11.7 0.0 copy-start.3
  11.7 1.7 memory_0_0.1
  13.4 0.0 collective-permute-done
  13.4 0.2 add_convert_fusion.2
  13.6 14.4 %all_to_all.40.terms_ref = bf16[32,64,128]{2,1,0:T(8,128)(2,1)S(1)} all-to-all(bf16[32,64,128]{2,1,0:T(8,128)(2,1)S(1)} %add_convert_fusion.2), channel_id=1, replica_groups=mesh['x_high'=2,'x_low'=2,'y_high'=2,'y_low'=2,'c'=2,'z_3'=2,'z_2'=2,'z_..., dimensions={0} | all-to-all | bytes 1048576 | tf_op jit(solution)/shard_map/all_to_all | solution.py:263
  28.0 2.1 %advance_10.1 = (bf16[8,2,64,128]{3,2,1,0:T(8,128)(2,1)S(1)}, f32[128,128]{1,0:T(8,128)S(1)}) custom-call(bf16[32,64,128]{2,1,0:T(8,128)(2,1)S(1)} %all_to_all.40.terms_ref, f32[128,128]{1,0:T(8,128)S(1)} %copy-done, f32[1,128]{1,0:T(1,128)S(1)} %bitcast.11), custom_call_target="tpu_custom_call" | custom-call | tf_op jit(solution)/shard_map/advance_10/pallas_call | solution.py:216
  30.2 27.6 %all_to_all.41 = bf16[8,2,64,128]{3,2,1,0:T(8,128)(2,1)S(1)} all-to-all(bf16[8,2,64,128]{3,2,1,0:T(8,128)(2,1)S(1)} %get-tuple-element.19), channel_id=1, replica_groups=mesh['x_high'=2,'x_low'=2,'y_high'=2,'y_low'=2,'c'=2,'z_3'=2,'z_2'=2,'z_..., dimensions={0} | all-to-all | bytes 524288 | tf_op jit(solution)/shard_map/all_to_all | solution.py:263
  57.8 20.1 %all_to_all.42.sigma_ref = bf16[32,64,128]{2,1,0:T(8,128)(2,1)S(1)} all-to-all(bf16[32,64,128]{2,1,0:T(8,128)(2,1)S(1)} %pad_maximum_fusion), channel_id=1, replica_groups=mesh['x_high'=2,'x_low'=2,'y_high'=2,'y_low'=2,'c'=2,'z_3'=2,'z_2'=2,'z_..., dimensions={0} | all-to-all | bytes 1048576 | tf_op jit(solution)/shard_map/all_to_all | solution.py:263
  77.9 2.1 %memory_1_1.1 = (bf16[32,64,128]{2,1,0:T(8,128)(2,1)S(1)}, bf16[256,1024]{1,0:T(8,128)(2,1)S(1)}) custom-call(s32[3,256]{1,0:T(4,128)S(1)} %copy-done.2, bf16[32,64,128]{2,1,0:T(8,128)(2,1)S(1)} %all_to_all.42.sigma_ref, bf16[1024,2048]{1,0:T(8,128)(2,1)S(1)} %get-tuple-element.17.hist_ref), custom_call_target="tpu_custom_call" | custom-call | flops 536870912 | bytes 4194304 | tf_op jit(solution)/shard_map/memory_1_1/pallas_call | solution.py:104
  80.0 3.6 %collective-permute-start.1 = (bf16[32,64,128]{2,1,0:T(8,128)(2,1)S(1)}, bf16[32,64,128]{2,1,0:T(8,128)(2,1)S(1)}, u32[]{:S(2)}, u32[]{:S(2)}) collective-permute-start(bf16[32,64,128]{2,1,0:T(8,128)(2,1)S(1)} %get-tuple-element.21), channel_id=1, source_target_pairs={{0,16},{16,0},{1,17},{17,1},{2,18},{18,2},{3,19},{19,3},{4,20},{20... | collective-permute-start | bytes 1572872 | tf_op jit(solution)/shard_map/ppermute | solution.py:276
  83.6 1.7 memory_1_0.1
  85.3 0.0 collective-permute-done.1
  85.4 0.2 add_convert_fusion.1
  85.5 14.7 %all_to_all.43.terms_ref = bf16[32,64,128]{2,1,0:T(8,128)(2,1)S(1)} all-to-all(bf16[32,64,128]{2,1,0:T(8,128)(2,1)S(1)} %add_convert_fusion.1), channel_id=1, replica_groups=mesh['x_high'=2,'x_low'=2,'y_high'=2,'y_low'=2,'c'=2,'z_3'=2,'z_2'=2,'z_..., dimensions={0} | all-to-all | bytes 1048576 | tf_op jit(solution)/shard_map/all_to_all | solution.py:263
  100.3 2.1 %advance_00.1 = (bf16[8,2,64,128]{3,2,1,0:T(8,128)(2,1)S(1)}, f32[128,128]{1,0:T(8,128)S(1)}) custom-call(bf16[32,64,128]{2,1,0:T(8,128)(2,1)S(1)} %all_to_all.43.terms_ref, f32[128,128]{1,0:T(8,128)S(1)} %copy-done, f32[1,128]{1,0:T(1,128)S(1)} %bitcast.12, f32[128,128]{1,0:T(8,128)S(1)} %get-tuple-element.22.refs_0_), custom_call_target="tpu_custom_call" | custom-call | tf_op jit(solution)/shard_map/advance_00/pallas_call | solution.py:216
  102.4 18.2 %all_to_all.44 = bf16[8,2,64,128]{3,2,1,0:T(8,128)(2,1)S(1)} all-to-all(bf16[8,2,64,128]{3,2,1,0:T(8,128)(2,1)S(1)} %get-tuple-element.23), channel_id=1, replica_groups=mesh['x_high'=2,'x_low'=2,'y_high'=2,'y_low'=2,'c'=2,'z_3'=2,'z_2'=2,'z_..., dimensions={0} | all-to-all | bytes 524288 | tf_op jit(solution)/shard_map/all_to_all | solution.py:263
  120.7 20.1 %all_to_all.45.sigma_ref = bf16[32,64,128]{2,1,0:T(8,128)(2,1)S(1)} all-to-all(bf16[32,64,128]{2,1,0:T(8,128)(2,1)S(1)} %pad_maximum_fusion.1), channel_id=1, replica_groups=mesh['x_high'=2,'x_low'=2,'y_high'=2,'y_low'=2,'c'=2,'z_3'=2,'z_2'=2,'z_..., dimensions={0} | all-to-all | bytes 1048576 | tf_op jit(solution)/shard_map/all_to_all | solution.py:263
  140.8 2.1 %memory_2_1.1 = (bf16[32,64,128]{2,1,0:T(8,128)(2,1)S(1)}, bf16[256,1024]{1,0:T(8,128)(2,1)S(1)}) custom-call(s32[3,256]{1,0:T(4,128)S(1)} %copy-done.2, bf16[32,64,128]{2,1,0:T(8,128)(2,1)S(1)} %all_to_all.45.sigma_ref, bf16[1024,2048]{1,0:T(8,128)(2,1)S(1)} %get-tuple-element.17.hist_ref), custom_call_target="tpu_custom_call" | custom-call | flops 536870912 | bytes 4194304 | tf_op jit(solution)/shard_map/memory_2_1/pallas_call | solution.py:104
  142.8 3.6 %collective-permute-start.2 = (bf16[32,64,128]{2,1,0:T(8,128)(2,1)S(1)}, bf16[32,64,128]{2,1,0:T(8,128)(2,1)S(1)}, u32[]{:S(2)}, u32[]{:S(2)}) collective-permute-start(bf16[32,64,128]{2,1,0:T(8,128)(2,1)S(1)} %get-tuple-element.25), channel_id=1, source_target_pairs={{0,16},{16,0},{1,17},{17,1},{2,18},{18,2},{3,19},{19,3},{4,20},{20... | collective-permute-start | bytes 1572872 | tf_op jit(solution)/shard_map/ppermute | solution.py:276
  146.5 1.7 memory_2_0.1
  148.2 0.0 collective-permute-done.2
  148.2 0.2 add_convert_fusion
  148.4 14.7 %all_to_all.46.terms_ref = bf16[32,64,128]{2,1,0:T(8,128)(2,1)S(1)} all-to-all(bf16[32,64,128]{2,1,0:T(8,128)(2,1)S(1)} %add_convert_fusion), channel_id=1, replica_groups=mesh['x_high'=2,'x_low'=2,'y_high'=2,'y_low'=2,'c'=2,'z_3'=2,'z_2'=2,'z_..., dimensions={0} | all-to-all | bytes 1048576 | tf_op jit(solution)/shard_map/all_to_all | solution.py:263
  163.1 0.7 advance_01.1
  163.8 13.4 %all_to_all.47.pieces_ref = bf16[32,64,128]{2,1,0:T(8,128)(2,1)S(1)} all-to-all(bf16[32,64,128]{2,1,0:T(8,128)(2,1)S(1)} %bitcast.10), channel_id=1, replica_groups=mesh['x_high'=2,'x_low'=2,'y_high'=2,'y_low'=2,'c'=2,'z_3'=2,'z_2'=2,'z_..., dimensions={0} | all-to-all | bytes 1048576 | tf_op jit(solution)/shard_map/all_to_all | solution.py:263
  177.2 5.0 %collective-permute-start.3 = (bf16[32,64,128]{2,1,0:T(8,128)(2,1)S(1)}, bf16[32,64,128]{2,1,0:T(8,128)(2,1)S(1)}, u32[]{:S(2)}, u32[]{:S(2)}) collective-permute-start(bf16[32,64,128]{2,1,0:T(8,128)(2,1)S(1)} %all_to_all.47.pieces_ref), channel_id=1, source_target_pairs={{0,16},{16,0},{1,17},{17,1},{2,18},{18,2},{3,19},{19,3},{4,20},{20... | collective-permute-start | bytes 1572872 | tf_op jit(solution)/shard_map/ppermute | solution.py:283
  182.2 1.4 spread_1.1.refs_0_
  183.6 0.1 collective-permute-done.3.pieces_ref
  183.7 1.4 spread_0.1
  (10 shorter events, 0.1 us)
Async XLA Ops:
  0.0 11.6 %copy-start.2 = (s32[3,256]{1,0:T(4,128)S(1)}, s32[3,256]{1,0:T(4,128)}, u32[]{:S(2)}) copy-start(s32[3,256]{1,0:T(4,128)} %reach_ref.9) | copy-start | bytes 9220
  0.0 11.6 %copy-start.1 = (bf16[128,2048]{1,0:T(8,128)(2,1)S(1)}, bf16[128,2048]{1,0:T(8,128)(2,1)}, u32[]{:S(2)}) copy-start(bf16[128,2048]{1,0:T(8,128)(2,1)} %rest_0_.1) | copy-start | bytes 1572868
  2.9 10.5 %collective-permute-start = (bf16[32,64,128]{2,1,0:T(8,128)(2,1)S(1)}, bf16[32,64,128]{2,1,0:T(8,128)(2,1)S(1)}, u32[]{:S(2)}, u32[]{:S(2)}) collective-permute-start(bf16[32,64,128]{2,1,0:T(8,128)(2,1)S(1)} %get-tuple-element.18), channel_id=1, source_target_pairs={{0,16},{16,0},{1,17},{17,1},{2,18},{18,2},{3,19},{19,3},{4,20},{20... | collective-permute-start | bytes 1572872 | tf_op jit(solution)/shard_map/ppermute | solution.py:276
  11.6 16.4 %copy-start = (f32[128,128]{1,0:T(8,128)S(1)}, f32[128,128]{1,0:T(8,128)}, u32[]{:S(2)}) copy-start(f32[128,128]{1,0:T(8,128)} %step_ref.5) | copy-start | bytes 196612
  11.7 16.4 %copy-start.3 = (f32[128]{0:T(128)S(1)}, f32[128]{0:T(128)}, u32[]{:S(2)}) copy-start(f32[128]{0:T(128)} %param.10) | copy-start | bytes 1540
  80.0 5.4 %collective-permute-start.1 = (bf16[32,64,128]{2,1,0:T(8,128)(2,1)S(1)}, bf16[32,64,128]{2,1,0:T(8,128)(2,1)S(1)}, u32[]{:S(2)}, u32[]{:S(2)}) collective-permute-start(bf16[32,64,128]{2,1,0:T(8,128)(2,1)S(1)} %get-tuple-element.21), channel_id=1, source_target_pairs={{0,16},{16,0},{1,17},{17,1},{2,18},{18,2},{3,19},{19,3},{4,20},{20... | collective-permute-start | bytes 1572872 | tf_op jit(solution)/shard_map/ppermute | solution.py:276
  142.8 5.4 %collective-permute-start.2 = (bf16[32,64,128]{2,1,0:T(8,128)(2,1)S(1)}, bf16[32,64,128]{2,1,0:T(8,128)(2,1)S(1)}, u32[]{:S(2)}, u32[]{:S(2)}) collective-permute-start(bf16[32,64,128]{2,1,0:T(8,128)(2,1)S(1)} %get-tuple-element.25), channel_id=1, source_target_pairs={{0,16},{16,0},{1,17},{17,1},{2,18},{18,2},{3,19},{19,3},{4,20},{20... | collective-permute-start | bytes 1572872 | tf_op jit(solution)/shard_map/ppermute | solution.py:276
  177.2 6.5 %collective-permute-start.3 = (bf16[32,64,128]{2,1,0:T(8,128)(2,1)S(1)}, bf16[32,64,128]{2,1,0:T(8,128)(2,1)S(1)}, u32[]{:S(2)}, u32[]{:S(2)}) collective-permute-start(bf16[32,64,128]{2,1,0:T(8,128)(2,1)S(1)} %all_to_all.47.pieces_ref), channel_id=1, source_target_pairs={{0,16},{16,0},{1,17},{17,1},{2,18},{18,2},{3,19},{19,3},{4,20},{20... | collective-permute-start | bytes 1572872 | tf_op jit(solution)/shard_map/ppermute | solution.py:283

commit v10 on v8

--- a/solution.py
+++ b/solution.py
@@ -16,6 +16,7 @@
 HALF = 64
 QUARTER = 32
 TILE = 512
+STAGGER = 1000
 
 VMEM = pl.BlockSpec(memory_space=pltpu.VMEM)
 SMEM = pl.BlockSpec(memory_space=pltpu.SMEM)
@@ -86,6 +87,11 @@
                 sigma[at : at + HALF, group * ROW_T : (group + 1) * ROW_T] = value.astype(sigma.dtype)
     for step in range(hist_ref.shape[1] // 2 // TILE):
         column_tile(block, half, step, reach_ref, sigma, hist_ref, outs[0], edge_ref)
+    if not first_half:
+
+        @pl.when(own == 0)
+        def _():
+            pl.delay(STAGGER)
 
 
 def product_cost(rows, cols):

time: 181 us -> 179 us (0.989)
  blocking collectives: 139 us -> 133 us
  starting transfers between devices: 24.2 us -> 27.6 us
    all_to_all x8, blocking collectives: 139 us -> 133 us  [exchange(): return lax.all_to_all(x, axis, 0, 0, tiled=True)]
    ppermute x3, starting transfers between devices: 19.1 us -> 22 us  [local(): arrived = lax.ppermute(away, 'c', swap)]
where the time goes in v10:
time: 179 us
  blocking collectives  133 us (74%)
  starting transfers between devices  27.6 us (15%)
  Pallas kernels  16.8 us (9%)
    all_to_all x8, blocking collectives, exchange(): return lax.all_to_all(x, axis, 0, 0, tiled=True)  133 us
    ppermute x3, starting transfers between devices, local(): arrived = lax.ppermute(away, 'c', swap)  22 us
    pallas_call x5, Pallas kernels, memory_terms(): pl.pallas_call(functools.partial(memory_kernel, block, first_half, edge i...  9.3 us
    ppermute x1, starting transfers between devices, local(): other = lax.ppermute(own, 'c', swap)  5.61 us
  transfers between devices with their start and end apart: 4, of which 1 were waited for; matrix products, arithmetic and copies ran while one was open for 0% of the time, Pallas kernels for 4%

profile of v10, /device:TPU:1, one launch (start us, length us, event | category | flops | bytes accessed | tf_op | source)
XLA Modules:
  0.0 178.6 jit_solution(4069627137675561889)
XLA Ops:
  0.0 2.9 %memory_first.1 = (bf16[32,64,128]{2,1,0:T(8,128)(2,1)S(1)}, bf16[1024,2048]{1,0:T(8,128)(2,1)S(1)}, bf16[256,1024]{1,0:T(8,128)(2,1)S(1)}) custom-call(s32[3,256]{1,0:T(4,128)} %reach_ref.9, bf16[256,1024]{1,0:T(8,128)(2,1)} %sigma_hbm.1, bf16[1024,2048]{1,0:T(8,128)(2,1)} %hist_hbm.1), custom_call_target="tpu_custom_call" | custom-call | flops 536870912 | bytes 4194304 | tf_op jit(solution)/shard_map/memory_first/pallas_call | solution.py:147
  2.9 8.7 %collective-permute-start = (bf16[32,64,128]{2,1,0:T(8,128)(2,1)S(1)}, bf16[32,64,128]{2,1,0:T(8,128)(2,1)S(1)}, u32[]{:S(2)}, u32[]{:S(2)}) collective-permute-start(bf16[32,64,128]{2,1,0:T(8,128)(2,1)S(1)} %get-tuple-element.18), channel_id=1, source_target_pairs={{0,16},{16,0},{1,17},{17,1},{2,18},{18,2},{3,19},{19,3},{4,20},{20... | collective-permute-start | bytes 1572872 | tf_op jit(solution)/shard_map/ppermute | solution.py:275
  11.6 0.0 copy-start
  11.7 0.0 copy-start.3
  11.7 1.7 memory_0_0.1
  13.4 0.0 collective-permute-done
  13.4 0.2 add_convert_fusion.2
  13.6 13.8 %all_to_all.40.terms_ref = bf16[32,64,128]{2,1,0:T(8,128)(2,1)S(1)} all-to-all(bf16[32,64,128]{2,1,0:T(8,128)(2,1)S(1)} %add_convert_fusion.2), channel_id=1, replica_groups=mesh['x_high'=2,'x_low'=2,'y_high'=2,'y_low'=2,'c'=2,'z_3'=2,'z_2'=2,'z_..., dimensions={0} | all-to-all | bytes 1048576 | tf_op jit(solution)/shard_map/all_to_all | solution.py:262
  27.4 0.6 advance_10.1
  28.1 25.7 %all_to_all.41 = bf16[8,2,64,128]{3,2,1,0:T(8,128)(2,1)S(1)} all-to-all(bf16[8,2,64,128]{3,2,1,0:T(8,128)(2,1)S(1)} %get-tuple-element.19), channel_id=1, replica_groups=mesh['x_high'=2,'x_low'=2,'y_high'=2,'y_low'=2,'c'=2,'z_3'=2,'z_2'=2,'z_..., dimensions={0} | all-to-all | bytes 524288 | tf_op jit(solution)/shard_map/all_to_all | solution.py:262
  53.9 17.8 %all_to_all.42.sigma_ref = bf16[32,64,128]{2,1,0:T(8,128)(2,1)S(1)} all-to-all(bf16[32,64,128]{2,1,0:T(8,128)(2,1)S(1)} %pad_maximum_fusion), channel_id=1, replica_groups=mesh['x_high'=2,'x_low'=2,'y_high'=2,'y_low'=2,'c'=2,'z_3'=2,'z_2'=2,'z_..., dimensions={0} | all-to-all | bytes 1048576 | tf_op jit(solution)/shard_map/all_to_all | solution.py:262
  71.7 2.1 %memory_1_1.1 = (bf16[32,64,128]{2,1,0:T(8,128)(2,1)S(1)}, bf16[256,1024]{1,0:T(8,128)(2,1)S(1)}) custom-call(s32[3,256]{1,0:T(4,128)S(1)} %copy-done.2, bf16[32,64,128]{2,1,0:T(8,128)(2,1)S(1)} %all_to_all.42.sigma_ref, bf16[1024,2048]{1,0:T(8,128)(2,1)S(1)} %get-tuple-element.17.hist_ref), custom_call_target="tpu_custom_call" | custom-call | flops 536870912 | bytes 4194304 | tf_op jit(solution)/shard_map/memory_1_1/pallas_call | solution.py:109
  73.8 6.6 %collective-permute-start.1 = (bf16[32,64,128]{2,1,0:T(8,128)(2,1)S(1)}, bf16[32,64,128]{2,1,0:T(8,128)(2,1)S(1)}, u32[]{:S(2)}, u32[]{:S(2)}) collective-permute-start(bf16[32,64,128]{2,1,0:T(8,128)(2,1)S(1)} %get-tuple-element.21), channel_id=1, source_target_pairs={{0,16},{16,0},{1,17},{17,1},{2,18},{18,2},{3,19},{19,3},{4,20},{20... | collective-permute-start | bytes 1572872 | tf_op jit(solution)/shard_map/ppermute | solution.py:275
  80.4 1.7 memory_1_0.1
  82.1 0.0 collective-permute-done.1
  82.1 0.2 add_convert_fusion.1
  82.3 13.8 %all_to_all.43.terms_ref = bf16[32,64,128]{2,1,0:T(8,128)(2,1)S(1)} all-to-all(bf16[32,64,128]{2,1,0:T(8,128)(2,1)S(1)} %add_convert_fusion.1), channel_id=1, replica_groups=mesh['x_high'=2,'x_low'=2,'y_high'=2,'y_low'=2,'c'=2,'z_3'=2,'z_2'=2,'z_..., dimensions={0} | all-to-all | bytes 1048576 | tf_op jit(solution)/shard_map/all_to_all | solution.py:262
  96.1 0.6 advance_00.1
  96.8 17.4 %all_to_all.44 = bf16[8,2,64,128]{3,2,1,0:T(8,128)(2,1)S(1)} all-to-all(bf16[8,2,64,128]{3,2,1,0:T(8,128)(2,1)S(1)} %get-tuple-element.23), channel_id=1, replica_groups=mesh['x_high'=2,'x_low'=2,'y_high'=2,'y_low'=2,'c'=2,'z_3'=2,'z_2'=2,'z_..., dimensions={0} | all-to-all | bytes 524288 | tf_op jit(solution)/shard_map/all_to_all | solution.py:262
  114.2 17.8 %all_to_all.45.sigma_ref = bf16[32,64,128]{2,1,0:T(8,128)(2,1)S(1)} all-to-all(bf16[32,64,128]{2,1,0:T(8,128)(2,1)S(1)} %pad_maximum_fusion.1), channel_id=1, replica_groups=mesh['x_high'=2,'x_low'=2,'y_high'=2,'y_low'=2,'c'=2,'z_3'=2,'z_2'=2,'z_..., dimensions={0} | all-to-all | bytes 1048576 | tf_op jit(solution)/shard_map/all_to_all | solution.py:262
  132.0 2.1 %memory_2_1.1 = (bf16[32,64,128]{2,1,0:T(8,128)(2,1)S(1)}, bf16[256,1024]{1,0:T(8,128)(2,1)S(1)}) custom-call(s32[3,256]{1,0:T(4,128)S(1)} %copy-done.2, bf16[32,64,128]{2,1,0:T(8,128)(2,1)S(1)} %all_to_all.45.sigma_ref, bf16[1024,2048]{1,0:T(8,128)(2,1)S(1)} %get-tuple-element.17.hist_ref), custom_call_target="tpu_custom_call" | custom-call | flops 536870912 | bytes 4194304 | tf_op jit(solution)/shard_map/memory_2_1/pallas_call | solution.py:109
  134.1 6.6 %collective-permute-start.2 = (bf16[32,64,128]{2,1,0:T(8,128)(2,1)S(1)}, bf16[32,64,128]{2,1,0:T(8,128)(2,1)S(1)}, u32[]{:S(2)}, u32[]{:S(2)}) collective-permute-start(bf16[32,64,128]{2,1,0:T(8,128)(2,1)S(1)} %get-tuple-element.25), channel_id=1, source_target_pairs={{0,16},{16,0},{1,17},{17,1},{2,18},{18,2},{3,19},{19,3},{4,20},{20... | collective-permute-start | bytes 1572872 | tf_op jit(solution)/shard_map/ppermute | solution.py:275
  140.7 1.7 memory_2_0.1
  142.5 0.0 collective-permute-done.2
  142.5 0.2 add_convert_fusion
  142.7 13.8 %all_to_all.46.terms_ref = bf16[32,64,128]{2,1,0:T(8,128)(2,1)S(1)} all-to-all(bf16[32,64,128]{2,1,0:T(8,128)(2,1)S(1)} %add_convert_fusion), channel_id=1, replica_groups=mesh['x_high'=2,'x_low'=2,'y_high'=2,'y_low'=2,'c'=2,'z_3'=2,'z_2'=2,'z_..., dimensions={0} | all-to-all | bytes 1048576 | tf_op jit(solution)/shard_map/all_to_all | solution.py:262
  156.5 0.7 advance_01.1
  157.1 13.0 %all_to_all.47.pieces_ref = bf16[32,64,128]{2,1,0:T(8,128)(2,1)S(1)} all-to-all(bf16[32,64,128]{2,1,0:T(8,128)(2,1)S(1)} %bitcast.10), channel_id=1, replica_groups=mesh['x_high'=2,'x_low'=2,'y_high'=2,'y_low'=2,'c'=2,'z_3'=2,'z_2'=2,'z_..., dimensions={0} | all-to-all | bytes 1048576 | tf_op jit(solution)/shard_map/all_to_all | solution.py:262
  170.1 5.6 %collective-permute-start.3 = (bf16[32,64,128]{2,1,0:T(8,128)(2,1)S(1)}, bf16[32,64,128]{2,1,0:T(8,128)(2,1)S(1)}, u32[]{:S(2)}, u32[]{:S(2)}) collective-permute-start(bf16[32,64,128]{2,1,0:T(8,128)(2,1)S(1)} %all_to_all.47.pieces_ref), channel_id=1, source_target_pairs={{0,16},{16,0},{1,17},{17,1},{2,18},{18,2},{3,19},{19,3},{4,20},{20... | collective-permute-start | bytes 1572872 | tf_op jit(solution)/shard_map/ppermute | solution.py:282
  175.7 1.4 spread_1.1.refs_0_
  177.1 0.1 collective-permute-done.3.pieces_ref
  177.3 1.4 spread_0.1
  (10 shorter events, 0.1 us)
Async XLA Ops:
  0.0 11.6 %copy-start.2 = (s32[3,256]{1,0:T(4,128)S(1)}, s32[3,256]{1,0:T(4,128)}, u32[]{:S(2)}) copy-start(s32[3,256]{1,0:T(4,128)} %reach_ref.9) | copy-start | bytes 9220
  0.0 11.6 %copy-start.1 = (bf16[128,2048]{1,0:T(8,128)(2,1)S(1)}, bf16[128,2048]{1,0:T(8,128)(2,1)}, u32[]{:S(2)}) copy-start(bf16[128,2048]{1,0:T(8,128)(2,1)} %rest_0_.1) | copy-start | bytes 1572868
  2.9 10.5 %collective-permute-start = (bf16[32,64,128]{2,1,0:T(8,128)(2,1)S(1)}, bf16[32,64,128]{2,1,0:T(8,128)(2,1)S(1)}, u32[]{:S(2)}, u32[]{:S(2)}) collective-permute-start(bf16[32,64,128]{2,1,0:T(8,128)(2,1)S(1)} %get-tuple-element.18), channel_id=1, source_target_pairs={{0,16},{16,0},{1,17},{17,1},{2,18},{18,2},{3,19},{19,3},{4,20},{20... | collective-permute-start | bytes 1572872 | tf_op jit(solution)/shard_map/ppermute | solution.py:275
  11.6 15.8 %copy-start = (f32[128,128]{1,0:T(8,128)S(1)}, f32[128,128]{1,0:T(8,128)}, u32[]{:S(2)}) copy-start(f32[128,128]{1,0:T(8,128)} %step_ref.5) | copy-start | bytes 196612
  11.7 15.8 %copy-start.3 = (f32[128]{0:T(128)S(1)}, f32[128]{0:T(128)}, u32[]{:S(2)}) copy-start(f32[128]{0:T(128)} %param.10) | copy-start | bytes 1540
  73.8 8.4 %collective-permute-start.1 = (bf16[32,64,128]{2,1,0:T(8,128)(2,1)S(1)}, bf16[32,64,128]{2,1,0:T(8,128)(2,1)S(1)}, u32[]{:S(2)}, u32[]{:S(2)}) collective-permute-start(bf16[32,64,128]{2,1,0:T(8,128)(2,1)S(1)} %get-tuple-element.21), channel_id=1, source_target_pairs={{0,16},{16,0},{1,17},{17,1},{2,18},{18,2},{3,19},{19,3},{4,20},{20... | collective-permute-start | bytes 1572872 | tf_op jit(solution)/shard_map/ppermute | solution.py:275
  134.1 8.4 %collective-permute-start.2 = (bf16[32,64,128]{2,1,0:T(8,128)(2,1)S(1)}, bf16[32,64,128]{2,1,0:T(8,128)(2,1)S(1)}, u32[]{:S(2)}, u32[]{:S(2)}) collective-permute-start(bf16[32,64,128]{2,1,0:T(8,128)(2,1)S(1)} %get-tuple-element.25), channel_id=1, source_target_pairs={{0,16},{16,0},{1,17},{17,1},{2,18},{18,2},{3,19},{19,3},{4,20},{20... | collective-permute-start | bytes 1572872 | tf_op jit(solution)/shard_map/ppermute | solution.py:275
  170.1 7.1 %collective-permute-start.3 = (bf16[32,64,128]{2,1,0:T(8,128)(2,1)S(1)}, bf16[32,64,128]{2,1,0:T(8,128)(2,1)S(1)}, u32[]{:S(2)}, u32[]{:S(2)}) collective-permute-start(bf16[32,64,128]{2,1,0:T(8,128)(2,1)S(1)} %all_to_all.47.pieces_ref), channel_id=1, source_target_pairs={{0,16},{16,0},{1,17},{17,1},{2,18},{18,2},{3,19},{19,3},{4,20},{20... | collective-permute-start | bytes 1572872 | tf_op jit(solution)/shard_map/ppermute | solution.py:282

commit v11 on v10

--- a/solution.py
+++ b/solution.py
@@ -16,7 +16,7 @@
 HALF = 64
 QUARTER = 32
 TILE = 512
-STAGGER = 1000
+STAGGER = 1500
 
 VMEM = pl.BlockSpec(memory_space=pltpu.VMEM)
 SMEM = pl.BlockSpec(memory_space=pltpu.SMEM)

time: 179 us -> 178 us (level)
  blocking collectives: 133 us -> 126 us
  starting transfers between devices: 27.6 us -> 33.7 us
    all_to_all x8, blocking collectives: 133 us -> 126 us  [exchange(): return lax.all_to_all(x, axis, 0, 0, tiled=True)]
    ppermute x3, starting transfers between devices: 22 us -> 27.7 us  [local(): arrived = lax.ppermute(away, 'c', swap)]
where the time goes in v11:
time: 178 us
  blocking collectives  126 us (71%)
  starting transfers between devices  33.7 us (19%)
  Pallas kernels  16.8 us (9%)
    all_to_all x8, blocking collectives, exchange(): return lax.all_to_all(x, axis, 0, 0, tiled=True)  126 us
    ppermute x3, starting transfers between devices, local(): arrived = lax.ppermute(away, 'c', swap)  27.7 us
    pallas_call x5, Pallas kernels, memory_terms(): pl.pallas_call(functools.partial(memory_kernel, block, first_half, edge i...  9.3 us
    ppermute x1, starting transfers between devices, local(): other = lax.ppermute(own, 'c', swap)  6.06 us
  transfers between devices with their start and end apart: 4, of which 1 were waited for; matrix products, arithmetic and copies ran while one was open for 0% of the time, Pallas kernels for 4%

profile of v11, /device:TPU:1, one launch (start us, length us, event | category | flops | bytes accessed | tf_op | source)
XLA Modules:
  0.0 177.6 jit_solution(859490206904452901)
XLA Ops:
  0.0 2.9 %memory_first.1 = (bf16[32,64,128]{2,1,0:T(8,128)(2,1)S(1)}, bf16[1024,2048]{1,0:T(8,128)(2,1)S(1)}, bf16[256,1024]{1,0:T(8,128)(2,1)S(1)}) custom-call(s32[3,256]{1,0:T(4,128)} %reach_ref.9, bf16[256,1024]{1,0:T(8,128)(2,1)} %sigma_hbm.1, bf16[1024,2048]{1,0:T(8,128)(2,1)} %hist_hbm.1), custom_call_target="tpu_custom_call" | custom-call | flops 536870912 | bytes 4194304 | tf_op jit(solution)/shard_map/memory_first/pallas_call | solution.py:147
  2.9 8.7 %collective-permute-start = (bf16[32,64,128]{2,1,0:T(8,128)(2,1)S(1)}, bf16[32,64,128]{2,1,0:T(8,128)(2,1)S(1)}, u32[]{:S(2)}, u32[]{:S(2)}) collective-permute-start(bf16[32,64,128]{2,1,0:T(8,128)(2,1)S(1)} %get-tuple-element.18), channel_id=1, source_target_pairs={{0,16},{16,0},{1,17},{17,1},{2,18},{18,2},{3,19},{19,3},{4,20},{20... | collective-permute-start | bytes 1572872 | tf_op jit(solution)/shard_map/ppermute | solution.py:275
  11.6 0.0 copy-start
  11.7 0.0 copy-start.3
  11.7 1.7 memory_0_0.1
  13.4 0.0 collective-permute-done
  13.4 0.2 add_convert_fusion.2
  13.6 13.0 %all_to_all.40.terms_ref = bf16[32,64,128]{2,1,0:T(8,128)(2,1)S(1)} all-to-all(bf16[32,64,128]{2,1,0:T(8,128)(2,1)S(1)} %add_convert_fusion.2), channel_id=1, replica_groups=mesh['x_high'=2,'x_low'=2,'y_high'=2,'y_low'=2,'c'=2,'z_3'=2,'z_2'=2,'z_..., dimensions={0} | all-to-all | bytes 1048576 | tf_op jit(solution)/shard_map/all_to_all | solution.py:262
  26.6 0.6 advance_10.1
  27.3 26.1 %all_to_all.41 = bf16[8,2,64,128]{3,2,1,0:T(8,128)(2,1)S(1)} all-to-all(bf16[8,2,64,128]{3,2,1,0:T(8,128)(2,1)S(1)} %get-tuple-element.19), channel_id=1, replica_groups=mesh['x_high'=2,'x_low'=2,'y_high'=2,'y_low'=2,'c'=2,'z_3'=2,'z_2'=2,'z_..., dimensions={0} | all-to-all | bytes 524288 | tf_op jit(solution)/shard_map/all_to_all | solution.py:262
  53.4 15.0 %all_to_all.42.sigma_ref = bf16[32,64,128]{2,1,0:T(8,128)(2,1)S(1)} all-to-all(bf16[32,64,128]{2,1,0:T(8,128)(2,1)S(1)} %pad_maximum_fusion), channel_id=1, replica_groups=mesh['x_high'=2,'x_low'=2,'y_high'=2,'y_low'=2,'c'=2,'z_3'=2,'z_2'=2,'z_..., dimensions={0} | all-to-all | bytes 1048576 | tf_op jit(solution)/shard_map/all_to_all | solution.py:262
  68.4 2.1 %memory_1_1.1 = (bf16[32,64,128]{2,1,0:T(8,128)(2,1)S(1)}, bf16[256,1024]{1,0:T(8,128)(2,1)S(1)}) custom-call(s32[3,256]{1,0:T(4,128)S(1)} %copy-done.2, bf16[32,64,128]{2,1,0:T(8,128)(2,1)S(1)} %all_to_all.42.sigma_ref, bf16[1024,2048]{1,0:T(8,128)(2,1)S(1)} %get-tuple-element.17.hist_ref), custom_call_target="tpu_custom_call" | custom-call | flops 536870912 | bytes 4194304 | tf_op jit(solution)/shard_map/memory_1_1/pallas_call | solution.py:109
  70.5 9.4 %collective-permute-start.1 = (bf16[32,64,128]{2,1,0:T(8,128)(2,1)S(1)}, bf16[32,64,128]{2,1,0:T(8,128)(2,1)S(1)}, u32[]{:S(2)}, u32[]{:S(2)}) collective-permute-start(bf16[32,64,128]{2,1,0:T(8,128)(2,1)S(1)} %get-tuple-element.21), channel_id=1, source_target_pairs={{0,16},{16,0},{1,17},{17,1},{2,18},{18,2},{3,19},{19,3},{4,20},{20... | collective-permute-start | bytes 1572872 | tf_op jit(solution)/shard_map/ppermute | solution.py:275
  79.9 1.7 memory_1_0.1
  81.6 0.0 collective-permute-done.1
  81.6 0.2 add_convert_fusion.1
  81.8 13.4 %all_to_all.43.terms_ref = bf16[32,64,128]{2,1,0:T(8,128)(2,1)S(1)} all-to-all(bf16[32,64,128]{2,1,0:T(8,128)(2,1)S(1)} %add_convert_fusion.1), channel_id=1, replica_groups=mesh['x_high'=2,'x_low'=2,'y_high'=2,'y_low'=2,'c'=2,'z_3'=2,'z_2'=2,'z_..., dimensions={0} | all-to-all | bytes 1048576 | tf_op jit(solution)/shard_map/all_to_all | solution.py:262
  95.2 0.6 advance_00.1
  95.9 17.2 %all_to_all.44 = bf16[8,2,64,128]{3,2,1,0:T(8,128)(2,1)S(1)} all-to-all(bf16[8,2,64,128]{3,2,1,0:T(8,128)(2,1)S(1)} %get-tuple-element.23), channel_id=1, replica_groups=mesh['x_high'=2,'x_low'=2,'y_high'=2,'y_low'=2,'c'=2,'z_3'=2,'z_2'=2,'z_..., dimensions={0} | all-to-all | bytes 524288 | tf_op jit(solution)/shard_map/all_to_all | solution.py:262
  113.2 15.0 %all_to_all.45.sigma_ref = bf16[32,64,128]{2,1,0:T(8,128)(2,1)S(1)} all-to-all(bf16[32,64,128]{2,1,0:T(8,128)(2,1)S(1)} %pad_maximum_fusion.1), channel_id=1, replica_groups=mesh['x_high'=2,'x_low'=2,'y_high'=2,'y_low'=2,'c'=2,'z_3'=2,'z_2'=2,'z_..., dimensions={0} | all-to-all | bytes 1048576 | tf_op jit(solution)/shard_map/all_to_all | solution.py:262
  128.1 2.1 %memory_2_1.1 = (bf16[32,64,128]{2,1,0:T(8,128)(2,1)S(1)}, bf16[256,1024]{1,0:T(8,128)(2,1)S(1)}) custom-call(s32[3,256]{1,0:T(4,128)S(1)} %copy-done.2, bf16[32,64,128]{2,1,0:T(8,128)(2,1)S(1)} %all_to_all.45.sigma_ref, bf16[1024,2048]{1,0:T(8,128)(2,1)S(1)} %get-tuple-element.17.hist_ref), custom_call_target="tpu_custom_call" | custom-call | flops 536870912 | bytes 4194304 | tf_op jit(solution)/shard_map/memory_2_1/pallas_call | solution.py:109
  130.2 9.5 %collective-permute-start.2 = (bf16[32,64,128]{2,1,0:T(8,128)(2,1)S(1)}, bf16[32,64,128]{2,1,0:T(8,128)(2,1)S(1)}, u32[]{:S(2)}, u32[]{:S(2)}) collective-permute-start(bf16[32,64,128]{2,1,0:T(8,128)(2,1)S(1)} %get-tuple-element.25), channel_id=1, source_target_pairs={{0,16},{16,0},{1,17},{17,1},{2,18},{18,2},{3,19},{19,3},{4,20},{20... | collective-permute-start | bytes 1572872 | tf_op jit(solution)/shard_map/ppermute | solution.py:275
  139.7 1.7 memory_2_0.1
  141.4 0.0 collective-permute-done.2
  141.4 0.2 add_convert_fusion
  141.6 13.4 %all_to_all.46.terms_ref = bf16[32,64,128]{2,1,0:T(8,128)(2,1)S(1)} all-to-all(bf16[32,64,128]{2,1,0:T(8,128)(2,1)S(1)} %add_convert_fusion), channel_id=1, replica_groups=mesh['x_high'=2,'x_low'=2,'y_high'=2,'y_low'=2,'c'=2,'z_3'=2,'z_2'=2,'z_..., dimensions={0} | all-to-all | bytes 1048576 | tf_op jit(solution)/shard_map/all_to_all | solution.py:262
  155.0 0.7 advance_01.1
  155.7 12.9 %all_to_all.47.pieces_ref = bf16[32,64,128]{2,1,0:T(8,128)(2,1)S(1)} all-to-all(bf16[32,64,128]{2,1,0:T(8,128)(2,1)S(1)} %bitcast.10), channel_id=1, replica_groups=mesh['x_high'=2,'x_low'=2,'y_high'=2,'y_low'=2,'c'=2,'z_3'=2,'z_2'=2,'z_..., dimensions={0} | all-to-all | bytes 1048576 | tf_op jit(solution)/shard_map/all_to_all | solution.py:262
  168.6 6.1 %collective-permute-start.3 = (bf16[32,64,128]{2,1,0:T(8,128)(2,1)S(1)}, bf16[32,64,128]{2,1,0:T(8,128)(2,1)S(1)}, u32[]{:S(2)}, u32[]{:S(2)}) collective-permute-start(bf16[32,64,128]{2,1,0:T(8,128)(2,1)S(1)} %all_to_all.47.pieces_ref), channel_id=1, source_target_pairs={{0,16},{16,0},{1,17},{17,1},{2,18},{18,2},{3,19},{19,3},{4,20},{20... | collective-permute-start | bytes 1572872 | tf_op jit(solution)/shard_map/ppermute | solution.py:282
  174.7 1.4 spread_1.1.refs_0_
  176.1 0.1 collective-permute-done.3.pieces_ref
  176.2 1.4 spread_0.1
  (10 shorter events, 0.1 us)
Async XLA Ops:
  0.0 11.6 %copy-start.2 = (s32[3,256]{1,0:T(4,128)S(1)}, s32[3,256]{1,0:T(4,128)}, u32[]{:S(2)}) copy-start(s32[3,256]{1,0:T(4,128)} %reach_ref.9) | copy-start | bytes 9220
  0.0 11.6 %copy-start.1 = (bf16[128,2048]{1,0:T(8,128)(2,1)S(1)}, bf16[128,2048]{1,0:T(8,128)(2,1)}, u32[]{:S(2)}) copy-start(bf16[128,2048]{1,0:T(8,128)(2,1)} %rest_0_.1) | copy-start | bytes 1572868
  2.9 10.5 %collective-permute-start = (bf16[32,64,128]{2,1,0:T(8,128)(2,1)S(1)}, bf16[32,64,128]{2,1,0:T(8,128)(2,1)S(1)}, u32[]{:S(2)}, u32[]{:S(2)}) collective-permute-start(bf16[32,64,128]{2,1,0:T(8,128)(2,1)S(1)} %get-tuple-element.18), channel_id=1, source_target_pairs={{0,16},{16,0},{1,17},{17,1},{2,18},{18,2},{3,19},{19,3},{4,20},{20... | collective-permute-start | bytes 1572872 | tf_op jit(solution)/shard_map/ppermute | solution.py:275
  11.6 15.0 %copy-start = (f32[128,128]{1,0:T(8,128)S(1)}, f32[128,128]{1,0:T(8,128)}, u32[]{:S(2)}) copy-start(f32[128,128]{1,0:T(8,128)} %step_ref.5) | copy-start | bytes 196612
  11.7 15.0 %copy-start.3 = (f32[128]{0:T(128)S(1)}, f32[128]{0:T(128)}, u32[]{:S(2)}) copy-start(f32[128]{0:T(128)} %param.10) | copy-start | bytes 1540
  70.5 11.2 %collective-permute-start.1 = (bf16[32,64,128]{2,1,0:T(8,128)(2,1)S(1)}, bf16[32,64,128]{2,1,0:T(8,128)(2,1)S(1)}, u32[]{:S(2)}, u32[]{:S(2)}) collective-permute-start(bf16[32,64,128]{2,1,0:T(8,128)(2,1)S(1)} %get-tuple-element.21), channel_id=1, source_target_pairs={{0,16},{16,0},{1,17},{17,1},{2,18},{18,2},{3,19},{19,3},{4,20},{20... | collective-permute-start | bytes 1572872 | tf_op jit(solution)/shard_map/ppermute | solution.py:275
  130.2 11.2 %collective-permute-start.2 = (bf16[32,64,128]{2,1,0:T(8,128)(2,1)S(1)}, bf16[32,64,128]{2,1,0:T(8,128)(2,1)S(1)}, u32[]{:S(2)}, u32[]{:S(2)}) collective-permute-start(bf16[32,64,128]{2,1,0:T(8,128)(2,1)S(1)} %get-tuple-element.25), channel_id=1, source_target_pairs={{0,16},{16,0},{1,17},{17,1},{2,18},{18,2},{3,19},{19,3},{4,20},{20... | collective-permute-start | bytes 1572872 | tf_op jit(solution)/shard_map/ppermute | solution.py:275
  168.6 7.6 %collective-permute-start.3 = (bf16[32,64,128]{2,1,0:T(8,128)(2,1)S(1)}, bf16[32,64,128]{2,1,0:T(8,128)(2,1)S(1)}, u32[]{:S(2)}, u32[]{:S(2)}) collective-permute-start(bf16[32,64,128]{2,1,0:T(8,128)(2,1)S(1)} %all_to_all.47.pieces_ref), channel_id=1, source_target_pairs={{0,16},{16,0},{1,17},{17,1},{2,18},{18,2},{3,19},{19,3},{4,20},{20... | collective-permute-start | bytes 1572872 | tf_op jit(solution)/shard_map/ppermute | solution.py:282

commit v12 on v11

--- a/solution.py
+++ b/solution.py
@@ -16,7 +16,7 @@
 HALF = 64
 QUARTER = 32
 TILE = 512
-STAGGER = 1500
+STAGGER = 2200
 
 VMEM = pl.BlockSpec(memory_space=pltpu.VMEM)
 SMEM = pl.BlockSpec(memory_space=pltpu.SMEM)

time: 178 us -> 178 us (level)
  no operation moved by 1% of the time
where the time goes in v12:
time: 178 us
  blocking collectives  125 us (70%)
  starting transfers between devices  35.2 us (20%)
  Pallas kernels  16.8 us (9%)
    all_to_all x8, blocking collectives, exchange(): return lax.all_to_all(x, axis, 0, 0, tiled=True)  125 us
    ppermute x3, starting transfers between devices, local(): arrived = lax.ppermute(away, 'c', swap)  28.6 us
    pallas_call x5, Pallas kernels, memory_terms(): pl.pallas_call(functools.partial(memory_kernel, block, first_half, edge i...  9.31 us
    ppermute x1, starting transfers between devices, local(): other = lax.ppermute(own, 'c', swap)  6.61 us
  transfers between devices with their start and end apart: 4, of which 1 were waited for; matrix products, arithmetic and copies ran while one was open for 0% of the time, Pallas kernels for 4%

profile of v12, /device:TPU:1, one launch (start us, length us, event | category | flops | bytes accessed | tf_op | source)
XLA Modules:
  0.0 177.7 jit_solution(3647671448420500241)
XLA Ops:
  0.0 2.9 %memory_first.1 = (bf16[32,64,128]{2,1,0:T(8,128)(2,1)S(1)}, bf16[1024,2048]{1,0:T(8,128)(2,1)S(1)}, bf16[256,1024]{1,0:T(8,128)(2,1)S(1)}) custom-call(s32[3,256]{1,0:T(4,128)} %reach_ref.9, bf16[256,1024]{1,0:T(8,128)(2,1)} %sigma_hbm.1, bf16[1024,2048]{1,0:T(8,128)(2,1)} %hist_hbm.1), custom_call_target="tpu_custom_call" | custom-call | flops 536870912 | bytes 4194304 | tf_op jit(solution)/shard_map/memory_first/pallas_call | solution.py:147
  2.9 8.7 %collective-permute-start = (bf16[32,64,128]{2,1,0:T(8,128)(2,1)S(1)}, bf16[32,64,128]{2,1,0:T(8,128)(2,1)S(1)}, u32[]{:S(2)}, u32[]{:S(2)}) collective-permute-start(bf16[32,64,128]{2,1,0:T(8,128)(2,1)S(1)} %get-tuple-element.18), channel_id=1, source_target_pairs={{0,16},{16,0},{1,17},{17,1},{2,18},{18,2},{3,19},{19,3},{4,20},{20... | collective-permute-start | bytes 1572872 | tf_op jit(solution)/shard_map/ppermute | solution.py:275
  11.6 0.0 copy-start
  11.7 0.0 copy-start.3
  11.7 1.7 memory_0_0.1
  13.4 0.0 collective-permute-done
  13.4 0.2 add_convert_fusion.2
  13.6 12.6 %all_to_all.40.terms_ref = bf16[32,64,128]{2,1,0:T(8,128)(2,1)S(1)} all-to-all(bf16[32,64,128]{2,1,0:T(8,128)(2,1)S(1)} %add_convert_fusion.2), channel_id=1, replica_groups=mesh['x_high'=2,'x_low'=2,'y_high'=2,'y_low'=2,'c'=2,'z_3'=2,'z_2'=2,'z_..., dimensions={0} | all-to-all | bytes 1048576 | tf_op jit(solution)/shard_map/all_to_all | solution.py:262
  26.2 0.6 advance_10.1
  26.9 26.0 %all_to_all.41 = bf16[8,2,64,128]{3,2,1,0:T(8,128)(2,1)S(1)} all-to-all(bf16[8,2,64,128]{3,2,1,0:T(8,128)(2,1)S(1)} %get-tuple-element.19), channel_id=1, replica_groups=mesh['x_high'=2,'x_low'=2,'y_high'=2,'y_low'=2,'c'=2,'z_3'=2,'z_2'=2,'z_..., dimensions={0} | all-to-all | bytes 524288 | tf_op jit(solution)/shard_map/all_to_all | solution.py:262
  52.9 14.8 %all_to_all.42.sigma_ref = bf16[32,64,128]{2,1,0:T(8,128)(2,1)S(1)} all-to-all(bf16[32,64,128]{2,1,0:T(8,128)(2,1)S(1)} %pad_maximum_fusion), channel_id=1, replica_groups=mesh['x_high'=2,'x_low'=2,'y_high'=2,'y_low'=2,'c'=2,'z_3'=2,'z_2'=2,'z_..., dimensions={0} | all-to-all | bytes 1048576 | tf_op jit(solution)/shard_map/all_to_all | solution.py:262
  67.7 2.1 %memory_1_1.1 = (bf16[32,64,128]{2,1,0:T(8,128)(2,1)S(1)}, bf16[256,1024]{1,0:T(8,128)(2,1)S(1)}) custom-call(s32[3,256]{1,0:T(4,128)S(1)} %copy-done.2, bf16[32,64,128]{2,1,0:T(8,128)(2,1)S(1)} %all_to_all.42.sigma_ref, bf16[1024,2048]{1,0:T(8,128)(2,1)S(1)} %get-tuple-element.17.hist_ref), custom_call_target="tpu_custom_call" | custom-call | flops 536870912 | bytes 4194304 | tf_op jit(solution)/shard_map/memory_1_1/pallas_call | solution.py:109
  69.8 9.9 %collective-permute-start.1 = (bf16[32,64,128]{2,1,0:T(8,128)(2,1)S(1)}, bf16[32,64,128]{2,1,0:T(8,128)(2,1)S(1)}, u32[]{:S(2)}, u32[]{:S(2)}) collective-permute-start(bf16[32,64,128]{2,1,0:T(8,128)(2,1)S(1)} %get-tuple-element.21), channel_id=1, source_target_pairs={{0,16},{16,0},{1,17},{17,1},{2,18},{18,2},{3,19},{19,3},{4,20},{20... | collective-permute-start | bytes 1572872 | tf_op jit(solution)/shard_map/ppermute | solution.py:275
  79.7 1.7 memory_1_0.1
  81.5 0.0 collective-permute-done.1
  81.5 0.2 add_convert_fusion.1
  81.7 13.0 %all_to_all.43.terms_ref = bf16[32,64,128]{2,1,0:T(8,128)(2,1)S(1)} all-to-all(bf16[32,64,128]{2,1,0:T(8,128)(2,1)S(1)} %add_convert_fusion.1), channel_id=1, replica_groups=mesh['x_high'=2,'x_low'=2,'y_high'=2,'y_low'=2,'c'=2,'z_3'=2,'z_2'=2,'z_..., dimensions={0} | all-to-all | bytes 1048576 | tf_op jit(solution)/shard_map/all_to_all | solution.py:262
  94.7 0.6 advance_00.1
  95.3 17.5 %all_to_all.44 = bf16[8,2,64,128]{3,2,1,0:T(8,128)(2,1)S(1)} all-to-all(bf16[8,2,64,128]{3,2,1,0:T(8,128)(2,1)S(1)} %get-tuple-element.23), channel_id=1, replica_groups=mesh['x_high'=2,'x_low'=2,'y_high'=2,'y_low'=2,'c'=2,'z_3'=2,'z_2'=2,'z_..., dimensions={0} | all-to-all | bytes 524288 | tf_op jit(solution)/shard_map/all_to_all | solution.py:262
  112.9 14.8 %all_to_all.45.sigma_ref = bf16[32,64,128]{2,1,0:T(8,128)(2,1)S(1)} all-to-all(bf16[32,64,128]{2,1,0:T(8,128)(2,1)S(1)} %pad_maximum_fusion.1), channel_id=1, replica_groups=mesh['x_high'=2,'x_low'=2,'y_high'=2,'y_low'=2,'c'=2,'z_3'=2,'z_2'=2,'z_..., dimensions={0} | all-to-all | bytes 1048576 | tf_op jit(solution)/shard_map/all_to_all | solution.py:262
  127.7 2.1 %memory_2_1.1 = (bf16[32,64,128]{2,1,0:T(8,128)(2,1)S(1)}, bf16[256,1024]{1,0:T(8,128)(2,1)S(1)}) custom-call(s32[3,256]{1,0:T(4,128)S(1)} %copy-done.2, bf16[32,64,128]{2,1,0:T(8,128)(2,1)S(1)} %all_to_all.45.sigma_ref, bf16[1024,2048]{1,0:T(8,128)(2,1)S(1)} %get-tuple-element.17.hist_ref), custom_call_target="tpu_custom_call" | custom-call | flops 536870912 | bytes 4194304 | tf_op jit(solution)/shard_map/memory_2_1/pallas_call | solution.py:109
  129.7 9.9 %collective-permute-start.2 = (bf16[32,64,128]{2,1,0:T(8,128)(2,1)S(1)}, bf16[32,64,128]{2,1,0:T(8,128)(2,1)S(1)}, u32[]{:S(2)}, u32[]{:S(2)}) collective-permute-start(bf16[32,64,128]{2,1,0:T(8,128)(2,1)S(1)} %get-tuple-element.25), channel_id=1, source_target_pairs={{0,16},{16,0},{1,17},{17,1},{2,18},{18,2},{3,19},{19,3},{4,20},{20... | collective-permute-start | bytes 1572872 | tf_op jit(solution)/shard_map/ppermute | solution.py:275
  139.7 1.7 memory_2_0.1
  141.4 0.0 collective-permute-done.2
  141.4 0.2 add_convert_fusion
  141.6 13.0 %all_to_all.46.terms_ref = bf16[32,64,128]{2,1,0:T(8,128)(2,1)S(1)} all-to-all(bf16[32,64,128]{2,1,0:T(8,128)(2,1)S(1)} %add_convert_fusion), channel_id=1, replica_groups=mesh['x_high'=2,'x_low'=2,'y_high'=2,'y_low'=2,'c'=2,'z_3'=2,'z_2'=2,'z_..., dimensions={0} | all-to-all | bytes 1048576 | tf_op jit(solution)/shard_map/all_to_all | solution.py:262
  154.6 0.7 advance_01.1
  155.2 12.9 %all_to_all.47.pieces_ref = bf16[32,64,128]{2,1,0:T(8,128)(2,1)S(1)} all-to-all(bf16[32,64,128]{2,1,0:T(8,128)(2,1)S(1)} %bitcast.10), channel_id=1, replica_groups=mesh['x_high'=2,'x_low'=2,'y_high'=2,'y_low'=2,'c'=2,'z_3'=2,'z_2'=2,'z_..., dimensions={0} | all-to-all | bytes 1048576 | tf_op jit(solution)/shard_map/all_to_all | solution.py:262
  168.2 6.6 %collective-permute-start.3 = (bf16[32,64,128]{2,1,0:T(8,128)(2,1)S(1)}, bf16[32,64,128]{2,1,0:T(8,128)(2,1)S(1)}, u32[]{:S(2)}, u32[]{:S(2)}) collective-permute-start(bf16[32,64,128]{2,1,0:T(8,128)(2,1)S(1)} %all_to_all.47.pieces_ref), channel_id=1, source_target_pairs={{0,16},{16,0},{1,17},{17,1},{2,18},{18,2},{3,19},{19,3},{4,20},{20... | collective-permute-start | bytes 1572872 | tf_op jit(solution)/shard_map/ppermute | solution.py:282
  174.8 1.4 spread_1.1.refs_0_
  176.2 0.1 collective-permute-done.3.pieces_ref
  176.3 1.4 spread_0.1
  (10 shorter events, 0.1 us)
Async XLA Ops:
  0.0 11.6 %copy-start.2 = (s32[3,256]{1,0:T(4,128)S(1)}, s32[3,256]{1,0:T(4,128)}, u32[]{:S(2)}) copy-start(s32[3,256]{1,0:T(4,128)} %reach_ref.9) | copy-start | bytes 9220
  0.0 11.6 %copy-start.1 = (bf16[128,2048]{1,0:T(8,128)(2,1)S(1)}, bf16[128,2048]{1,0:T(8,128)(2,1)}, u32[]{:S(2)}) copy-start(bf16[128,2048]{1,0:T(8,128)(2,1)} %rest_0_.1) | copy-start | bytes 1572868
  2.9 10.5 %collective-permute-start = (bf16[32,64,128]{2,1,0:T(8,128)(2,1)S(1)}, bf16[32,64,128]{2,1,0:T(8,128)(2,1)S(1)}, u32[]{:S(2)}, u32[]{:S(2)}) collective-permute-start(bf16[32,64,128]{2,1,0:T(8,128)(2,1)S(1)} %get-tuple-element.18), channel_id=1, source_target_pairs={{0,16},{16,0},{1,17},{17,1},{2,18},{18,2},{3,19},{19,3},{4,20},{20... | collective-permute-start | bytes 1572872 | tf_op jit(solution)/shard_map/ppermute | solution.py:275
  11.6 14.6 %copy-start = (f32[128,128]{1,0:T(8,128)S(1)}, f32[128,128]{1,0:T(8,128)}, u32[]{:S(2)}) copy-start(f32[128,128]{1,0:T(8,128)} %step_ref.5) | copy-start | bytes 196612
  11.7 14.6 %copy-start.3 = (f32[128]{0:T(128)S(1)}, f32[128]{0:T(128)}, u32[]{:S(2)}) copy-start(f32[128]{0:T(128)} %param.10) | copy-start | bytes 1540
  69.8 11.7 %collective-permute-start.1 = (bf16[32,64,128]{2,1,0:T(8,128)(2,1)S(1)}, bf16[32,64,128]{2,1,0:T(8,128)(2,1)S(1)}, u32[]{:S(2)}, u32[]{:S(2)}) collective-permute-start(bf16[32,64,128]{2,1,0:T(8,128)(2,1)S(1)} %get-tuple-element.21), channel_id=1, source_target_pairs={{0,16},{16,0},{1,17},{17,1},{2,18},{18,2},{3,19},{19,3},{4,20},{20... | collective-permute-start | bytes 1572872 | tf_op jit(solution)/shard_map/ppermute | solution.py:275
  129.7 11.7 %collective-permute-start.2 = (bf16[32,64,128]{2,1,0:T(8,128)(2,1)S(1)}, bf16[32,64,128]{2,1,0:T(8,128)(2,1)S(1)}, u32[]{:S(2)}, u32[]{:S(2)}) collective-permute-start(bf16[32,64,128]{2,1,0:T(8,128)(2,1)S(1)} %get-tuple-element.25), channel_id=1, source_target_pairs={{0,16},{16,0},{1,17},{17,1},{2,18},{18,2},{3,19},{19,3},{4,20},{20... | collective-permute-start | bytes 1572872 | tf_op jit(solution)/shard_map/ppermute | solution.py:275
  168.2 8.1 %collective-permute-start.3 = (bf16[32,64,128]{2,1,0:T(8,128)(2,1)S(1)}, bf16[32,64,128]{2,1,0:T(8,128)(2,1)S(1)}, u32[]{:S(2)}, u32[]{:S(2)}) collective-permute-start(bf16[32,64,128]{2,1,0:T(8,128)(2,1)S(1)} %all_to_all.47.pieces_ref), channel_id=1, source_target_pairs={{0,16},{16,0},{1,17},{17,1},{2,18},{18,2},{3,19},{19,3},{4,20},{20... | collective-permute-start | bytes 1572872 | tf_op jit(solution)/shard_map/ppermute | solution.py:282
